TPU v7x, 32 devices: a whole 2x2x4 slice. The times are simulated.
32 devices in a mesh: section: 2 (over core), ctx: 4 (over y, x), wt: 4 (over z).
Axes of the slice: x: 2, y: 2, z: 4, core: 2. Of those that a mesh axis runs over, the one named last changes fastest.
Arguments:
- hidden_in: bfloat16 [4, 512, 2560], P(None, 'ctx', 'wt'), may hold values from -6 to 6
- out_grad: bfloat16 [4, 512, 2560], P(None, 'ctx', 'wt'), may hold values from -6 to 6
- block_pos: int32 [4, 8], replicated, may hold values from 0 to 7, as said below
- norm1_gain: float32 [2, 2560], P('section', 'wt'), may hold values from 0.25 to 1.75
- norm2_gain: float32 [2, 2560], P('section', 'wt'), may hold values from 0.25 to 1.75
- wq: bfloat16 [2, 2560, 2560], P('section', 'wt'), as said below
- wk: bfloat16 [2, 2560, 256], P('section', 'wt'), as said below
- wv: bfloat16 [2, 2560, 256], P('section', 'wt'), may hold values from -0.125 to 0.125
- wo: bfloat16 [2, 2560, 2560], P('section', None, 'wt'), may hold values from -2 to 2
- w_gate: bfloat16 [2, 2560, 7680], P('section', None, 'wt'), may hold values from -0.125 to 0.125
- w_up: bfloat16 [2, 2560, 7680], P('section', None, 'wt'), may hold values from -0.125 to 0.125
- w_down: bfloat16 [2, 7680, 2560], P('section', 'wt'), may hold values from -0.0625 to 0.0625
Outputs:
- out: bfloat16 [4, 512, 2560], P(None, 'ctx', 'wt')
- in_grad: float32 [4, 512, 2560], P(None, 'ctx', 'wt')
- grad_wq: float32 [2, 2560, 2560], P('section', 'wt', 'ctx')
- grad_wk: float32 [2, 2560, 256], P('section', 'wt', 'ctx')
- grad_wv: float32 [2, 2560, 256], P('section', 'wt', 'ctx')
- grad_wo: float32 [2, 2560, 2560], P('section', 'ctx', 'wt')
- grad_gate: float32 [2, 2560, 7680], P('section', 'ctx', 'wt')
- grad_up: float32 [2, 2560, 7680], P('section', 'ctx', 'wt')
- grad_down: float32 [2, 7680, 2560], P('section', 'wt', 'ctx')
- grad_gain1: float32 [2, 2560], P('section', 'wt')
- grad_gain2: float32 [2, 2560], P('section', 'wt')
Inputs may be any that keep to these rules, and one draw needn't show every extreme that they name: `block_pos`: in every micro-batch's row each block number appears once, and the entries at places 2 * c and 2 * c + 1 add up to 7. `wq`: entries are of order 2560 ** -0.5 times a factor of at most 16. `wk`: entries are of order 2560 ** -0.5.
All inputs are finite; a program needn't handle non-finite values.
Results may differ from a plain program's by a relative error of at most 0.028.
Values may be sent and summed in bfloat16 or wider, within the bound.
No kernel may reach another device: no remote copies, remote signals or barrier semaphores. Data moves between devices by JAX's collectives and lax.ppermute only.
A program may use at most 576 MiB of HBM per device.

v0:
```python
import math

import jax
import jax.numpy as jnp
from jax import lax
from jax.sharding import PartitionSpec as P

EPS = 1e-06
ROPE_LOG = math.log(10000.0)
NEG_FILL = -1e30


def from_behind(value, axis, steps):
    count = lax.axis_size(axis)
    pairs = [(source, (source + steps) % count) for source in range(count)]
    return lax.ppermute(value, axis, pairs)


def gelu_tanh(values):
    return jax.nn.gelu(values, approximate=True)


def rotate(values, positions, direction):
    half_size = values.shape[-1] // 2
    freqs = jnp.exp(jnp.arange(half_size, dtype=jnp.float32) * (-2.0 * ROPE_LOG / values.shape[-1]))
    angles = positions.astype(jnp.float32)[:, None, None] * freqs
    cosine = jnp.cos(angles)
    sine = jnp.sin(angles) * direction
    first_half = values[..., :half_size]
    second_half = values[..., half_size:]
    return jnp.concatenate(
        [first_half * cosine - second_half * sine, second_half * cosine + first_half * sine],
        axis=-1,
    )


def positions_for(block_row, seq_len, block_len):
    places = jnp.arange(seq_len, dtype=jnp.int32)
    owners = (places // block_len)[:, None] == jnp.arange(block_row.shape[0], dtype=jnp.int32)[
        None, :
    ]
    return (
        jnp.sum(jnp.where(owners, block_row[None, :], 0), axis=1) * block_len + places % block_len
    )


def masked_scores(query_rows, key_rows, query_pos, key_pos, score_scale):
    raw = jnp.dot(query_rows, key_rows.T, preferred_element_type=jnp.float32) * score_scale
    return jnp.where(key_pos[None, :] <= query_pos[:, None], raw, NEG_FILL)


def feature_sum(values):
    return lax.psum(values, "wt")


def section_pass(values):
    return from_behind(values, "section", 1)


def fetch_keys(key_rows, value_rows):
    return (
        lax.all_gather(key_rows, ("ctx", "wt"), axis=0, tiled=True),
        lax.all_gather(value_rows, ("ctx", "wt"), axis=0, tiled=True),
    )


def norm_back(d_normed, source, inverse, gain, carried):
    scaled = d_normed * gain
    width_all = source.shape[1] * lax.axis_size("wt")
    inner = feature_sum(jnp.sum(scaled * source, axis=1)) / width_all
    d_source = carried + inverse[:, None] * scaled - source * (inverse**3 * inner)[:, None]
    d_gain = jnp.sum(d_normed * source * inverse[:, None], axis=0)
    return (d_gain, d_source)


def layer_forward(source, block_row, params):
    gain_first, gain_second, w_proj, w_out, w_gate_up, w_down_l = params
    row_count, width_local = source.shape
    query_width = w_out.shape[0]
    head_size = (w_proj.shape[1] - query_width) // 2
    head_count = query_width // head_size
    query_count = row_count // lax.axis_size("wt")
    seq_len = row_count * lax.axis_size("ctx")
    width_all = width_local * lax.axis_size("wt")
    key_pos = positions_for(block_row, seq_len, row_count // 2)
    first_row = lax.axis_index("ctx") * row_count + lax.axis_index("wt") * query_count
    query_pos = lax.dynamic_slice_in_dim(key_pos, first_row, query_count)
    inv_first = lax.rsqrt(feature_sum(jnp.sum(source * source, axis=1)) / width_all + EPS)
    normed_first = (source * inv_first[:, None] * gain_first).astype(jnp.bfloat16)
    projected = lax.psum_scatter(
        jnp.dot(normed_first, w_proj, preferred_element_type=jnp.float32),
        "wt",
        scatter_dimension=0,
        tiled=True,
    )
    queries = rotate(
        projected[:, :query_width].reshape(query_count, head_count, head_size), query_pos, 1.0
    ).astype(jnp.bfloat16)
    key_rows = rotate(
        projected[:, query_width : query_width + head_size][:, None, :], query_pos, 1.0
    )[:, 0].astype(jnp.bfloat16)
    value_rows = projected[:, query_width + head_size :].astype(jnp.bfloat16)
    all_keys, all_values = fetch_keys(key_rows, value_rows)
    query_rows = queries.reshape(query_count * head_count, head_size)
    row_pos = jnp.repeat(query_pos, head_count)
    scores = masked_scores(query_rows, all_keys, row_pos, key_pos, head_size ** (-0.5))
    row_max = jnp.max(scores, axis=1, keepdims=True)
    log_total = row_max[:, 0] + jnp.log(jnp.sum(jnp.exp(scores - row_max), axis=1))
    probs = jnp.exp(scores - log_total[:, None]).astype(jnp.bfloat16)
    attended = (
        jnp.dot(probs, all_values, preferred_element_type=jnp.float32)
        .astype(jnp.bfloat16)
        .reshape(query_count, query_width)
    )
    attended_full = lax.all_gather(attended, "wt", axis=0, tiled=True)
    middle = source + jnp.dot(attended_full, w_out, preferred_element_type=jnp.float32)
    inv_second = lax.rsqrt(feature_sum(jnp.sum(middle * middle, axis=1)) / width_all + EPS)
    normed_second = (middle * inv_second[:, None] * gain_second).astype(jnp.bfloat16)
    normed_second_full = lax.all_gather(normed_second, "wt", axis=1, tiled=True)
    gate_up = jnp.dot(normed_second_full, w_gate_up, preferred_element_type=jnp.float32)
    hidden_local = w_gate_up.shape[1] // 2
    gate_pre = gate_up[:, :hidden_local]
    up_pre = gate_up[:, hidden_local:]
    hidden_act = (gelu_tanh(gate_pre) * up_pre).astype(jnp.bfloat16)
    update = lax.psum_scatter(
        jnp.dot(hidden_act, w_down_l, preferred_element_type=jnp.float32),
        "wt",
        scatter_dimension=1,
        tiled=True,
    )
    result = middle + update
    saved_state = (
        source,
        inv_first,
        normed_first,
        queries,
        key_rows,
        value_rows,
        all_keys,
        all_values,
        log_total,
        attended_full,
        middle,
        inv_second,
        normed_second_full,
        gate_pre,
        up_pre,
        key_pos,
        query_pos,
    )
    return (result, saved_state)


def layer_backward(grad_out, saved_state, params):
    gain_first, gain_second, w_proj, w_out, w_gate_up, w_down_l = params
    (
        source,
        inv_first,
        normed_first,
        queries,
        key_rows,
        value_rows,
        kept_keys,
        kept_values,
        log_total,
        attended_full,
        middle,
        inv_second,
        normed_second_full,
        gate_pre,
        up_pre,
        key_pos,
        query_pos,
    ) = saved_state
    query_count, head_count, head_size = queries.shape
    query_width = head_count * head_size
    score_scale = head_size ** (-0.5)
    grad_low = grad_out.astype(jnp.bfloat16)
    grad_full = lax.all_gather(grad_low, "wt", axis=1, tiled=True)
    hidden_act = (gelu_tanh(gate_pre) * up_pre).astype(jnp.bfloat16)
    d_down = jnp.dot(hidden_act.T, grad_full, preferred_element_type=jnp.float32)
    d_hidden = jnp.dot(grad_full, w_down_l.T, preferred_element_type=jnp.float32)
    activated, pull_back = jax.vjp(gelu_tanh, gate_pre)
    d_gate_pre = pull_back(d_hidden * up_pre)[0].astype(jnp.bfloat16)
    d_up_pre = (d_hidden * activated).astype(jnp.bfloat16)
    d_both = jnp.concatenate([d_gate_pre, d_up_pre], axis=1)
    d_gate_up = jnp.dot(normed_second_full.T, d_both, preferred_element_type=jnp.float32)
    d_normed_second = lax.psum_scatter(
        jnp.dot(d_both, w_gate_up.T, preferred_element_type=jnp.float32).astype(jnp.bfloat16),
        "wt",
        scatter_dimension=1,
        tiled=True,
    ).astype(jnp.float32)
    d_gain_second, d_middle = norm_back(d_normed_second, middle, inv_second, gain_second, grad_out)
    d_middle_low = d_middle.astype(jnp.bfloat16)
    d_out_w = jnp.dot(attended_full.T, d_middle_low, preferred_element_type=jnp.float32)
    d_attended = lax.psum_scatter(
        jnp.dot(d_middle_low, w_out.T, preferred_element_type=jnp.float32).astype(jnp.bfloat16),
        "wt",
        scatter_dimension=0,
        tiled=True,
    )
    all_keys, all_values = (kept_keys, kept_values)
    query_rows = queries.reshape(query_count * head_count, head_size)
    row_pos = jnp.repeat(query_pos, head_count)
    scores = masked_scores(query_rows, all_keys, row_pos, key_pos, score_scale)
    probs = jnp.exp(scores - log_total[:, None])
    probs_low = probs.astype(jnp.bfloat16)
    d_rows = d_attended.reshape(query_count * head_count, head_size)
    d_values_all = jnp.dot(probs_low.T, d_rows, preferred_element_type=jnp.float32)
    d_probs = jnp.dot(d_rows, all_values.T, preferred_element_type=jnp.float32)
    delta_sum = jnp.sum(probs * d_probs, axis=1)
    d_scores = (probs * (d_probs - delta_sum[:, None]) * score_scale).astype(jnp.bfloat16)
    d_query_rows = jnp.dot(d_scores, all_keys, preferred_element_type=jnp.float32)
    d_keys_all = jnp.dot(d_scores.T, query_rows, preferred_element_type=jnp.float32)
    d_keys, d_values = (
        lax.psum_scatter(d_keys_all, ("ctx", "wt"), scatter_dimension=0, tiled=True),
        lax.psum_scatter(d_values_all, ("ctx", "wt"), scatter_dimension=0, tiled=True),
    )
    d_query = (
        rotate(d_query_rows.reshape(query_count, head_count, head_size), query_pos, -1.0)
        .reshape(query_count, query_width)
        .astype(jnp.bfloat16)
    )
    d_key = rotate(d_keys[:, None, :], query_pos, -1.0)[:, 0].astype(jnp.bfloat16)
    d_projected = jnp.concatenate([d_query, d_key, d_values.astype(jnp.bfloat16)], axis=1)
    d_projected_full = lax.all_gather(d_projected, "wt", axis=0, tiled=True)
    d_proj_w = jnp.dot(normed_first.T, d_projected_full, preferred_element_type=jnp.float32)
    d_normed_first = jnp.dot(d_projected_full, w_proj.T, preferred_element_type=jnp.float32)
    d_gain_first, d_source = norm_back(d_normed_first, source, inv_first, gain_first, d_middle)
    return (d_source, (d_proj_w, d_out_w, d_gate_up, d_down, d_gain_first, d_gain_second))


def reduce_grads(grad_terms, query_width, head_size, hidden_local):
    d_proj_w, d_out_w, d_gate_up, d_down, d_gain_first, d_gain_second = grad_terms
    pieces = (
        d_proj_w[:, :query_width],
        d_proj_w[:, query_width : query_width + head_size],
        d_proj_w[:, query_width + head_size :],
        d_out_w,
        d_gate_up[:, :hidden_local],
        d_gate_up[:, hidden_local:],
        d_down,
    )
    summed = (
        lax.psum_scatter(
            pieces[0].astype(jnp.bfloat16), "ctx", scatter_dimension=1, tiled=True
        ).astype(jnp.float32),
        lax.psum_scatter(
            pieces[1].astype(jnp.bfloat16), "ctx", scatter_dimension=1, tiled=True
        ).astype(jnp.float32),
        lax.psum_scatter(
            pieces[2].astype(jnp.bfloat16), "ctx", scatter_dimension=1, tiled=True
        ).astype(jnp.float32),
        lax.psum_scatter(
            pieces[3].astype(jnp.bfloat16), "ctx", scatter_dimension=0, tiled=True
        ).astype(jnp.float32),
        lax.psum_scatter(
            pieces[4].astype(jnp.bfloat16), "ctx", scatter_dimension=0, tiled=True
        ).astype(jnp.float32),
        lax.psum_scatter(
            pieces[5].astype(jnp.bfloat16), "ctx", scatter_dimension=0, tiled=True
        ).astype(jnp.float32),
        lax.psum_scatter(
            pieces[6].astype(jnp.bfloat16), "ctx", scatter_dimension=1, tiled=True
        ).astype(jnp.float32),
    )
    gains = lax.psum((d_gain_first, d_gain_second), "ctx")
    return tuple(summed) + tuple(gains)


def local(
    hidden_in, out_grad, block_pos, norm1_gain, norm2_gain, wq, wk, wv, wo, w_gate, w_up, w_down
):
    micro_count = hidden_in.shape[0]
    section_id = lax.axis_index("section")
    first_section = section_id == 0
    query_width = wq.shape[2]
    head_size = wk.shape[2]
    hidden_local = w_gate.shape[2]
    params = (
        norm1_gain[0],
        norm2_gain[0],
        jnp.concatenate([wq[0], wk[0], wv[0]], axis=1),
        wo[0],
        jnp.concatenate([w_gate[0], w_up[0]], axis=1),
        w_down[0],
    )
    received = jnp.zeros(hidden_in.shape[1:], jnp.float32)
    saved_list = []
    outputs_list = []
    for tick_index in range(micro_count + 1):
        micro_now = jnp.clip(tick_index - section_id, 0, micro_count - 1)
        block_row = lax.dynamic_index_in_dim(block_pos, micro_now, 0, keepdims=False)
        source = jnp.where(
            first_section, hidden_in[min(tick_index, micro_count - 1)].astype(jnp.float32), received
        )
        result, saved_state = layer_forward(source, block_row, params)
        saved_list.append(saved_state)
        received = section_pass(result)
        if tick_index > 0:
            outputs_list.append(jnp.where(first_section, received, result).astype(jnp.bfloat16))
    stacked_saved = jax.tree.map(lambda *leaves: jnp.stack(leaves), *saved_list)
    got_grad = jnp.zeros(hidden_in.shape[1:], jnp.float32)
    in_grads = []
    totals = None
    for tick_index in range(micro_count + 1):
        slot_now = jnp.clip(tick_index + 2 * section_id - 1, 0, micro_count)
        saved_state = jax.tree.map(
            lambda leaf: lax.dynamic_index_in_dim(leaf, slot_now, 0, keepdims=False), stacked_saved
        )
        micro_raw = tick_index + section_id - 1
        is_valid = jnp.logical_and(micro_raw >= 0, micro_raw < micro_count).astype(jnp.float32)
        incoming = jnp.where(
            first_section, got_grad, out_grad[min(tick_index, micro_count - 1)].astype(jnp.float32)
        )
        d_input, grad_terms = layer_backward(incoming, saved_state, params)
        grad_terms = tuple((leaf * is_valid for leaf in grad_terms))
        if totals is None:
            totals = grad_terms
        else:
            totals = tuple((old_term + new_term for old_term, new_term in zip(totals, grad_terms)))
        got_grad = section_pass(d_input)
        if tick_index > 0:
            in_grads.append(jnp.where(first_section, d_input, got_grad))
    totals = reduce_grads(totals, query_width, head_size, hidden_local)
    out = jnp.stack(outputs_list)
    in_grad = jnp.stack(in_grads)
    return (
        out,
        in_grad,
        totals[0][None],
        totals[1][None],
        totals[2][None],
        totals[3][None],
        totals[4][None],
        totals[5][None],
        totals[6][None],
        totals[7][None],
        totals[8][None],
    )


def solution(mesh):
    return jax.shard_map(
        local,
        mesh=mesh,
        in_specs=(
            P(None, "ctx", "wt"),
            P(None, "ctx", "wt"),
            P(),
            P("section", "wt"),
            P("section", "wt"),
            P("section", "wt", None),
            P("section", "wt", None),
            P("section", "wt", None),
            P("section", None, "wt"),
            P("section", None, "wt"),
            P("section", None, "wt"),
            P("section", "wt", None),
        ),
        out_specs=(
            P(None, "ctx", "wt"),
            P(None, "ctx", "wt"),
            P("section", "wt", "ctx"),
            P("section", "wt", "ctx"),
            P("section", "wt", "ctx"),
            P("section", "ctx", "wt"),
            P("section", "ctx", "wt"),
            P("section", "ctx", "wt"),
            P("section", "wt", "ctx"),
            P("section", "wt"),
            P("section", "wt"),
        ),
        check_vma=False,
    )
```

profile of v0, /device:TPU:0, one launch (start us, length us, event | category | flops | bytes accessed | tf_op | source)
XLA Modules:
  0.0 3118.3 jit_solution(15713615378445174570)
XLA Ops:
  37.8 27.1 reduce-scatter.56.cloned.1.call-done
  73.3 41.1 %all-gather = bf16[512,1,256]{2,0,1:T(8,128)(2,1)S(1)} all-gather(bf16[32,1,256]{2,0,1:T(8,128)(2,1)S(1)} %pad_maximum_fusion.24), channel_id=2, replica_groups=mesh['section'=2,'ctx'=4,'wt'=4] {'ctx','wt'}, dimensions={0}, use_global_device_ids=true | all-gather | bytes 278528 | tf_op jit(solution)/shard_map/all_gather | solution.py:62
  115.1 37.7 %all_gather.91 = bf16[512,256]{1,0:T(8,128)(2,1)S(1)} all-gather(bf16[32,256]{1,0:T(8,128)(2,1)S(1)} %slice.572), channel_id=1, replica_groups=mesh['section'=2,'ctx'=4,'wt'=4] {'ctx','wt'}, dimensions={0}, use_global_device_ids=true | all-gather | bytes 278528 | tf_op jit(solution)/shard_map/all_gather | solution.py:63
  221.2 28.0 reduce-scatter.58.cloned.1.call-done
  271.7 32.0 %reduce-scatter.60.cloned.1.call-done = f32[32,3072]{1,0:T(8,128)} async-done(((f32[128,3072]{1,0:T(8,128)}), f32[32,3072]{1,0:T(8,128)}) %reduce-scatter.60.cloned.1.call-update) | async-done | bytes 393232 | tf_op jit(solution)/shard_map/reduce_scatter | solution.py:90
  315.0 41.0 %all-gather.1 = bf16[512,1,256]{2,0,1:T(8,128)(2,1)S(1)} all-gather(bf16[32,1,256]{2,0,1:T(8,128)(2,1)S(1)} %pad_maximum_fusion.25), channel_id=3, replica_groups=mesh['section'=2,'ctx'=4,'wt'=4] {'ctx','wt'}, dimensions={0}, use_global_device_ids=true | all-gather | bytes 278528 | tf_op jit(solution)/shard_map/all_gather | solution.py:62
  358.5 38.2 %all_gather.95 = bf16[512,256]{1,0:T(8,128)(2,1)S(1)} all-gather(bf16[32,256]{1,0:T(8,128)(2,1)S(1)} %slice.571), channel_id=1, replica_groups=mesh['section'=2,'ctx'=4,'wt'=4] {'ctx','wt'}, dimensions={0}, use_global_device_ids=true | all-gather | bytes 278528 | tf_op jit(solution)/shard_map/all_gather | solution.py:63
  463.1 29.0 reduce-scatter.62.cloned.1.call-done
  514.7 32.0 %reduce-scatter.64.cloned.1.call-done = f32[32,3072]{1,0:T(8,128)} async-done(((f32[128,3072]{1,0:T(8,128)}), f32[32,3072]{1,0:T(8,128)}) %reduce-scatter.64.cloned.1.call-update) | async-done | bytes 393232 | tf_op jit(solution)/shard_map/reduce_scatter | solution.py:90
  558.1 41.0 %all-gather.2 = bf16[512,1,256]{2,0,1:T(8,128)(2,1)S(1)} all-gather(bf16[32,1,256]{2,0,1:T(8,128)(2,1)S(1)} %pad_maximum_fusion.26), channel_id=4, replica_groups=mesh['section'=2,'ctx'=4,'wt'=4] {'ctx','wt'}, dimensions={0}, use_global_device_ids=true | all-gather | bytes 278528 | tf_op jit(solution)/shard_map/all_gather | solution.py:62
  601.5 38.2 %all_gather.99 = bf16[512,256]{1,0:T(8,128)(2,1)S(1)} all-gather(bf16[32,256]{1,0:T(8,128)(2,1)S(1)} %slice.570), channel_id=1, replica_groups=mesh['section'=2,'ctx'=4,'wt'=4] {'ctx','wt'}, dimensions={0}, use_global_device_ids=true | all-gather | bytes 278528 | tf_op jit(solution)/shard_map/all_gather | solution.py:63
  706.2 29.1 reduce-scatter.66.cloned.1.call-done
  757.8 32.0 %reduce-scatter.68.cloned.1.call-done = f32[32,3072]{1,0:T(8,128)} async-done(((f32[128,3072]{1,0:T(8,128)}), f32[32,3072]{1,0:T(8,128)}) %reduce-scatter.68.cloned.1.call-update) | async-done | bytes 393232 | tf_op jit(solution)/shard_map/reduce_scatter | solution.py:90
  801.1 41.0 %all-gather.3 = bf16[512,1,256]{2,0,1:T(8,128)(2,1)S(1)} all-gather(bf16[32,1,256]{2,0,1:T(8,128)(2,1)S(1)} %pad_maximum_fusion.27), channel_id=5, replica_groups=mesh['section'=2,'ctx'=4,'wt'=4] {'ctx','wt'}, dimensions={0}, use_global_device_ids=true | all-gather | bytes 278528 | tf_op jit(solution)/shard_map/all_gather | solution.py:62
  844.6 38.1 %all_gather.103 = bf16[512,256]{1,0:T(8,128)(2,1)S(1)} all-gather(bf16[32,256]{1,0:T(8,128)(2,1)S(1)} %slice.569), channel_id=1, replica_groups=mesh['section'=2,'ctx'=4,'wt'=4] {'ctx','wt'}, dimensions={0}, use_global_device_ids=true | all-gather | bytes 278528 | tf_op jit(solution)/shard_map/all_gather | solution.py:63
  962.1 20.5 all_gather.110
  1018.1 21.5 reduce-scatter.72.cloned.1.call-done
  1047.9 41.0 %all-gather.4 = bf16[512,1,256]{2,0,1:T(8,128)(2,1)S(1)} all-gather(bf16[32,1,256]{2,0,1:T(8,128)(2,1)S(1)} %pad_maximum_fusion.28), channel_id=6, replica_groups=mesh['section'=2,'ctx'=4,'wt'=4] {'ctx','wt'}, dimensions={0}, use_global_device_ids=true | all-gather | bytes 278528 | tf_op jit(solution)/shard_map/all_gather | solution.py:62
  1091.4 38.2 %all_gather.107 = bf16[512,256]{1,0:T(8,128)(2,1)S(1)} all-gather(bf16[32,256]{1,0:T(8,128)(2,1)S(1)} %slice.568), channel_id=1, replica_groups=mesh['section'=2,'ctx'=4,'wt'=4] {'ctx','wt'}, dimensions={0}, use_global_device_ids=true | all-gather | bytes 278528 | tf_op jit(solution)/shard_map/all_gather | solution.py:63
  1293.7 61.9 %reduce-scatter.78.cloned.1.call-done = f32[32,256]{1,0:T(8,128)} async-done(((f32[512,256]{1,0:T(8,128)}), f32[32,256]{1,0:T(8,128)}) %reduce-scatter.78.cloned.1.call-update) | async-done | bytes 32784 | tf_op jit(solution)/shard_map/reduce_scatter | solution.py:217
  1356.4 76.5 %reduce-scatter.80.cloned.1.call-done = f32[32,256]{1,0:T(8,128)} async-done(((f32[512,256]{1,0:T(8,128)}), f32[32,256]{1,0:T(8,128)}) %reduce-scatter.80.cloned.1.call-update) | async-done | bytes 32784 | tf_op jit(solution)/shard_map/reduce_scatter | solution.py:218
  1468.5 17.3 all_gather.112
  1508.3 20.3 reduce-scatter.114.cloned.1.call-done
  1546.1 20.0 reduce-scatter.82.cloned.1.call-done
  1579.4 70.9 %reduce-scatter.84.cloned.1.call-done = f32[32,256]{1,0:T(8,128)} async-done(((f32[512,256]{1,0:T(8,128)}), f32[32,256]{1,0:T(8,128)}) %reduce-scatter.84.cloned.1.call-update) | async-done | bytes 32784 | tf_op jit(solution)/shard_map/reduce_scatter | solution.py:217
  1651.2 76.4 %reduce-scatter.86.cloned.1.call-done = f32[32,256]{1,0:T(8,128)} async-done(((f32[512,256]{1,0:T(8,128)}), f32[32,256]{1,0:T(8,128)}) %reduce-scatter.86.cloned.1.call-update) | async-done | bytes 32784 | tf_op jit(solution)/shard_map/reduce_scatter | solution.py:218
  1762.7 17.5 all_gather.114
  1802.7 20.3 reduce-scatter.116.cloned.1.call-done
  1841.2 20.0 reduce-scatter.88.cloned.1.call-done
  1874.4 70.9 %reduce-scatter.90.cloned.1.call-done = f32[32,256]{1,0:T(8,128)} async-done(((f32[512,256]{1,0:T(8,128)}), f32[32,256]{1,0:T(8,128)}) %reduce-scatter.90.cloned.1.call-update) | async-done | bytes 32784 | tf_op jit(solution)/shard_map/reduce_scatter | solution.py:217
  1946.3 76.5 %reduce-scatter.92.cloned.1.call-done = f32[32,256]{1,0:T(8,128)} async-done(((f32[512,256]{1,0:T(8,128)}), f32[32,256]{1,0:T(8,128)}) %reduce-scatter.92.cloned.1.call-update) | async-done | bytes 32784 | tf_op jit(solution)/shard_map/reduce_scatter | solution.py:218
  2057.8 17.2 all_gather.116
  2097.5 20.3 reduce-scatter.118.cloned.1.call-done
  2136.0 20.0 reduce-scatter.94.cloned.1.call-done
  2169.3 71.0 %reduce-scatter.96.cloned.1.call-done = f32[32,256]{1,0:T(8,128)} async-done(((f32[512,256]{1,0:T(8,128)}), f32[32,256]{1,0:T(8,128)}) %reduce-scatter.96.cloned.1.call-update) | async-done | bytes 32784 | tf_op jit(solution)/shard_map/reduce_scatter | solution.py:217
  2241.2 76.5 %reduce-scatter.98.cloned.1.call-done = f32[32,256]{1,0:T(8,128)} async-done(((f32[512,256]{1,0:T(8,128)}), f32[32,256]{1,0:T(8,128)}) %reduce-scatter.98.cloned.1.call-update) | async-done | bytes 32784 | tf_op jit(solution)/shard_map/reduce_scatter | solution.py:218
  2352.8 17.3 all_gather.118
  2394.8 18.2 reduce-scatter.120.cloned.1.call-done
  2434.1 17.2 reduce-scatter.100.cloned.1.call-done
  2495.8 37.2 %reduce-scatter.104.cloned.1.call-done = f32[32,256]{1,0:T(8,128)} async-done(((f32[512,256]{1,0:T(8,128)}), f32[32,256]{1,0:T(8,128)}) %reduce-scatter.104.cloned.1.call-update) | async-done | bytes 32784 | tf_op jit(solution)/shard_map/reduce_scatter | solution.py:218
  2533.8 76.6 %reduce-scatter.102.cloned.1.call-done = f32[32,256]{1,0:T(8,128)} async-done(((f32[512,256]{1,0:T(8,128)}), f32[32,256]{1,0:T(8,128)}) %reduce-scatter.102.cloned.1.call-update) | async-done | bytes 32784 | tf_op jit(solution)/shard_map/reduce_scatter | solution.py:217
  2611.4 20.6 all_gather.119
  2717.5 31.6 %add_convert_fusion.1 = bf16[1920,2560]{1,0:T(8,128)(2,1)} fusion(f32[1920,2560]{1,0:T(8,128)} %fusion.199, f32[1920,2560]{1,0:T(8,128)} %fusion.197, f32[1920,2560]{1,0:T(8,128)} %fusion.195, f32[1920,2560]{1,0:T(8,128)} %fusion.193, bf16[128,2560]{1,0:T(8,128)(2,1)S(1)} %copy-done.51, f32[]{:T(128)S(6)} %convert_element_type.629, ...), kind=kOutput, calls=%fused_computation.2 | convolution fusion | flops 1309900800 | bytes 91095064 | tf_op jit(solution)/shard_map/dot_general | solution.py:181
  2798.7 16.6 fusion.168
  2815.4 16.4 fusion.166
  2831.8 60.2 %add_convert_fusion = bf16[2560,3840]{1,0:T(8,128)(2,1)} fusion(f32[2560,3840]{1,0:T(8,128)} %fusion.166, f32[2560,3840]{1,0:T(8,128)} %fusion.168, f32[2560,3840]{1,0:T(8,128)} %fusion.170, f32[2560,3840]{1,0:T(8,128)} %fusion.172, f32[]{:T(128)S(6)} %convert_element_type.629, f32[]{:T(128)S(6)} %convert_element_type.628, f32[]{:T(128)S(6)} %convert_element_type.627, ...), kind=kOutput, calls=%fused_computation | convolution fusion | flops 2616852480 | bytes 178585632 | tf_op jit(solution)/shard_map/dot_general | solution.py:187
  2955.6 50.0 %reduce-scatter.108.cloned.1.call-done = bf16[640,1920]{1,0:T(8,128)(2,1)} async-done(((bf16[2560,1920]{1,0:T(8,128)(2,1)}), bf16[640,1920]{1,0:T(8,128)(2,1)}) %reduce-scatter.108.cloned.1.call-update) | async-done | bytes 2457616 | tf_op jit(solution)/shard_map/reduce_scatter | solution.py:258
  3010.0 96.7 %reduce-scatter.110.cloned.1.call-done = bf16[640,1920]{1,0:T(8,128)(2,1)} async-done(((bf16[2560,1920]{1,0:T(8,128)(2,1)}), bf16[640,1920]{1,0:T(8,128)(2,1)}) %reduce-scatter.110.cloned.1.call-update) | async-done | bytes 2457616 | tf_op jit(solution)/shard_map/reduce_scatter | solution.py:261
  (947 shorter events, 1242.2 us)
Async XLA Ops:
  7.2 166.9 %copy-start = (bf16[1,2560,640]{2,1,0:T(8,128)(2,1)S(1)}, bf16[1,2560,640]{2,1,0:T(8,128)(2,1)}, u32[]{:S(2)}) copy-start(bf16[1,2560,640]{2,1,0:T(8,128)(2,1)} %param.20) | copy-start | bytes 9830404
  7.2 57.7 %reduce-scatter.56.cloned.1.call-start = ((), (), s32[]{:S(2)}) async-start(), calls=%async_computation.37 | async-start | bytes 1966080 | tf_op jit(solution)/shard_map/reduce_scatter | solution.py:90
  31.0 218.1 %reduce-scatter.58.cloned.1.call-start = ((), (), s32[]{:S(2)}) async-start(), calls=%async_computation.38 | async-start | bytes 1638400 | tf_op jit(solution)/shard_map/reduce_scatter | solution.py:125
  221.1 82.5 %reduce-scatter.60.cloned.1.call-start = ((), (), s32[]{:S(2)}) async-start(), calls=%async_computation.39 | async-start | bytes 1966080 | tf_op jit(solution)/shard_map/reduce_scatter | solution.py:90
  250.2 1.8 collective-permute-start
  269.5 222.6 %reduce-scatter.62.cloned.1.call-start = ((), (), s32[]{:S(2)}) async-start(), calls=%async_computation.40 | async-start | bytes 1638400 | tf_op jit(solution)/shard_map/reduce_scatter | solution.py:125
  463.1 83.6 %reduce-scatter.64.cloned.1.call-start = ((), (), s32[]{:S(2)}) async-start(), calls=%async_computation.41 | async-start | bytes 1966080 | tf_op jit(solution)/shard_map/reduce_scatter | solution.py:90
  493.3 1.7 collective-permute-start.1
  512.6 222.7 %reduce-scatter.66.cloned.1.call-start = ((), (), s32[]{:S(2)}) async-start(), calls=%async_computation.42 | async-start | bytes 1638400 | tf_op jit(solution)/shard_map/reduce_scatter | solution.py:125
  706.1 83.6 %reduce-scatter.68.cloned.1.call-start = ((), (), s32[]{:S(2)}) async-start(), calls=%async_computation.43 | async-start | bytes 1966080 | tf_op jit(solution)/shard_map/reduce_scatter | solution.py:90
  736.3 1.7 collective-permute-start.2
  755.6 228.3 %reduce-scatter.70.cloned.1.call-start = ((), (), s32[]{:S(2)}) async-start(), calls=%async_computation.44 | async-start | bytes 1638400 | tf_op jit(solution)/shard_map/reduce_scatter | solution.py:125
  949.7 90.0 %reduce-scatter.72.cloned.1.call-start = ((), (), s32[]{:S(2)}) async-start(), calls=%async_computation.45 | async-start | bytes 1966080 | tf_op jit(solution)/shard_map/reduce_scatter | solution.py:90
  985.0 3.5 collective-permute-start.3
  1006.9 224.9 %reduce-scatter.112.cloned.1.call-start = ((), (), s32[]{:S(2)}) async-start(), calls=%async_computation.65 | async-start | bytes 819200
  1211.5 59.8 %reduce-scatter.76.cloned.1.call-start = ((), (), s32[]{:S(2)}) async-start(), calls=%async_computation.47 | async-start | bytes 819200 | tf_op jit(solution)/shard_map/reduce_scatter | solution.py:197
  1250.1 105.5 %reduce-scatter.78.cloned.1.call-start = ((), (), s32[]{:S(2)}) async-start(), calls=%async_computation.48 | async-start | bytes 557056 | tf_op jit(solution)/shard_map/reduce_scatter | solution.py:217
  1278.8 154.1 %reduce-scatter.80.cloned.1.call-start = ((), (), s32[]{:S(2)}) async-start(), calls=%async_computation.49 | async-start | bytes 557056 | tf_op jit(solution)/shard_map/reduce_scatter | solution.py:218
  1287.8 240.8 %reduce-scatter.114.cloned.1.call-start = ((), (), s32[]{:S(2)}) async-start(), calls=%async_computation.66 | async-start | bytes 819200
  1465.2 1.7 collective-permute-start.5
  1508.2 57.9 %reduce-scatter.82.cloned.1.call-start = ((), (), s32[]{:S(2)}) async-start(), calls=%async_computation.50 | async-start | bytes 819200 | tf_op jit(solution)/shard_map/reduce_scatter | solution.py:197
  1544.8 105.5 %reduce-scatter.84.cloned.1.call-start = ((), (), s32[]{:S(2)}) async-start(), calls=%async_computation.51 | async-start | bytes 557056 | tf_op jit(solution)/shard_map/reduce_scatter | solution.py:217
  1573.6 154.1 %reduce-scatter.86.cloned.1.call-start = ((), (), s32[]{:S(2)}) async-start(), calls=%async_computation.52 | async-start | bytes 557056 | tf_op jit(solution)/shard_map/reduce_scatter | solution.py:218
  1575.9 247.0 %reduce-scatter.116.cloned.1.call-start = ((), (), s32[]{:S(2)}) async-start(), calls=%async_computation.67 | async-start | bytes 819200
  1759.9 1.7 collective-permute-start.6
  1802.6 58.6 %reduce-scatter.88.cloned.1.call-start = ((), (), s32[]{:S(2)}) async-start(), calls=%async_computation.53 | async-start | bytes 819200 | tf_op jit(solution)/shard_map/reduce_scatter | solution.py:197
  1839.9 105.5 %reduce-scatter.90.cloned.1.call-start = ((), (), s32[]{:S(2)}) async-start(), calls=%async_computation.54 | async-start | bytes 557056 | tf_op jit(solution)/shard_map/reduce_scatter | solution.py:217
  1868.6 154.1 %reduce-scatter.92.cloned.1.call-start = ((), (), s32[]{:S(2)}) async-start(), calls=%async_computation.55 | async-start | bytes 557056 | tf_op jit(solution)/shard_map/reduce_scatter | solution.py:218
  1870.9 246.9 %reduce-scatter.118.cloned.1.call-start = ((), (), s32[]{:S(2)}) async-start(), calls=%async_computation.68 | async-start | bytes 819200
  2055.0 1.7 collective-permute-start.7
  2097.4 58.6 %reduce-scatter.94.cloned.1.call-start = ((), (), s32[]{:S(2)}) async-start(), calls=%async_computation.56 | async-start | bytes 819200 | tf_op jit(solution)/shard_map/reduce_scatter | solution.py:197
  2134.8 105.5 %reduce-scatter.96.cloned.1.call-start = ((), (), s32[]{:S(2)}) async-start(), calls=%async_computation.57 | async-start | bytes 557056 | tf_op jit(solution)/shard_map/reduce_scatter | solution.py:217
  2163.5 154.2 %reduce-scatter.98.cloned.1.call-start = ((), (), s32[]{:S(2)}) async-start(), calls=%async_computation.58 | async-start | bytes 557056 | tf_op jit(solution)/shard_map/reduce_scatter | solution.py:218
  2165.8 247.2 %reduce-scatter.120.cloned.1.call-start = ((), (), s32[]{:S(2)}) async-start(), calls=%async_computation.69 | async-start | bytes 819200
  2350.0 1.7 collective-permute-start.8
  2392.6 58.7 %reduce-scatter.100.cloned.1.call-start = ((), (), s32[]{:S(2)}) async-start(), calls=%async_computation.59 | async-start | bytes 819200 | tf_op jit(solution)/shard_map/reduce_scatter | solution.py:197
  2430.0 103.1 %reduce-scatter.104.cloned.1.call-start = ((), (), s32[]{:S(2)}) async-start(), calls=%async_computation.61 | async-start | bytes 557056 | tf_op jit(solution)/shard_map/reduce_scatter | solution.py:218
  2456.2 154.2 %reduce-scatter.102.cloned.1.call-start = ((), (), s32[]{:S(2)}) async-start(), calls=%async_computation.60 | async-start | bytes 557056 | tf_op jit(solution)/shard_map/reduce_scatter | solution.py:217
  2458.5 450.0 %reduce-scatter.74.cloned.1.call-start = ((), (), s32[]{:S(2)}) async-start(), calls=%async_computation.46 | async-start | bytes 1638400 | tf_op jit(solution)/shard_map/reduce_scatter | solution.py:125
  2466.7 473.4 %reduce-scatter.126.cloned.1.call-start = ((), (), s32[]{:S(2)}) async-start(), calls=%async_computation.72 | async-start | bytes 409600
  2646.7 295.3 %reduce-scatter.124.cloned.1.call-start = ((), (), s32[]{:S(2)}) async-start(), calls=%async_computation.71 | async-start | bytes 409600
  2657.5 286.4 %reduce-scatter.106.cloned.1.call-start = ((), (), s32[]{:S(2)}) async-start(), calls=%async_computation.62 | async-start | bytes 4096000 | tf_op jit(solution)/shard_map/reduce_scatter | solution.py:255
  2670.4 276.0 %reduce-scatter.122.cloned.1.call-start = ((), (), s32[]{:S(2)}) async-start(), calls=%async_computation.70 | async-start | bytes 4096000
  2675.8 273.8 %reduce-scatter.128.cloned.1.call-start = ((), (), s32[]{:S(2)}) async-start(), calls=%async_computation.73 | async-start | bytes 12288000
  2763.1 242.5 %reduce-scatter.108.cloned.1.call-start = ((), (), s32[]{:S(2)}) async-start(), calls=%async_computation.63 | async-start | bytes 12288000 | tf_op jit(solution)/shard_map/reduce_scatter | solution.py:258
  2907.1 199.6 %reduce-scatter.110.cloned.1.call-start = ((), (), s32[]{:S(2)}) async-start(), calls=%async_computation.64 | async-start | bytes 12288000 | tf_op jit(solution)/shard_map/reduce_scatter | solution.py:261
  2909.6 1.5 collective-permute-start.4
  2929.7 9.2 collective-permute-start.9
  (203 other events, 3003.5 us)
Sparse Core Ops, SparseCore 0:
  31.2 33.7 reduce-scatter.55
  221.2 27.8 reduce-scatter.57
  269.6 33.9 reduce-scatter.59
  463.2 28.8 reduce-scatter.61
  512.7 33.9 reduce-scatter.63
  706.2 28.9 reduce-scatter.65
  755.8 33.9 reduce-scatter.67
  949.8 32.3 reduce-scatter.69
  1007.1 32.5 reduce-scatter.71
  1211.6 20.1 reduce-scatter.111
  1250.2 21.0 reduce-scatter.75
  1278.9 76.5 reduce-scatter.77
  1358.4 74.5 reduce-scatter.79
  1508.3 20.2 reduce-scatter.113
  1544.9 21.1 reduce-scatter.81
  1573.7 76.5 reduce-scatter.83
  1653.0 74.6 reduce-scatter.85
  1802.7 20.1 reduce-scatter.115
  1840.0 21.1 reduce-scatter.87
  1868.7 76.6 reduce-scatter.89
  1948.2 74.5 reduce-scatter.91
  2097.5 20.2 reduce-scatter.117
  2134.9 21.1 reduce-scatter.93
  2163.6 76.6 reduce-scatter.95
  2243.1 74.5 reduce-scatter.97
  2392.7 20.2 reduce-scatter.119
  2430.1 21.1 reduce-scatter.99
  2456.4 76.6 reduce-scatter.103
  2535.9 74.5 reduce-scatter.101
  2613.2 31.8 reduce-scatter.73
  2647.8 23.1 reduce-scatter.125
  2673.8 24.5 reduce-scatter.123
  2701.2 44.9 reduce-scatter.105
  2749.3 44.9 reduce-scatter.121
  2797.4 98.0 reduce-scatter.127
  2907.3 98.2 reduce-scatter.107
  3008.6 98.1 reduce-scatter.109
where the time goes:
time: 3130 us; the launch traced here: 3120 us
  waiting for transfers between devices  1250 us (40%)
  blocking collectives  931 us (30%)
  matrix products  551 us (18%)
  local copies, waits for them, and re-layouts  229 us (7%)
  other arithmetic  133 us (4%)
    reduce_scatter x5, waiting for transfers between devices, layer_backward(): lax.psum_scatter(d_keys_all, ('ctx', 'wt'), scatter_dimension=0, tiled=True)  351 us
    reduce_scatter x5, waiting for transfers between devices, layer_backward(): lax.psum_scatter(d_values_all, ('ctx', 'wt'), scatter_dimension=0, tiled=...  343 us
    all_gather x5, blocking collectives, fetch_keys(): lax.all_gather(key_rows, ('ctx', 'wt'), axis=0, tiled=True)  205 us
    psum x20, blocking collectives, feature_sum(): return lax.psum(values, 'wt')  200 us
    all_gather x5, blocking collectives, fetch_keys(): lax.all_gather(value_rows, ('ctx', 'wt'), axis=0, tiled=True)  190 us
    reduce_scatter x5, waiting for transfers between devices, layer_forward(): lax.psum_scatter(jnp.dot(normed_first, w_proj, preferred_element_type=jnp...  145 us
    dot_general x5, matrix products, layer_backward(): jnp.dot(normed_second_full.T, d_both, preferred_element_type=jnp.float32)  125 us
    unnamed x450, local copies, waits for them, and re-layouts  112 us
  transfers between devices with their start and end apart: 47, of which 37 were waited for; matrix products, arithmetic and copies ran while one was open for 15% of the time, Pallas kernels for 0%

commit v1 on v0

v1 whole, which is shorter than its diff:
```python
import math

import jax
import jax.numpy as jnp
from jax import lax
from jax.sharding import PartitionSpec as P

EPS = 1e-06
ROPE_LOG = math.log(10000.0)
NEG_FILL = -1e30
LANES = 128
STREAMS = 1
BF = jnp.bfloat16
F32 = jnp.float32


def shift(value, axis, steps, group=None):
    count = lax.axis_size(axis)
    group = count if group is None else group
    pairs = [(i, i // group * group + (i % group + steps) % group) for i in range(count)]
    return lax.ppermute(value, axis, pairs)


def mm(a, b):
    return jnp.dot(a, b, preferred_element_type=F32)


def mm_nt(a, b):
    return lax.dot_general(a, b, (((1,), (1,)), ((), ())), preferred_element_type=F32)


def mm_tn(a, b):
    return lax.dot_general(a, b, (((0,), (0,)), ((), ())), preferred_element_type=F32)


def pick(index, options):
    result = options[0]
    for number in range(1, len(options)):
        result = jnp.where(index == number, options[number], result)
    return result


def gather_parts(value, axis):
    count = lax.axis_size(axis)
    me = lax.axis_index(axis)
    parts = [value] + [shift(value, axis, s) for s in range(1, count)]
    return [pick((me - place) % count, parts) for place in range(count)]


def gather_cols(value, axis):
    return jnp.concatenate(gather_parts(value, axis), axis=1)


def gather_rows(value, axis):
    count = lax.axis_size(axis)
    me = lax.axis_index(axis)
    rows = value.shape[0]
    full = jnp.zeros((count * rows, value.shape[1]), value.dtype)
    for s in range(count):
        part = value if s == 0 else shift(value, axis, s)
        full = lax.dynamic_update_slice_in_dim(full, part, (me - s) % count * rows, 0)
    return full


def reduce_rows(value, axis):
    count = lax.axis_size(axis)
    me = lax.axis_index(axis)
    rows = value.shape[0] // count
    total = lax.dynamic_slice_in_dim(value, me * rows, rows, 0).astype(F32)
    for s in range(1, count):
        block = lax.dynamic_slice_in_dim(value, (me + s) % count * rows, rows, 0)
        total = total + shift(block, axis, s).astype(F32)
    return total


def reduce_cols(value, axis):
    count = lax.axis_size(axis)
    me = lax.axis_index(axis)
    width = value.shape[1] // count
    blocks = [value[:, p * width : (p + 1) * width] for p in range(count)]
    total = pick(me, blocks).astype(F32)
    for s in range(1, count):
        total = total + shift(pick((me + s) % count, blocks), axis, s).astype(F32)
    return total


def sum_small(value, axis):
    total = value
    for s in range(1, lax.axis_size(axis)):
        total = total + shift(value, axis, s)
    return total


def split_two(value):
    high = lax.reduce_precision(value, 8, 7)
    return high, value - high


def side_columns(terms):
    rows = terms[0].shape[0]
    column = lax.broadcasted_iota(jnp.int32, (rows, LANES), 1)
    block = jnp.zeros((rows, LANES), F32)
    for number, term in enumerate(terms):
        high, low = split_two(term)
        block = jnp.where(column == 2 * number, high[:, None], block)
        block = jnp.where(column == 2 * number + 1, low[:, None], block)
    return block.astype(BF)


def rope(positions, head_size):
    half = head_size // 2
    freqs = jnp.exp(jnp.arange(half, dtype=F32) * (-2.0 * ROPE_LOG / head_size))
    angles = positions.astype(F32)[:, None] * freqs
    return jnp.cos(angles), jnp.sin(angles)


def rotate(values, cosine, sine):
    half = values.shape[-1] // 2
    first = values[..., :half]
    second = values[..., half:]
    return jnp.concatenate([first * cosine - second * sine, second * cosine + first * sine], axis=-1)


def gelu_tanh(values):
    return jax.nn.gelu(values, approximate=True)


class Layout:
    def __init__(self, block_pos, first_micro, micros, row_count):
        self.n_wt = lax.axis_size("wt")
        self.n_ctx = lax.axis_size("ctx")
        self.group = self.n_wt // micros
        wt = lax.axis_index("wt")
        ctx = lax.axis_index("ctx")
        self.rows = row_count // self.group
        block_row = lax.dynamic_index_in_dim(block_pos, first_micro + wt // self.group, 0, keepdims=False)
        block_len = row_count * self.n_ctx // block_pos.shape[1]
        mine = wt % self.group

        def positions(ctx_at, group_at):
            places = ctx_at * row_count + group_at * self.rows + jnp.arange(self.rows, dtype=jnp.int32)
            blocks = (places // block_len)[:, None] == jnp.arange(block_row.shape[0], dtype=jnp.int32)[None, :]
            return jnp.sum(jnp.where(blocks, block_row[None, :], 0), axis=1) * block_len + places % block_len

        self.query_pos = positions(ctx, mine)
        self.key_pos = jnp.concatenate(
            [
                positions((ctx - s) % self.n_ctx, (mine - j) % self.group)
                for s in range(self.n_ctx)
                for j in range(self.group)
            ]
        )

    def gather_keys(self, rows):
        near = jnp.concatenate([rows] + [shift(rows, "wt", j, self.group) for j in range(1, self.group)], axis=0)
        return jnp.concatenate([near] + [shift(near, "ctx", s) for s in range(1, self.n_ctx)], axis=0)

    def reduce_keys(self, rows):
        near_rows = self.rows * self.group
        near = rows[:near_rows].astype(F32)
        for s in range(1, self.n_ctx):
            near = near + shift(rows[s * near_rows : (s + 1) * near_rows].astype(BF), "ctx", -s).astype(F32)
        total = near[: self.rows]
        for j in range(1, self.group):
            block = near[j * self.rows : (j + 1) * self.rows].astype(BF)
            total = total + shift(block, "wt", -j, self.group).astype(F32)
        return total


def layer_forward(source, layout, params):
    gain_first, gain_second, w_proj, w_out, w_gate, w_up, w_down = params
    query_width = w_out.shape[0]
    head_size = (w_proj.shape[1] - query_width) // 2
    head_count = query_width // head_size
    width_all = source.shape[1] * layout.n_wt
    rows = layout.rows
    square = jnp.sum(source * source, axis=1)
    scaled = (source * gain_first).astype(BF)
    partial = jnp.concatenate([mm(scaled, w_proj).astype(BF), side_columns([square])], axis=1)
    total = reduce_rows(partial, "wt")
    proj_width = query_width + 2 * head_size
    square_all = total[:, proj_width] + total[:, proj_width + 1]
    inv_first = lax.rsqrt(square_all / width_all + EPS)
    projected = total[:, :proj_width] * inv_first[:, None]
    cosine, sine = rope(layout.query_pos, head_size)
    queries = rotate(
        projected[:, :query_width].reshape(rows, head_count, head_size), cosine[:, None], sine[:, None]
    ).astype(BF)
    key_rows = rotate(projected[:, query_width : query_width + head_size], cosine, sine).astype(BF)
    value_rows = projected[:, query_width + head_size :].astype(BF)
    pairs_all = layout.gather_keys(jnp.concatenate([key_rows, value_rows], axis=1))
    all_keys = pairs_all[:, :head_size]
    all_values = pairs_all[:, head_size:]
    query_rows = queries.reshape(rows * head_count, head_size)
    row_pos = jnp.repeat(layout.query_pos, head_count)
    raw = mm_nt(query_rows, all_keys) * head_size ** (-0.5)
    scores = jnp.where(layout.key_pos[None, :] <= row_pos[:, None], raw, NEG_FILL)
    row_max = jnp.max(scores, axis=1, keepdims=True)
    raised = jnp.exp(scores - row_max)
    log_total = row_max + jnp.log(jnp.sum(raised, axis=1, keepdims=True))
    probs = jnp.exp(scores - log_total)
    probs_low = probs.astype(BF)
    attended = mm(probs_low, all_values).astype(BF).reshape(rows, query_width)
    attended_full = gather_rows(attended, "wt")
    middle = source + mm(attended_full, w_out)
    middle_full = gather_cols(middle.astype(BF), "wt").astype(F32)
    inv_second = lax.rsqrt(jnp.sum(middle_full * middle_full, axis=1) / width_all + EPS)
    normed_second = (middle_full * inv_second[:, None] * gain_second).astype(BF)
    gate_pre = mm(normed_second, w_gate)
    up_pre = mm(normed_second, w_up)
    hidden_act = (gelu_tanh(gate_pre) * up_pre).astype(BF)
    update = reduce_cols(mm(hidden_act, w_down).astype(BF), "wt")
    saved = (
        source,
        inv_first,
        projected,
        query_rows,
        all_keys,
        all_values,
        probs,
        attended_full,
        middle,
        inv_second,
        normed_second,
        gate_pre,
        up_pre,
        hidden_act,
        cosine,
        sine,
    )
    return middle + update, saved


def layer_backward(grad_out, layout, saved, params):
    gain_first, gain_second, w_proj, w_out, w_gate, w_up, w_down = params
    (
        source,
        inv_first,
        projected,
        query_rows,
        all_keys,
        all_values,
        probs,
        attended_full,
        middle,
        inv_second,
        normed_second,
        gate_pre,
        up_pre,
        hidden_act,
        cosine,
        sine,
    ) = saved
    query_width = w_out.shape[0]
    proj_width = w_proj.shape[1]
    head_size = (proj_width - query_width) // 2
    head_count = query_width // head_size
    width_all = source.shape[1] * layout.n_wt
    rows = layout.rows
    score_scale = head_size ** (-0.5)
    grad_full = gather_cols(grad_out.astype(BF), "wt")
    d_hidden = mm_nt(grad_full, w_down)
    activated, pull_back = jax.vjp(gelu_tanh, gate_pre)
    d_gate = pull_back(d_hidden * up_pre)[0].astype(BF)
    d_up = (d_hidden * activated).astype(BF)
    inner_part = jnp.sum(d_gate.astype(F32) * gate_pre + d_up.astype(F32) * up_pre, axis=1)
    inner = sum_small(inner_part, "wt") / (inv_second * width_all)
    d_normed = reduce_cols((mm_nt(d_gate, w_gate) + mm_nt(d_up, w_up)).astype(BF), "wt")
    d_middle = (
        grad_out
        + inv_second[:, None] * d_normed * gain_second_local(gain_second, source.shape[1])
        - middle * (inv_second**3 * inner)[:, None]
    )
    d_gain_second = jnp.sum(d_normed * middle * inv_second[:, None], axis=0)
    d_middle_low = d_middle.astype(BF)
    d_attended = reduce_rows(mm_nt(d_middle_low, w_out).astype(BF), "wt").astype(BF)
    d_rows = d_attended.reshape(rows * head_count, head_size)
    probs_low = probs.astype(BF)
    d_values_all = mm_tn(probs_low, d_rows)
    d_probs = mm_nt(d_rows, all_values)
    delta = jnp.sum(probs * d_probs, axis=1, keepdims=True)
    d_scores = (probs * (d_probs - delta) * score_scale).astype(BF)
    d_query_rows = mm(d_scores, all_keys)
    d_keys_all = mm_tn(d_scores, query_rows)
    d_pairs = layout.reduce_keys(jnp.concatenate([d_keys_all, d_values_all], axis=1))
    d_query = rotate(
        d_query_rows.reshape(rows, head_count, head_size), cosine[:, None], -sine[:, None]
    ).reshape(rows, query_width)
    d_key = rotate(d_pairs[:, :head_size], cosine, -sine)
    d_projected = jnp.concatenate([d_query, d_key, d_pairs[:, head_size:]], axis=1).astype(BF)
    inner_own = jnp.sum(d_projected.astype(F32) * projected, axis=1) * inv_first * inv_first / width_all
    packed = gather_rows(jnp.concatenate([d_projected, side_columns([inv_first, inner_own])], axis=1), "wt")
    d_projected_full = packed[:, :proj_width]
    side = packed[:, proj_width : proj_width + 4].astype(F32)
    inv_full = side[:, 0:1] + side[:, 1:2]
    inner_full = side[:, 2:3] + side[:, 3:4]
    d_first = mm_nt(d_projected_full, w_proj)
    d_source = d_middle + inv_full * d_first * gain_first - source * inner_full
    d_gain_first = jnp.sum(d_first * source * inv_full, axis=0)
    normed_first = (source * inv_full * gain_first).astype(BF)
    terms = dict(
        act=hidden_act,
        grad=grad_full,
        normed=normed_second,
        d_gate=d_gate,
        d_up=d_up,
        attended=attended_full,
        d_middle=d_middle_low,
        first=normed_first,
        d_projected=d_projected_full,
    )
    return d_source, terms, d_gain_first, d_gain_second


def gain_second_local(gain_full, width):
    return lax.dynamic_slice_in_dim(gain_full, lax.axis_index("wt") * width, width, 0)


def both_sections(value):
    count = lax.axis_size("section")
    return jnp.concatenate([value] + [shift(value, "section", s) for s in range(1, count)], axis=0)


def both_halves(section_id, low, high):
    own = jnp.where(section_id == 0, low, high)
    other = jnp.where(section_id == 0, high, low)
    return jnp.concatenate([own, shift(other, "section", 1)], axis=0)


def halves(value):
    width = value.shape[1] // 2
    return value[:, :width], value[:, width:]


def by_owner(value, query_width, head_size, n_ctx):
    query_part = query_width // n_ctx
    head_part = head_size // n_ctx
    pieces = []
    for c in range(n_ctx):
        pieces.append(value[:, c * query_part : (c + 1) * query_part])
        for base in (query_width, query_width + head_size):
            pieces.append(value[:, base + c * head_part : base + (c + 1) * head_part])
    return jnp.concatenate(pieces, axis=1)


def weight_grads(section_id, terms, query_width, head_size):
    n_ctx = lax.axis_size("ctx")

    def keep(partial):
        return lax.psum_scatter(partial.astype(BF), "ctx", scatter_dimension=0, tiled=True)

    grad = both_sections(terms["grad"])
    down = keep(mm_tn(grad, both_halves(section_id, *halves(terms["act"]))))
    normed = both_sections(terms["normed"])
    gate_up = keep(mm_tn(normed, both_halves(section_id, terms["d_gate"], terms["d_up"])))
    attended = both_sections(terms["attended"])
    out = keep(mm_tn(attended, both_halves(section_id, *halves(terms["d_middle"]))))
    projected = both_sections(by_owner(terms["d_projected"], query_width, head_size, n_ctx))
    proj = keep(mm_tn(projected, both_halves(section_id, *halves(terms["first"]))))
    return down, gate_up, out, proj


def home(section_id, first_block, second_block):
    kept = jnp.where(section_id == 0, first_block, second_block)
    sent = jnp.where(section_id == 0, second_block, first_block)
    received = shift(sent, "section", 1)
    low = jnp.where(section_id == 0, kept, received)
    high = jnp.where(section_id == 0, received, kept)
    return low, high


def local(hidden_in, out_grad, block_pos, norm1_gain, norm2_gain, wq, wk, wv, wo, w_gate, w_up, w_down):
    n_section = lax.axis_size("section")
    assert n_section == 2
    n_ctx = lax.axis_size("ctx")
    section_id = lax.axis_index("section")
    micro_count, row_count, width = hidden_in.shape
    micro_own = micro_count // n_section
    query_width = wq.shape[2]
    head_size = wk.shape[2]

    def fetch(weight):
        return lax.all_gather(weight, "section", axis=0, tiled=False)

    w_proj = fetch(jnp.concatenate([wq[0], wk[0], wv[0]], axis=1))
    weights = [w_proj] + [fetch(w[0]) for w in (wo, w_gate, w_up, w_down)]
    gains = jnp.concatenate([norm1_gain, norm2_gain], axis=0)
    other_gains = shift(gains, "section", 1)
    gains = jnp.concatenate(
        [jnp.where(section_id == 0, gains, other_gains), jnp.where(section_id == 0, other_gains, gains)], axis=0
    )
    gains_full = gather_cols(gains, "wt")
    params = [
        (gains[2 * l], gains_full[2 * l + 1]) + tuple(w[l] for w in weights) for l in range(n_section)
    ]
    first_micro = section_id * micro_own
    micros = micro_own // STREAMS
    hidden = lax.dynamic_slice_in_dim(hidden_in, first_micro, micro_own, 0)
    cotangent = lax.dynamic_slice_in_dim(out_grad, first_micro, micro_own, 0)
    layouts = [Layout(block_pos, first_micro + k * micros, micros, row_count) for k in range(STREAMS)]

    def rows_of(value, k):
        return value[k * micros : (k + 1) * micros].reshape(micros * row_count, width).astype(F32)

    states = [rows_of(hidden, k) for k in range(STREAMS)]
    saved = []
    for l in range(n_section):
        results = [layer_forward(states[k], layouts[k], params[l]) for k in range(STREAMS)]
        states = [result[0] for result in results]
        saved.append([result[1] for result in results])
    out_own = jnp.concatenate([state.astype(BF) for state in states], axis=0)
    grads = [rows_of(cotangent, k) for k in range(STREAMS)]
    blocks = {}
    gain_grads = {}
    for l in reversed(range(n_section)):
        results = [layer_backward(grads[k], layouts[k], saved[l][k], params[l]) for k in range(STREAMS)]
        grads = [result[0] for result in results]
        terms = {
            name: jnp.concatenate([result[1][name] for result in results], axis=0) for name in results[0][1]
        }
        blocks[l] = weight_grads(section_id, terms, query_width, head_size)
        gain_grads[l] = jnp.stack([sum(r[2] for r in results), sum(r[3] for r in results)])
    in_grad_own = jnp.concatenate(grads, axis=0)

    def everywhere(own):
        low, high = own, shift(own, "section", 1)
        both = jnp.concatenate(
            [jnp.where(section_id == 0, low, high), jnp.where(section_id == 0, high, low)], axis=0
        )
        return both.reshape(micro_count, row_count, width)

    out = everywhere(out_own)
    in_grad = everywhere(in_grad_own)
    gain_sum = lax.psum(jnp.stack([gain_grads[0], gain_grads[1]]), ("section", "ctx"))
    gain_mine = jnp.where(section_id == 0, gain_sum[0], gain_sum[1])
    down, gate_up, out_w, proj = (home(section_id, a, b) for a, b in zip(blocks[0], blocks[1]))
    grad_down = jnp.concatenate(down, axis=1).T.astype(F32)
    grad_gate, grad_up = (half.astype(F32) for half in gate_up)
    grad_wo = jnp.concatenate(out_w, axis=1).astype(F32)
    grad_proj = jnp.concatenate(proj, axis=1).T.astype(F32)
    query_part = query_width // n_ctx
    head_part = head_size // n_ctx
    return (
        out,
        in_grad,
        grad_proj[:, :query_part][None],
        grad_proj[:, query_part : query_part + head_part][None],
        grad_proj[:, query_part + head_part :][None],
        grad_wo[None],
        grad_gate[None],
        grad_up[None],
        grad_down[None],
        gain_mine[0][None],
        gain_mine[1][None],
    )


def solution(mesh):
    return jax.shard_map(
        local,
        mesh=mesh,
        in_specs=(
            P(None, "ctx", "wt"),
            P(None, "ctx", "wt"),
            P(),
            P("section", "wt"),
            P("section", "wt"),
            P("section", "wt", None),
            P("section", "wt", None),
            P("section", "wt", None),
            P("section", None, "wt"),
            P("section", None, "wt"),
            P("section", None, "wt"),
            P("section", "wt", None),
        ),
        out_specs=(
            P(None, "ctx", "wt"),
            P(None, "ctx", "wt"),
            P("section", "wt", "ctx"),
            P("section", "wt", "ctx"),
            P("section", "wt", "ctx"),
            P("section", "ctx", "wt"),
            P("section", "ctx", "wt"),
            P("section", "ctx", "wt"),
            P("section", "wt", "ctx"),
            P("section", "wt"),
            P("section", "wt"),
        ),
        check_vma=False,
    )
```

time: 3130 us -> 1200 us (0.38)
  blocking collectives: 931 us -> 27.3 us
  waiting for transfers between devices: 1250 us -> 586 us
  matrix products: 551 us -> 167 us
  starting transfers between devices: 3.05 us -> 173 us
  local copies, waits for them, and re-layouts: 229 us -> 150 us
  other arithmetic: 133 us -> 67.4 us
    reduce_scatter x28 -> x4, waiting for transfers between devices: 1150 us -> 200 us  [keep(): lax.psum_scatter(partial.astype(BF), 'ctx', scatter_dimension=0, tiled=True)]
    all_gather x30 -> x0, blocking collectives: 722 us -> none  [the longest x5 205 us: fetch_keys(): lax.all_gather(key_rows, ('ctx', 'wt'), axis=0, tiled=True)]
    dot_general x95 -> x40, matrix products: 551 us -> 167 us  [the longest x14 57.9 us: mm(): return jnp.dot(a, b, preferred_element_type=F32)]
    ppermute x10 -> x96, waiting for transfers between devices: 11 us -> 315 us  [shift(): return lax.ppermute(value, axis, pairs)]
    psum x21 -> x1, blocking collectives: 209 us -> 27.3 us  [local(): lax.psum(jnp.stack([gain_grads[0], gain_grads[1]]), ('section', 'ctx'))]
    ppermute x10 -> x96, starting transfers between devices: 0.71 us -> 171 us  [shift(): return lax.ppermute(value, axis, pairs)]
    dynamic_update_slice x0 -> x16, local copies, waits for them, and re-layouts: none -> 62.7 us  [gather_rows(): lax.dynamic_update_slice_in_dim(full, part, (me - s) % count * rows, 0)]
    unnamed x450 -> x319, local copies, waits for them, and re-layouts: 112 us -> 58.5 us
  transfers between devices with their start and end apart: 47 -> 109, of which waited for: 37 -> 55; matrix products, arithmetic and copies ran while one was open for 15% -> 27% of each run, Pallas kernels for 0% -> 0%
where the time goes in v1:
time: 1200 us; the launch traced here: 1190 us
  waiting for transfers between devices  586 us (49%)
  starting transfers between devices  173 us (14%)
  matrix products  167 us (14%)
  local copies, waits for them, and re-layouts  150 us (12%)
  other arithmetic  67.4 us (6%)
  blocking collectives  27.3 us (2%)
  between operations  17.1 us (1%)
    ppermute x96, waiting for transfers between devices, shift(): return lax.ppermute(value, axis, pairs)  315 us
    reduce_scatter x4, waiting for transfers between devices, keep(): lax.psum_scatter(partial.astype(BF), 'ctx', scatter_dimension=0, tiled=True)  200 us
    ppermute x96, starting transfers between devices, shift(): return lax.ppermute(value, axis, pairs)  171 us
    dynamic_update_slice x16, local copies, waits for them, and re-layouts, gather_rows(): lax.dynamic_update_slice_in_dim(full, part, (me - s) % count * rows, 0)  62.7 us
    unnamed x17, waiting for transfers between devices  59 us
    unnamed x319, local copies, waits for them, and re-layouts  58.5 us
    dot_general x14, matrix products, mm(): return jnp.dot(a, b, preferred_element_type=F32)  57.9 us
    dot_general x14, matrix products, mm_nt(): lax.dot_general(a, b, (((1,), (1,)), ((), ())), preferred_element_type=F32)  57.7 us
  transfers between devices with their start and end apart: 109, of which 55 were waited for; matrix products, arithmetic and copies ran while one was open for 27% of the time, Pallas kernels for 0%

profile of v1, /device:TPU:0, one launch (start us, length us, event | category | flops | bytes accessed | tf_op | source)
XLA Modules:
  0.0 1187.8 jit_solution(4893346376339277154)
XLA Ops:
  20.8 12.3 %all-gather.15.cloned.1.call-done = bf16[1280,3072]{1,0:T(8,128)(2,1)} async-done(((bf16[640,3072]{1,0:T(8,128)(2,1)}), bf16[1280,3072]{1,0:T(8,128)(2,1)}) %all-gather.15.cloned.1.call-update) | async-done | bytes 7864336 | tf_op jit(solution)/shard_map/all_gather | solution.py:383
  45.7 32.7 %collective-permute-done.15 = f32[4,640]{1,0:T(4,128)S(1)} collective-permute-done((f32[4,640]{1,0:T(4,128)S(1)}, f32[4,640]{1,0:T(4,128)S(1)}, u32[]{:S(2)}, u32[]{:S(2)}) %collective-permute-start.15) | collective-permute-done | bytes 10272 | tf_op jit(solution)/shard_map/ppermute | solution.py:21
  101.6 8.5 collective-permute-done.8
  110.1 11.3 collective-permute-done.9
  139.8 22.2 %collective-permute-done.12 = bf16[256,640]{1,0:T(8,128)(2,1)S(1)} collective-permute-done((bf16[256,640]{1,0:T(8,128)(2,1)S(1)}, bf16[256,640]{1,0:T(8,128)(2,1)S(1)}, u32[]{:S(2)}, u32[]{:S(2)}) %collective-permute-start.12) | collective-permute-done | bytes 327712 | tf_op jit(solution)/shard_map/ppermute | solution.py:21
  164.1 7.1 fusion.1
  171.2 9.4 multiply_convert_fusion.3
  180.6 7.0 fusion.15
  193.2 8.0 collective-permute-done.17
  201.2 11.8 collective-permute-done.18
  237.7 12.5 %collective-permute-done.21 = bf16[64,3200]{1,0:T(8,128)(2,1)S(1)} collective-permute-done((bf16[64,3200]{1,0:T(8,128)(2,1)S(1)}, bf16[64,3200]{1,0:T(8,128)(2,1)S(1)}, u32[]{:S(2)}, u32[]{:S(2)}) %collective-permute-start.21) | collective-permute-done | bytes 409632 | tf_op jit(solution)/shard_map/ppermute | solution.py:21
  256.4 22.9 %collective-permute-start.23 = (bf16[64,512]{1,0:T(8,128)(2,1)S(1)}, bf16[64,512]{1,0:T(8,128)(2,1)S(1)}, u32[]{:S(2)}, u32[]{:S(2)}) collective-permute-start(bf16[64,512]{1,0:T(8,128)(2,1)S(1)} %get-tuple-element.201), channel_id=1, source_target_pairs={{0,1},{1,0},{2,3},{3,2},{4,5},{5,4},{6,7},{7,6},{8,9},{9,8},{10,11... | collective-permute-start | bytes 196616 | tf_op jit(solution)/shard_map/ppermute | solution.py:21
  279.3 8.3 collective-permute-done.23
  307.3 7.3 collective-permute-done.27
  342.9 20.9 %collective-permute-done.31 = bf16[256,640]{1,0:T(8,128)(2,1)} collective-permute-done((bf16[256,640]{1,0:T(8,128)(2,1)S(1)}, bf16[256,640]{1,0:T(8,128)(2,1)}, u32[]{:S(2)}, u32[]{:S(2)}) %collective-permute-start.31) | collective-permute-done | bytes 327712 | tf_op jit(solution)/shard_map/ppermute | solution.py:21
  366.1 7.4 fusion.7
  378.5 8.7 broadcast_select_fusion.7
  398.2 6.8 fusion.17
  407.3 6.8 fusion.14
  421.3 18.4 %collective-permute-done.41 = bf16[256,640]{1,0:T(8,128)(2,1)S(1)} collective-permute-done((bf16[256,640]{1,0:T(8,128)(2,1)S(1)}, bf16[256,640]{1,0:T(8,128)(2,1)S(1)}, u32[]{:S(2)}, u32[]{:S(2)}) %collective-permute-start.41) | collective-permute-done | bytes 327712 | tf_op jit(solution)/shard_map/ppermute | solution.py:21
  440.1 16.6 %collective-permute-done.34 = bf16[256,640]{1,0:T(8,128)(2,1)S(1)} collective-permute-done((bf16[256,640]{1,0:T(8,128)(2,1)S(1)}, bf16[256,640]{1,0:T(8,128)(2,1)S(1)}, u32[]{:S(2)}, u32[]{:S(2)}) %collective-permute-start.34) | collective-permute-done | bytes 327712 | tf_op jit(solution)/shard_map/ppermute | solution.py:21
  460.3 7.0 collective-permute-start.46
  476.7 10.6 collective-permute-done.47
  501.4 7.6 collective-permute-start.52
  524.3 8.3 dynamic_update_slice.56
  542.7 9.8 dynamic_update_slice.57
  553.7 8.2 dynamic_update_slice.58
  564.1 10.0 dynamic_update_slice.59
  596.0 15.4 %collective-permute-done.57 = bf16[256,640]{1,0:T(8,128)(2,1)S(1)} collective-permute-done((bf16[256,640]{1,0:T(8,128)(2,1)S(1)}, bf16[256,640]{1,0:T(8,128)(2,1)S(1)}, u32[]{:S(2)}, u32[]{:S(2)}) %collective-permute-start.57) | collective-permute-done | bytes 327712 | tf_op jit(solution)/shard_map/ppermute | solution.py:21
  611.7 9.2 broadcast_select_fusion.9
  627.4 6.7 fusion.16
  643.5 7.2 collective-permute-done.59
  650.7 12.3 %collective-permute-done.60 = bf16[256,640]{1,0:T(8,128)(2,1)S(1)} collective-permute-done((bf16[256,640]{1,0:T(8,128)(2,1)S(1)}, bf16[256,640]{1,0:T(8,128)(2,1)S(1)}, u32[]{:S(2)}, u32[]{:S(2)}) %collective-permute-start.60) | collective-permute-done | bytes 327712 | tf_op jit(solution)/shard_map/ppermute | solution.py:21
  668.5 6.6 collective-permute-start.65
  683.5 10.4 collective-permute-done.66
  709.5 12.7 %collective-permute-start.71 = (bf16[64,512]{1,0:T(8,128)(2,1)S(1)}, bf16[64,512]{1,0:T(8,128)(2,1)S(1)}, u32[]{:S(2)}, u32[]{:S(2)}) collective-permute-start(bf16[64,512]{1,0:T(8,128)(2,1)S(1)} %slice.984), channel_id=1, source_target_pairs={{0,1},{1,0},{2,3},{3,2},{4,5},{5,4},{6,7},{7,6},{8,9},{9,8},{10,11... | collective-permute-start | bytes 196616 | tf_op jit(solution)/shard_map/ppermute | solution.py:21
  743.8 6.6 dynamic_update_slice.61
  760.8 7.4 dynamic_update_slice.63
  782.6 11.0 convolution_convert_fusion.2
  793.6 8.0 copy.93
  806.8 11.0 convolution_convert_fusion.3
  817.8 7.9 copy.91
  830.7 8.1 convolution_convert_fusion
  843.6 8.2 convolution_convert_fusion.1
  855.6 27.3 %psum.7 = f32[2,2,640]{2,1,0:T(2,128)S(1)} all-reduce(f32[2,2,640]{2,1,0:T(2,128)S(1)} %pad_maximum_fusion.20), channel_id=1, replica_groups=mesh['section'=2,'ctx'=4,'wt'=4] {'section','ctx'}, use_global_device_ids=true, to_apply=%region_35.36 | all-reduce | flops 2560 | bytes 20480 | tf_op jit(solution)/shard_map/psum | solution.py:434
  892.6 56.4 %reduce-scatter.29.cloned.1.call-done = bf16[640,960]{1,0:T(8,128)(2,1)} async-done(((bf16[2560,960]{1,0:T(8,128)(2,1)}), bf16[640,960]{1,0:T(8,128)(2,1)}) %reduce-scatter.29.cloned.1.call-update) | async-done | bytes 1228816
  951.1 99.0 %reduce-scatter.23.cloned.1.call-done = bf16[640,1920]{1,0:T(8,128)(2,1)} async-done(((bf16[2560,1920]{1,0:T(8,128)(2,1)}), bf16[640,1920]{1,0:T(8,128)(2,1)}) %reduce-scatter.23.cloned.1.call-update) | async-done | bytes 2457616 | tf_op jit(solution)/shard_map/reduce_scatter | solution.py:350
  1050.1 101.3 %reduce-scatter.21.cloned.1.call-done = bf16[640,1920]{1,0:T(8,128)(2,1)} async-done(((bf16[2560,1920]{1,0:T(8,128)(2,1)}), bf16[640,1920]{1,0:T(8,128)(2,1)}) %reduce-scatter.21.cloned.1.call-update) | async-done | bytes 2457616 | tf_op jit(solution)/shard_map/reduce_scatter | solution.py:350
  (754 shorter events, 409.7 us)
Async XLA Ops:
  7.2 25.9 %all-gather.15.cloned.1.call-start = ((), (), s32[]{:S(2)}) async-start(), calls=%async_computation.16 | async-start | bytes 11796480 | tf_op jit(solution)/shard_map/all_gather | solution.py:383
  11.1 110.4 %all-gather.7.cloned.1.call-start = ((), (), s32[]{:S(2)}) async-start(), calls=%async_computation.8 | async-start | bytes 9830400 | tf_op jit(solution)/shard_map/all_gather | solution.py:383
  11.9 152.2 %all-gather.9.cloned.1.call-start = ((), (), s32[]{:S(2)}) async-start(), calls=%async_computation.9 | async-start | bytes 29491200 | tf_op jit(solution)/shard_map/all_gather | solution.py:383
  12.6 158.6 %all-gather.11.cloned.1.call-start = ((), (), s32[]{:S(2)}) async-start(), calls=%async_computation.10 | async-start | bytes 29491200 | tf_op jit(solution)/shard_map/all_gather | solution.py:383
  13.2 167.4 %all-gather.13.cloned.1.call-start = ((), (), s32[]{:S(2)}) async-start(), calls=%async_computation.11 | async-start | bytes 29491200 | tf_op jit(solution)/shard_map/all_gather | solution.py:383
  13.8 871.0 %reduce-scatter.27.cloned.1.call-start = ((), (), s32[]{:S(2)}) async-start(), calls=%async_computation.18 | async-start | bytes 2457600
  15.6 28.8 %collective-permute-start.14 = (f32[4,640]{1,0:T(4,128)S(1)}, f32[4,640]{1,0:T(4,128)S(1)}, u32[]{:S(2)}, u32[]{:S(2)}) collective-permute-start(f32[4,640]{1,0:T(4,128)S(1)} %pad_maximum_fusion.19), channel_id=1, source_target_pairs={{0,3},{1,0},{2,1},{3,2},{4,7},{5,4},{6,5},{7,6},{8,11},{9,8},{10,9... | collective-permute-start | bytes 30728 | tf_op jit(solution)/shard_map/ppermute | solution.py:21
  37.7 41.4 %collective-permute-start.1 = (bf16[64,3200]{1,0:T(8,128)(2,1)}, bf16[64,3200]{1,0:T(8,128)(2,1)S(1)}, u32[]{:S(2)}, u32[]{:S(2)}) collective-permute-start(bf16[64,3200]{1,0:T(8,128)(2,1)} %get-tuple-element.121), channel_id=1, source_target_pairs={{0,1},{1,2},{2,3},{3,0},{4,5},{5,6},{6,7},{7,4},{8,9},{9,10},{10,1... | collective-permute-start | bytes 1228808 | tf_op jit(solution)/shard_map/ppermute | solution.py:21
  39.4 39.7 %collective-permute-start.2 = (bf16[64,3200]{1,0:T(8,128)(2,1)}, bf16[64,3200]{1,0:T(8,128)(2,1)}, u32[]{:S(2)}, u32[]{:S(2)}) collective-permute-start(bf16[64,3200]{1,0:T(8,128)(2,1)} %get-tuple-element.122), channel_id=1, source_target_pairs={{0,2},{1,3},{2,0},{3,1},{4,6},{5,7},{6,4},{7,5},{8,10},{9,11},{10,... | collective-permute-start | bytes 1228808 | tf_op jit(solution)/shard_map/ppermute | solution.py:21
  41.8 37.2 %collective-permute-start.3 = (bf16[64,3200]{1,0:T(8,128)(2,1)}, bf16[64,3200]{1,0:T(8,128)(2,1)}, u32[]{:S(2)}, u32[]{:S(2)}) collective-permute-start(bf16[64,3200]{1,0:T(8,128)(2,1)} %get-tuple-element.123), channel_id=1, source_target_pairs={{0,3},{1,0},{2,1},{3,2},{4,7},{5,4},{6,5},{7,6},{8,11},{9,8},{10,9... | collective-permute-start | bytes 1228808 | tf_op jit(solution)/shard_map/ppermute | solution.py:21
  44.1 34.3 %collective-permute-start.15 = (f32[4,640]{1,0:T(4,128)S(1)}, f32[4,640]{1,0:T(4,128)S(1)}, u32[]{:S(2)}, u32[]{:S(2)}) collective-permute-start(f32[4,640]{1,0:T(4,128)S(1)} %pad_maximum_fusion.19), channel_id=1, source_target_pairs={{0,2},{1,3},{2,0},{3,1},{4,6},{5,7},{6,4},{7,5},{8,10},{9,11},{10,... | collective-permute-start | bytes 30728 | tf_op jit(solution)/shard_map/ppermute | solution.py:21
  44.4 34.0 %collective-permute-start.16 = (f32[4,640]{1,0:T(4,128)S(1)}, f32[4,640]{1,0:T(4,128)S(1)}, u32[]{:S(2)}, u32[]{:S(2)}) collective-permute-start(f32[4,640]{1,0:T(4,128)S(1)} %pad_maximum_fusion.19), channel_id=1, source_target_pairs={{0,1},{1,2},{2,3},{3,0},{4,5},{5,6},{6,7},{7,4},{8,9},{9,10},{10,1... | collective-permute-start | bytes 30728 | tf_op jit(solution)/shard_map/ppermute | solution.py:21
  131.9 30.2 %collective-permute-start.12 = (bf16[256,640]{1,0:T(8,128)(2,1)S(1)}, bf16[256,640]{1,0:T(8,128)(2,1)S(1)}, u32[]{:S(2)}, u32[]{:S(2)}) collective-permute-start(bf16[256,640]{1,0:T(8,128)(2,1)S(1)} %get-tuple-element.229), channel_id=1, source_target_pairs={{0,2},{1,3},{2,0},{3,1},{4,6},{5,7},{6,4},{7,5},{8,10},{9,11},{10,... | collective-permute-start | bytes 983048 | tf_op jit(solution)/shard_map/ppermute | solution.py:21
  133.9 28.2 %collective-permute-start.13 = (bf16[256,640]{1,0:T(8,128)(2,1)S(1)}, bf16[256,640]{1,0:T(8,128)(2,1)S(1)}, u32[]{:S(2)}, u32[]{:S(2)}) collective-permute-start(bf16[256,640]{1,0:T(8,128)(2,1)S(1)} %get-tuple-element.229), channel_id=1, source_target_pairs={{0,1},{1,2},{2,3},{3,0},{4,5},{5,6},{6,7},{7,4},{8,9},{9,10},{10,1... | collective-permute-start | bytes 983048 | tf_op jit(solution)/shard_map/ppermute | solution.py:21
  225.3 24.8 %collective-permute-start.21 = (bf16[64,3200]{1,0:T(8,128)(2,1)S(1)}, bf16[64,3200]{1,0:T(8,128)(2,1)S(1)}, u32[]{:S(2)}, u32[]{:S(2)}) collective-permute-start(bf16[64,3200]{1,0:T(8,128)(2,1)S(1)} %get-tuple-element.119), channel_id=1, source_target_pairs={{0,2},{1,3},{2,0},{3,1},{4,6},{5,7},{6,4},{7,5},{8,10},{9,11},{10,... | collective-permute-start | bytes 1228808 | tf_op jit(solution)/shard_map/ppermute | solution.py:21
  225.5 27.3 %collective-permute-start.22 = (bf16[64,3200]{1,0:T(8,128)(2,1)S(1)}, bf16[64,3200]{1,0:T(8,128)(2,1)S(1)}, u32[]{:S(2)}, u32[]{:S(2)}) collective-permute-start(bf16[64,3200]{1,0:T(8,128)(2,1)S(1)} %get-tuple-element.120), channel_id=1, source_target_pairs={{0,3},{1,0},{2,1},{3,2},{4,7},{5,4},{6,5},{7,6},{8,11},{9,8},{10,9... | collective-permute-start | bytes 1228808 | tf_op jit(solution)/shard_map/ppermute | solution.py:21
  228.5 107.3 %collective-permute-start.37 = (bf16[256,640]{1,0:T(8,128)(2,1)}, bf16[256,640]{1,0:T(8,128)(2,1)}, u32[]{:S(2)}, u32[]{:S(2)}) collective-permute-start(bf16[256,640]{1,0:T(8,128)(2,1)} %bitcast.16), channel_id=1, source_target_pairs={{0,3},{1,0},{2,1},{3,2},{4,7},{5,4},{6,5},{7,6},{8,11},{9,8},{10,9... | collective-permute-start | bytes 983048 | tf_op jit(solution)/shard_map/ppermute | solution.py:21
  230.5 106.0 %collective-permute-start.38 = (bf16[256,640]{1,0:T(8,128)(2,1)}, bf16[256,640]{1,0:T(8,128)(2,1)}, u32[]{:S(2)}, u32[]{:S(2)}) collective-permute-start(bf16[256,640]{1,0:T(8,128)(2,1)} %bitcast.16), channel_id=1, source_target_pairs={{0,2},{1,3},{2,0},{3,1},{4,6},{5,7},{6,4},{7,5},{8,10},{9,11},{10,... | collective-permute-start | bytes 983048 | tf_op jit(solution)/shard_map/ppermute | solution.py:21
  235.4 101.2 %collective-permute-start.39 = (bf16[256,640]{1,0:T(8,128)(2,1)}, bf16[256,640]{1,0:T(8,128)(2,1)}, u32[]{:S(2)}, u32[]{:S(2)}) collective-permute-start(bf16[256,640]{1,0:T(8,128)(2,1)} %bitcast.16), channel_id=1, source_target_pairs={{0,1},{1,2},{2,3},{3,0},{4,5},{5,6},{6,7},{7,4},{8,9},{9,10},{10,1... | collective-permute-start | bytes 983048 | tf_op jit(solution)/shard_map/ppermute | solution.py:21
  256.4 31.2 %collective-permute-start.23 = (bf16[64,512]{1,0:T(8,128)(2,1)S(1)}, bf16[64,512]{1,0:T(8,128)(2,1)S(1)}, u32[]{:S(2)}, u32[]{:S(2)}) collective-permute-start(bf16[64,512]{1,0:T(8,128)(2,1)S(1)} %get-tuple-element.201), channel_id=1, source_target_pairs={{0,1},{1,0},{2,3},{3,2},{4,5},{5,4},{6,7},{7,6},{8,9},{9,8},{10,11... | collective-permute-start | bytes 196616 | tf_op jit(solution)/shard_map/ppermute | solution.py:21
  334.8 29.1 %collective-permute-start.31 = (bf16[256,640]{1,0:T(8,128)(2,1)S(1)}, bf16[256,640]{1,0:T(8,128)(2,1)}, u32[]{:S(2)}, u32[]{:S(2)}) collective-permute-start(bf16[256,640]{1,0:T(8,128)(2,1)S(1)} %get-tuple-element.235), channel_id=1, source_target_pairs={{0,2},{1,3},{2,0},{3,1},{4,6},{5,7},{6,4},{7,5},{8,10},{9,11},{10,... | collective-permute-start | bytes 983048 | tf_op jit(solution)/shard_map/ppermute | solution.py:21
  335.8 28.0 %collective-permute-start.32 = (bf16[256,640]{1,0:T(8,128)(2,1)S(1)}, bf16[256,640]{1,0:T(8,128)(2,1)}, u32[]{:S(2)}, u32[]{:S(2)}) collective-permute-start(bf16[256,640]{1,0:T(8,128)(2,1)S(1)} %get-tuple-element.235), channel_id=1, source_target_pairs={{0,1},{1,2},{2,3},{3,0},{4,5},{5,6},{6,7},{7,4},{8,9},{9,10},{10,1... | collective-permute-start | bytes 983048 | tf_op jit(solution)/shard_map/ppermute | solution.py:21
  388.4 26.0 %collective-permute-start.43 = (f32[256]{0:T(256)S(1)}, f32[256]{0:T(256)S(1)}, u32[]{:S(2)}, u32[]{:S(2)}) collective-permute-start(f32[256]{0:T(256)S(1)} %get-tuple-element.112), channel_id=1, source_target_pairs={{0,1},{1,2},{2,3},{3,0},{4,5},{5,6},{6,7},{7,4},{8,9},{9,10},{10,1... | collective-permute-start | bytes 3080 | tf_op jit(solution)/shard_map/ppermute | solution.py:21
  388.4 28.9 %collective-permute-start.44 = (f32[256]{0:T(256)S(1)}, f32[256]{0:T(256)S(1)}, u32[]{:S(2)}, u32[]{:S(2)}) collective-permute-start(f32[256]{0:T(256)S(1)} %get-tuple-element.112), channel_id=1, source_target_pairs={{0,2},{1,3},{2,0},{3,1},{4,6},{5,7},{6,4},{7,5},{8,10},{9,11},{10,... | collective-permute-start | bytes 3080 | tf_op jit(solution)/shard_map/ppermute | solution.py:21
  388.5 28.9 %collective-permute-start.45 = (f32[256]{0:T(256)S(1)}, f32[256]{0:T(256)S(1)}, u32[]{:S(2)}, u32[]{:S(2)}) collective-permute-start(f32[256]{0:T(256)S(1)} %get-tuple-element.112), channel_id=1, source_target_pairs={{0,3},{1,0},{2,1},{3,2},{4,7},{5,4},{6,5},{7,6},{8,11},{9,8},{10,9... | collective-permute-start | bytes 3080 | tf_op jit(solution)/shard_map/ppermute | solution.py:21
  405.8 33.9 %collective-permute-start.41 = (bf16[256,640]{1,0:T(8,128)(2,1)S(1)}, bf16[256,640]{1,0:T(8,128)(2,1)S(1)}, u32[]{:S(2)}, u32[]{:S(2)}) collective-permute-start(bf16[256,640]{1,0:T(8,128)(2,1)S(1)} %get-tuple-element.144), channel_id=1, source_target_pairs={{0,2},{1,3},{2,0},{3,1},{4,6},{5,7},{6,4},{7,5},{8,10},{9,11},{10,... | collective-permute-start | bytes 983048 | tf_op jit(solution)/shard_map/ppermute | solution.py:21
  414.4 25.3 %collective-permute-start.42 = (bf16[256,640]{1,0:T(8,128)(2,1)S(1)}, bf16[256,640]{1,0:T(8,128)(2,1)S(1)}, u32[]{:S(2)}, u32[]{:S(2)}) collective-permute-start(bf16[256,640]{1,0:T(8,128)(2,1)S(1)} %select_select_fusion.7), channel_id=1, source_target_pairs={{0,3},{1,0},{2,1},{3,2},{4,7},{5,4},{6,5},{7,6},{8,11},{9,8},{10,9... | collective-permute-start | bytes 983048 | tf_op jit(solution)/shard_map/ppermute | solution.py:21
  417.4 39.3 %collective-permute-start.34 = (bf16[256,640]{1,0:T(8,128)(2,1)S(1)}, bf16[256,640]{1,0:T(8,128)(2,1)S(1)}, u32[]{:S(2)}, u32[]{:S(2)}) collective-permute-start(bf16[256,640]{1,0:T(8,128)(2,1)S(1)} %get-tuple-element.150), channel_id=1, source_target_pairs={{0,2},{1,3},{2,0},{3,1},{4,6},{5,7},{6,4},{7,5},{8,10},{9,11},{10,... | collective-permute-start | bytes 983048 | tf_op jit(solution)/shard_map/ppermute | solution.py:21
  418.4 38.3 %collective-permute-start.35 = (bf16[256,640]{1,0:T(8,128)(2,1)S(1)}, bf16[256,640]{1,0:T(8,128)(2,1)S(1)}, u32[]{:S(2)}, u32[]{:S(2)}) collective-permute-start(bf16[256,640]{1,0:T(8,128)(2,1)S(1)} %select_select_fusion.14), channel_id=1, source_target_pairs={{0,3},{1,0},{2,1},{3,2},{4,7},{5,4},{6,5},{7,6},{8,11},{9,8},{10,9... | collective-permute-start | bytes 983048 | tf_op jit(solution)/shard_map/ppermute | solution.py:21
  470.2 62.4 %collective-permute-start.83 = (bf16[256,2560]{1,0:T(8,128)(2,1)}, bf16[256,2560]{1,0:T(8,128)(2,1)}, u32[]{:S(2)}, u32[]{:S(2)}) collective-permute-start(bf16[256,2560]{1,0:T(8,128)(2,1)} %constant_dynamic-update-slice_fusion.40), channel_id=1, source_target_pairs={{0,16},{16,0},{1,17},{17,1},{2,18},{18,2},{3,19},{19,3},{4,20},{20... | collective-permute-start | bytes 3932168 | tf_op jit(solution)/shard_map/ppermute | solution.py:21
  514.9 25.6 %collective-permute-start.53 = (bf16[64,3200]{1,0:T(8,128)(2,1)}, bf16[64,3200]{1,0:T(8,128)(2,1)}, u32[]{:S(2)}, u32[]{:S(2)}) collective-permute-start(bf16[64,3200]{1,0:T(8,128)(2,1)} %constant_dynamic-update-slice_fusion.14), channel_id=1, source_target_pairs={{0,1},{1,2},{2,3},{3,0},{4,5},{5,6},{6,7},{7,4},{8,9},{9,10},{10,1... | collective-permute-start | bytes 1228808 | tf_op jit(solution)/shard_map/ppermute | solution.py:21
  516.9 35.6 %collective-permute-start.54 = (bf16[64,3200]{1,0:T(8,128)(2,1)}, bf16[64,3200]{1,0:T(8,128)(2,1)S(1)}, u32[]{:S(2)}, u32[]{:S(2)}) collective-permute-start(bf16[64,3200]{1,0:T(8,128)(2,1)} %constant_dynamic-update-slice_fusion.14), channel_id=1, source_target_pairs={{0,2},{1,3},{2,0},{3,1},{4,6},{5,7},{6,4},{7,5},{8,10},{9,11},{10,... | collective-permute-start | bytes 1228808 | tf_op jit(solution)/shard_map/ppermute | solution.py:21
  519.5 42.4 %collective-permute-start.55 = (bf16[64,3200]{1,0:T(8,128)(2,1)}, bf16[64,3200]{1,0:T(8,128)(2,1)}, u32[]{:S(2)}, u32[]{:S(2)}) collective-permute-start(bf16[64,3200]{1,0:T(8,128)(2,1)} %constant_dynamic-update-slice_fusion.14), channel_id=1, source_target_pairs={{0,3},{1,0},{2,1},{3,2},{4,7},{5,4},{6,5},{7,6},{8,11},{9,8},{10,9... | collective-permute-start | bytes 1228808 | tf_op jit(solution)/shard_map/ppermute | solution.py:21
  540.4 345.6 %reduce-scatter.25.cloned.1.call-start = ((), (), s32[]{:S(2)}) async-start(), calls=%async_computation.17 | async-start | bytes 2457600
  580.7 30.8 %collective-permute-start.57 = (bf16[256,640]{1,0:T(8,128)(2,1)S(1)}, bf16[256,640]{1,0:T(8,128)(2,1)S(1)}, u32[]{:S(2)}, u32[]{:S(2)}) collective-permute-start(bf16[256,640]{1,0:T(8,128)(2,1)S(1)} %get-tuple-element.90), channel_id=1, source_target_pairs={{0,2},{1,3},{2,0},{3,1},{4,6},{5,7},{6,4},{7,5},{8,10},{9,11},{10,... | collective-permute-start | bytes 983048 | tf_op jit(solution)/shard_map/ppermute | solution.py:21
  643.4 34.9 %collective-permute-start.81 = (bf16[256,2560]{1,0:T(8,128)(2,1)S(1)}, bf16[256,2560]{1,0:T(8,128)(2,1)S(1)}, u32[]{:S(2)}, u32[]{:S(2)}) collective-permute-start(bf16[256,2560]{1,0:T(8,128)(2,1)S(1)} %copy-done.54), channel_id=1, source_target_pairs={{0,16},{16,0},{1,17},{17,1},{2,18},{18,2},{3,19},{19,3},{4,20},{20... | collective-permute-start | bytes 3932168 | tf_op jit(solution)/shard_map/ppermute | solution.py:21
  678.3 59.6 %collective-permute-start.78 = (bf16[256,3072]{0,1:T(8,128)(2,1)}, bf16[256,3072]{0,1:T(8,128)(2,1)}, u32[]{:S(2)}, u32[]{:S(2)}) collective-permute-start(bf16[256,3072]{0,1:T(8,128)(2,1)} %constant_dynamic-update-slice_fusion.32), channel_id=1, source_target_pairs={{0,16},{16,0},{1,17},{17,1},{2,18},{18,2},{3,19},{19,3},{4,20},{20... | collective-permute-start | bytes 4718600 | tf_op jit(solution)/shard_map/ppermute | solution.py:21
  682.6 205.9 %reduce-scatter.19.cloned.1.call-start = ((), (), s32[]{:S(2)}) async-start(), calls=%async_computation.13 | async-start | bytes 2457600 | tf_op jit(solution)/shard_map/reduce_scatter | solution.py:350
  728.4 26.8 %collective-permute-start.73 = (bf16[64,3200]{1,0:T(8,128)(2,1)S(1)}, bf16[64,3200]{1,0:T(8,128)(2,1)}, u32[]{:S(2)}, u32[]{:S(2)}) collective-permute-start(bf16[64,3200]{1,0:T(8,128)(2,1)S(1)} %constant_dynamic-update-slice_fusion.19), channel_id=1, source_target_pairs={{0,2},{1,3},{2,0},{3,1},{4,6},{5,7},{6,4},{7,5},{8,10},{9,11},{10,... | collective-permute-start | bytes 1228808 | tf_op jit(solution)/shard_map/ppermute | solution.py:21
  731.1 29.3 %collective-permute-start.74 = (bf16[64,3200]{1,0:T(8,128)(2,1)S(1)}, bf16[64,3200]{1,0:T(8,128)(2,1)S(1)}, u32[]{:S(2)}, u32[]{:S(2)}) collective-permute-start(bf16[64,3200]{1,0:T(8,128)(2,1)S(1)} %constant_dynamic-update-slice_fusion.19), channel_id=1, source_target_pairs={{0,3},{1,0},{2,1},{3,2},{4,7},{5,4},{6,5},{7,6},{8,11},{9,8},{10,9... | collective-permute-start | bytes 1228808 | tf_op jit(solution)/shard_map/ppermute | solution.py:21
  742.3 146.2 %reduce-scatter.17.cloned.1.call-start = ((), (), s32[]{:S(2)}) async-start(), calls=%async_computation.12 | async-start | bytes 2457600 | tf_op jit(solution)/shard_map/reduce_scatter | solution.py:350
  777.4 113.0 %reduce-scatter.31.cloned.1.call-start = ((), (), s32[]{:S(2)}) async-start(), calls=%async_computation.20 | async-start | bytes 6553600
  801.6 147.4 %reduce-scatter.29.cloned.1.call-start = ((), (), s32[]{:S(2)}) async-start(), calls=%async_computation.19 | async-start | bytes 6553600
  825.6 224.5 %reduce-scatter.23.cloned.1.call-start = ((), (), s32[]{:S(2)}) async-start(), calls=%async_computation.15 | async-start | bytes 12288000 | tf_op jit(solution)/shard_map/reduce_scatter | solution.py:350
  838.8 312.6 %reduce-scatter.21.cloned.1.call-start = ((), (), s32[]{:S(2)}) async-start(), calls=%async_computation.14 | async-start | bytes 12288000 | tf_op jit(solution)/shard_map/reduce_scatter | solution.py:350
  855.3 28.2 %collective-permute-start.75 = (f32[256,640]{1,0:T(8,128)S(1)}, f32[256,640]{1,0:T(8,128)S(1)}, u32[]{:S(2)}, u32[]{:S(2)}) collective-permute-start(f32[256,640]{1,0:T(8,128)S(1)} %get-tuple-element.127), channel_id=1, source_target_pairs={{0,16},{16,0},{1,17},{17,1},{2,18},{18,2},{3,19},{19,3},{4,20},{20... | collective-permute-start | bytes 1966088 | tf_op jit(solution)/shard_map/ppermute | solution.py:21
  888.1 268.3 %collective-permute-start.85 = (bf16[640,320]{0,1:T(8,128)(2,1)}, bf16[640,320]{0,1:T(8,128)(2,1)}, u32[]{:S(2)}, u32[]{:S(2)}) collective-permute-start(bf16[640,320]{0,1:T(8,128)(2,1)} %broadcast_select_fusion.18), channel_id=1, source_target_pairs={{0,16},{16,0},{1,17},{17,1},{2,18},{18,2},{3,19},{19,3},{4,20},{20... | collective-permute-start | bytes 1228808 | tf_op jit(solution)/shard_map/ppermute | solution.py:21
  890.3 271.2 %collective-permute-start.80 = (bf16[768,320]{0,1:T(8,128)(2,1)}, bf16[768,320]{0,1:T(8,128)(2,1)}, u32[]{:S(2)}, u32[]{:S(2)}) collective-permute-start(bf16[768,320]{0,1:T(8,128)(2,1)} %broadcast_select_fusion.16), channel_id=1, source_target_pairs={{0,16},{16,0},{1,17},{17,1},{2,18},{18,2},{3,19},{19,3},{4,20},{20... | collective-permute-start | bytes 1474568 | tf_op jit(solution)/shard_map/ppermute | solution.py:21
  (197 other events, 3532.5 us)
Sparse Core Ops, SparseCore 0:
  11.2 21.7 all-gather.14
  34.6 18.3 all-gather.6
  54.5 35.5 all-gather.8
  91.5 35.5 all-gather.10
  128.5 35.5 all-gather.12
  540.5 33.6 reduce-scatter.26
  682.7 32.7 reduce-scatter.24
  742.4 33.9 reduce-scatter.18
  780.1 39.4 reduce-scatter.16
  822.5 61.9 reduce-scatter.30
  887.4 61.5 reduce-scatter.28
  952.0 98.0 reduce-scatter.22
  1053.2 98.0 reduce-scatter.20

commit v2 on v1

--- a/solution.py
+++ b/solution.py
@@ -3,13 +3,13 @@
 import jax
 import jax.numpy as jnp
 from jax import lax
+from jax.experimental.layout import Layout as ArrayLayout, with_layout_constraint
 from jax.sharding import PartitionSpec as P
 
 EPS = 1e-06
 ROPE_LOG = math.log(10000.0)
 NEG_FILL = -1e30
 LANES = 128
-STREAMS = 1
 BF = jnp.bfloat16
 F32 = jnp.float32
 
@@ -21,6 +21,17 @@
     return lax.ppermute(value, axis, pairs)
 
 
+def natural(value):
+    return with_layout_constraint(value, ArrayLayout(major_to_minor=tuple(range(value.ndim))))
+
+
+def after(values, fillers):
+    if not fillers:
+        return list(values)
+    held = lax.optimization_barrier(tuple(values) + tuple(fillers))
+    return list(held[: len(values)])
+
+
 def mm(a, b):
     return jnp.dot(a, b, preferred_element_type=F32)
 
@@ -40,48 +51,41 @@
     return result
 
 
-def gather_parts(value, axis):
+def gather_cols(value, axis, fillers=()):
     count = lax.axis_size(axis)
     me = lax.axis_index(axis)
-    parts = [value] + [shift(value, axis, s) for s in range(1, count)]
-    return [pick((me - place) % count, parts) for place in range(count)]
-
-
-def gather_cols(value, axis):
-    return jnp.concatenate(gather_parts(value, axis), axis=1)
-
-
-def gather_rows(value, axis):
+    parts = [value] + after([shift(value, axis, s) for s in range(1, count)], fillers)
+    return natural(jnp.concatenate([pick((me - place) % count, parts) for place in range(count)], axis=1))
+
+
+def gather_rows(value, axis, fillers=()):
     count = lax.axis_size(axis)
     me = lax.axis_index(axis)
     rows = value.shape[0]
     full = jnp.zeros((count * rows, value.shape[1]), value.dtype)
+    parts = [value] + after([shift(value, axis, s) for s in range(1, count)], fillers)
     for s in range(count):
-        part = value if s == 0 else shift(value, axis, s)
-        full = lax.dynamic_update_slice_in_dim(full, part, (me - s) % count * rows, 0)
-    return full
-
-
-def reduce_rows(value, axis):
+        full = lax.dynamic_update_slice_in_dim(full, parts[s], (me - s) % count * rows, 0)
+    return natural(full)
+
+
+def reduce_rows(value, axis, fillers=()):
     count = lax.axis_size(axis)
     me = lax.axis_index(axis)
     rows = value.shape[0] // count
-    total = lax.dynamic_slice_in_dim(value, me * rows, rows, 0).astype(F32)
-    for s in range(1, count):
-        block = lax.dynamic_slice_in_dim(value, (me + s) % count * rows, rows, 0)
-        total = total + shift(block, axis, s).astype(F32)
-    return total
-
-
-def reduce_cols(value, axis):
+    blocks = [lax.dynamic_slice_in_dim(value, (me + s) % count * rows, rows, 0) for s in range(count)]
+    received = after([shift(blocks[s], axis, s) for s in range(1, count)], fillers)
+    return sum((part.astype(F32) for part in received), blocks[0].astype(F32))
+
+
+def reduce_cols(value, axis, fillers=()):
     count = lax.axis_size(axis)
     me = lax.axis_index(axis)
     width = value.shape[1] // count
     blocks = [value[:, p * width : (p + 1) * width] for p in range(count)]
-    total = pick(me, blocks).astype(F32)
-    for s in range(1, count):
-        total = total + shift(pick((me + s) % count, blocks), axis, s).astype(F32)
-    return total
+    chosen = [pick((me + s) % count, blocks) for s in range(count)]
+    received = after([shift(chosen[s], axis, s) for s in range(1, count)], fillers)
+    return sum((part.astype(F32) for part in received), chosen[0].astype(F32))
 
 
 def sum_small(value, axis):
@@ -167,7 +171,7 @@
         return total
 
 
-def layer_forward(source, layout, params):
+def layer_forward(source, layout, params, early=None):
     gain_first, gain_second, w_proj, w_out, w_gate, w_up, w_down = params
     query_width = w_out.shape[0]
     head_size = (w_proj.shape[1] - query_width) // 2
@@ -203,7 +207,11 @@
     attended = mm(probs_low, all_values).astype(BF).reshape(rows, query_width)
     attended_full = gather_rows(attended, "wt")
     middle = source + mm(attended_full, w_out)
-    middle_full = gather_cols(middle.astype(BF), "wt").astype(F32)
+    middle_full = gather_cols(middle.astype(BF), "wt")
+    if early is not None:
+        middle_full, early = lax.optimization_barrier((middle_full, early))
+        early = gather_cols(early, "wt")
+    middle_full = middle_full.astype(F32)
     inv_second = lax.rsqrt(jnp.sum(middle_full * middle_full, axis=1) / width_all + EPS)
     normed_second = (middle_full * inv_second[:, None] * gain_second).astype(BF)
     gate_pre = mm(normed_second, w_gate)
@@ -228,10 +236,10 @@
         cosine,
         sine,
     )
-    return middle + update, saved
-
-
-def layer_backward(grad_out, layout, saved, params):
+    return middle + update, saved, early
+
+
+def layer_backward(grad_out, grad_full, layout, saved, params, pending, merge):
     gain_first, gain_second, w_proj, w_out, w_gate, w_up, w_down = params
     (
         source,
@@ -251,6 +259,8 @@
         cosine,
         sine,
     ) = saved
+    section_id = lax.axis_index("section")
+    n_ctx = layout.n_ctx
     query_width = w_out.shape[0]
     proj_width = w_proj.shape[1]
     head_size = (proj_width - query_width) // 2
@@ -258,22 +268,39 @@
     width_all = source.shape[1] * layout.n_wt
     rows = layout.rows
     score_scale = head_size ** (-0.5)
-    grad_full = gather_cols(grad_out.astype(BF), "wt")
+    pending_grads = pending() if pending else []
+    if grad_full is None:
+        grad_full = gather_cols(grad_out.astype(BF), "wt", pending_grads)
+    pending_kept = keep(*pending_grads) if pending_grads else None
+    down = weight_grad(
+        both_halves(section_id, *row_halves(grad_full, n_ctx)), both_sections(hidden_act)
+    )
+    if not merge:
+        down_kept = keep(down)
+        (grad_full,) = after([grad_full], [down])
     d_hidden = mm_nt(grad_full, w_down)
     activated, pull_back = jax.vjp(gelu_tanh, gate_pre)
     d_gate = pull_back(d_hidden * up_pre)[0].astype(BF)
     d_up = (d_hidden * activated).astype(BF)
     inner_part = jnp.sum(d_gate.astype(F32) * gate_pre + d_up.astype(F32) * up_pre, axis=1)
     inner = sum_small(inner_part, "wt") / (inv_second * width_all)
-    d_normed = reduce_cols((mm_nt(d_gate, w_gate) + mm_nt(d_up, w_up)).astype(BF), "wt")
+    gate_up = weight_grad(both_sections(normed_second), both_halves(section_id, d_gate, d_up))
+    feed_kept = keep(down, gate_up) if merge else (down_kept, keep(gate_up))
+    d_normed = reduce_cols(
+        (mm_nt(d_gate, w_gate) + mm_nt(d_up, w_up)).astype(BF), "wt", [down, gate_up] if merge else [gate_up]
+    )
+    gain_local = lax.dynamic_slice_in_dim(gain_second, lax.axis_index("wt") * source.shape[1], source.shape[1], 0)
     d_middle = (
         grad_out
-        + inv_second[:, None] * d_normed * gain_second_local(gain_second, source.shape[1])
+        + inv_second[:, None] * d_normed * gain_local
         - middle * (inv_second**3 * inner)[:, None]
     )
     d_gain_second = jnp.sum(d_normed * middle * inv_second[:, None], axis=0)
     d_middle_low = d_middle.astype(BF)
-    d_attended = reduce_rows(mm_nt(d_middle_low, w_out).astype(BF), "wt").astype(BF)
+    out_grad = weight_grad(
+        both_halves(section_id, *row_halves(attended_full, n_ctx)), both_sections(d_middle_low)
+    )
+    d_attended = reduce_rows(mm_nt(d_middle_low, w_out).astype(BF), "wt", [out_grad]).astype(BF)
     d_rows = d_attended.reshape(rows * head_count, head_size)
     probs_low = probs.astype(BF)
     d_values_all = mm_tn(probs_low, d_rows)
@@ -298,27 +325,19 @@
     d_source = d_middle + inv_full * d_first * gain_first - source * inner_full
     d_gain_first = jnp.sum(d_first * source * inv_full, axis=0)
     normed_first = (source * inv_full * gain_first).astype(BF)
-    terms = dict(
-        act=hidden_act,
-        grad=grad_full,
-        normed=normed_second,
-        d_gate=d_gate,
-        d_up=d_up,
-        attended=attended_full,
-        d_middle=d_middle_low,
-        first=normed_first,
-        d_projected=d_projected_full,
-    )
-    return d_source, terms, d_gain_first, d_gain_second
-
-
-def gain_second_local(gain_full, width):
-    return lax.dynamic_slice_in_dim(gain_full, lax.axis_index("wt") * width, width, 0)
+
+    def attention_grads():
+        owned = by_owner(d_projected_full, query_width, head_size, n_ctx)
+        proj_grad = weight_grad(
+            both_halves(section_id, *row_halves(owned, n_ctx)), both_sections(normed_first)
+        )
+        return [out_grad, proj_grad]
+
+    return d_source, feed_kept, attention_grads, pending_kept, d_gain_first, d_gain_second
 
 
 def both_sections(value):
-    count = lax.axis_size("section")
-    return jnp.concatenate([value] + [shift(value, "section", s) for s in range(1, count)], axis=0)
+    return jnp.concatenate([value, shift(value, "section", 1)], axis=0)
 
 
 def both_halves(section_id, low, high):
@@ -327,9 +346,13 @@
     return jnp.concatenate([own, shift(other, "section", 1)], axis=0)
 
 
-def halves(value):
-    width = value.shape[1] // 2
-    return value[:, :width], value[:, width:]
+def row_halves(value, n_ctx):
+    part = value.shape[1] // n_ctx
+    half = part // 2
+    return tuple(
+        jnp.concatenate([value[:, c * part + h * half : c * part + (h + 1) * half] for c in range(n_ctx)], axis=1)
+        for h in range(2)
+    )
 
 
 def by_owner(value, query_width, head_size, n_ctx):
@@ -343,21 +366,23 @@
     return jnp.concatenate(pieces, axis=1)
 
 
-def weight_grads(section_id, terms, query_width, head_size):
+def weight_grad(left, right):
+    return natural(mm_tn(left, right).astype(BF))
+
+
+def keep(*partials):
     n_ctx = lax.axis_size("ctx")
-
-    def keep(partial):
-        return lax.psum_scatter(partial.astype(BF), "ctx", scatter_dimension=0, tiled=True)
-
-    grad = both_sections(terms["grad"])
-    down = keep(mm_tn(grad, both_halves(section_id, *halves(terms["act"]))))
-    normed = both_sections(terms["normed"])
-    gate_up = keep(mm_tn(normed, both_halves(section_id, terms["d_gate"], terms["d_up"])))
-    attended = both_sections(terms["attended"])
-    out = keep(mm_tn(attended, both_halves(section_id, *halves(terms["d_middle"]))))
-    projected = both_sections(by_owner(terms["d_projected"], query_width, head_size, n_ctx))
-    proj = keep(mm_tn(projected, both_halves(section_id, *halves(terms["first"]))))
-    return down, gate_up, out, proj
+    heights = [partial.shape[0] // n_ctx for partial in partials]
+    width = partials[0].shape[1]
+    joined = partials[0]
+    if len(partials) > 1:
+        blocks = [partial.reshape(n_ctx, height, width) for partial, height in zip(partials, heights)]
+        joined = jnp.concatenate(blocks, axis=1).reshape(n_ctx * sum(heights), width)
+    mine = lax.psum_scatter(joined, "ctx", scatter_dimension=0, tiled=True)
+    if len(partials) == 1:
+        return mine
+    ends = [sum(heights[: k + 1]) for k in range(len(heights))]
+    return tuple(mine[end - height : end] for end, height in zip(ends, heights))
 
 
 def home(section_id, first_block, second_block):
@@ -382,8 +407,14 @@
     def fetch(weight):
         return lax.all_gather(weight, "section", axis=0, tiled=False)
 
-    w_proj = fetch(jnp.concatenate([wq[0], wk[0], wv[0]], axis=1))
-    weights = [w_proj] + [fetch(w[0]) for w in (wo, w_gate, w_up, w_down)]
+    def fetch_fast(weight):
+        received = shift(weight, "section", 1)
+        return lax.optimization_barrier(
+            (jnp.where(section_id == 0, weight, received), jnp.where(section_id == 0, received, weight))
+        )
+
+    w_proj = fetch_fast(jnp.concatenate([wq[0], wk[0], wv[0]], axis=1))
+    weights = (w_proj, fetch(wo[0]), fetch(w_gate[0]), fetch(w_up[0]), fetch_fast(w_down[0]))
     gains = jnp.concatenate([norm1_gain, norm2_gain], axis=0)
     other_gains = shift(gains, "section", 1)
     gains = jnp.concatenate(
@@ -394,33 +425,22 @@
         (gains[2 * l], gains_full[2 * l + 1]) + tuple(w[l] for w in weights) for l in range(n_section)
     ]
     first_micro = section_id * micro_own
-    micros = micro_own // STREAMS
-    hidden = lax.dynamic_slice_in_dim(hidden_in, first_micro, micro_own, 0)
-    cotangent = lax.dynamic_slice_in_dim(out_grad, first_micro, micro_own, 0)
-    layouts = [Layout(block_pos, first_micro + k * micros, micros, row_count) for k in range(STREAMS)]
-
-    def rows_of(value, k):
-        return value[k * micros : (k + 1) * micros].reshape(micros * row_count, width).astype(F32)
-
-    states = [rows_of(hidden, k) for k in range(STREAMS)]
-    saved = []
-    for l in range(n_section):
-        results = [layer_forward(states[k], layouts[k], params[l]) for k in range(STREAMS)]
-        states = [result[0] for result in results]
-        saved.append([result[1] for result in results])
-    out_own = jnp.concatenate([state.astype(BF) for state in states], axis=0)
-    grads = [rows_of(cotangent, k) for k in range(STREAMS)]
-    blocks = {}
-    gain_grads = {}
-    for l in reversed(range(n_section)):
-        results = [layer_backward(grads[k], layouts[k], saved[l][k], params[l]) for k in range(STREAMS)]
-        grads = [result[0] for result in results]
-        terms = {
-            name: jnp.concatenate([result[1][name] for result in results], axis=0) for name in results[0][1]
-        }
-        blocks[l] = weight_grads(section_id, terms, query_width, head_size)
-        gain_grads[l] = jnp.stack([sum(r[2] for r in results), sum(r[3] for r in results)])
-    in_grad_own = jnp.concatenate(grads, axis=0)
+    layout = Layout(block_pos, first_micro, micro_own, row_count)
+
+    def own_rows(value):
+        return lax.dynamic_slice_in_dim(value, first_micro, micro_own, 0).reshape(micro_own * row_count, width)
+
+    cotangent = own_rows(out_grad)
+    state, saved_0, grad_full = layer_forward(own_rows(hidden_in).astype(F32), layout, params[0], cotangent)
+    state, saved_1, _ = layer_forward(state, layout, params[1])
+    out_own = state.astype(BF)
+    grad, feed_1, pending, _, d_first_1, d_second_1 = layer_backward(
+        cotangent.astype(F32), grad_full, layout, saved_1, params[1], None, False
+    )
+    in_grad_own, feed_0, pending, attention_1, d_first_0, d_second_0 = layer_backward(
+        grad, None, layout, saved_0, params[0], pending, True
+    )
+    attention_0 = keep(*pending())
 
     def everywhere(own):
         low, high = own, shift(own, "section", 1)
@@ -431,13 +451,16 @@
 
     out = everywhere(out_own)
     in_grad = everywhere(in_grad_own)
-    gain_sum = lax.psum(jnp.stack([gain_grads[0], gain_grads[1]]), ("section", "ctx"))
+    gain_sum = lax.psum(
+        jnp.stack([jnp.stack([d_first_0, d_second_0]), jnp.stack([d_first_1, d_second_1])]), ("section", "ctx")
+    )
     gain_mine = jnp.where(section_id == 0, gain_sum[0], gain_sum[1])
-    down, gate_up, out_w, proj = (home(section_id, a, b) for a, b in zip(blocks[0], blocks[1]))
-    grad_down = jnp.concatenate(down, axis=1).T.astype(F32)
+    down, gate_up = (home(section_id, a, b) for a, b in zip(feed_0, feed_1))
+    out_w, proj = (home(section_id, a, b) for a, b in zip(attention_0, attention_1))
+    grad_down = jnp.concatenate(down, axis=0).T.astype(F32)
     grad_gate, grad_up = (half.astype(F32) for half in gate_up)
-    grad_wo = jnp.concatenate(out_w, axis=1).astype(F32)
-    grad_proj = jnp.concatenate(proj, axis=1).T.astype(F32)
+    grad_wo = jnp.concatenate(out_w, axis=0).astype(F32)
+    grad_proj = jnp.concatenate(proj, axis=0).T.astype(F32)
     query_part = query_width // n_ctx
     head_part = head_size // n_ctx
     return (

time: 1200 us -> 1210 us (level)
  local copies, waits for them, and re-layouts: 150 us -> 60.8 us
  waiting for transfers between devices: 586 us -> 659 us
  other arithmetic: 67.4 us -> 111 us
    reduce_scatter x4 -> x5, waiting for transfers between devices: 200 us -> 306 us  [keep(): mine = lax.psum_scatter(joined, 'ctx', scatter_dimension=0, tiled=True)]
    dynamic_update_slice x16, local copies, waits for them, and re-layouts: 62.7 us -> 0.53 us  [gather_rows(): lax.dynamic_update_slice_in_dim(full, parts[s], (me - s) % count * rows, 0)]
    unnamed x17 -> x8, waiting for transfers between devices: 59 us -> 3.32 us
    unnamed x319 -> x281, local copies, waits for them, and re-layouts: 58.5 us -> 17.4 us
    ppermute x96 -> x98, waiting for transfers between devices: 315 us -> 350 us  [shift(): return lax.ppermute(value, axis, pairs)]
    concatenate x4 -> x7, other arithmetic: 5.14 us -> 22.5 us  [the longest x3 17.5 us: keep(): jnp.concatenate(blocks, axis=1).reshape(n_ctx * sum(heights), width)]
    concatenate x4 -> x8, local copies, waits for them, and re-layouts: 3.23 us -> 20.2 us  [row_halves(): jnp.concatenate([value[:, c * part + h * half:c * part + (h + 1) * half]...]
    select_n x0 -> x2, other arithmetic: none -> 16.2 us  [fetch_fast(): jnp.where(section_id == 0, received, weight)]
  transfers between devices with their start and end apart: 109 -> 106, of which waited for: 55 -> 51; matrix products, arithmetic and copies ran while one was open for 27% -> 23% of each run, Pallas kernels for 0% -> 0%
where the time goes in v2:
time: 1210 us; the launch traced here: 1200 us
  waiting for transfers between devices  659 us (54%)
  starting transfers between devices  168 us (14%)
  matrix products  156 us (13%)
  other arithmetic  111 us (9%)
  local copies, waits for them, and re-layouts  60.8 us (5%)
  blocking collectives  28.6 us (2%)
  between operations  17.4 us (1%)
    ppermute x98, waiting for transfers between devices, shift(): return lax.ppermute(value, axis, pairs)  350 us
    reduce_scatter x5, waiting for transfers between devices, keep(): mine = lax.psum_scatter(joined, 'ctx', scatter_dimension=0, tiled=True)  306 us
    ppermute x98, starting transfers between devices, shift(): return lax.ppermute(value, axis, pairs)  167 us
    dot_general x14, matrix products, mm(): return jnp.dot(a, b, preferred_element_type=F32)  55.5 us
    dot_general x14, matrix products, mm_nt(): lax.dot_general(a, b, (((1,), (1,)), ((), ())), preferred_element_type=F32)  55.5 us
    dot_general x12, matrix products, mm_tn(): lax.dot_general(a, b, (((0,), (0,)), ((), ())), preferred_element_type=F32)  44.8 us
    psum x1, blocking collectives, local(): lax.psum(jnp.stack([jnp.stack([d_first_0, d_second_0]), jnp.stack([d_firs...  28.6 us
  transfers between devices with their start and end apart: 106, of which 51 were waited for; matrix products, arithmetic and copies ran while one was open for 23% of the time, Pallas kernels for 0%

profile of v2, /device:TPU:0, one launch (start us, length us, event | category | flops | bytes accessed | tf_op | source)
XLA Modules:
  0.0 1200.5 jit_solution(1692601619024210157)
XLA Ops:
  40.8 24.2 %collective-permute-done.17 = f32[4,640]{1,0:T(4,128)S(1)} collective-permute-done((f32[4,640]{1,0:T(4,128)S(1)}, f32[4,640]{1,0:T(4,128)S(1)}, u32[]{:S(2)}, u32[]{:S(2)}) %collective-permute-start.17) | collective-permute-done | bytes 10272 | tf_op jit(solution)/shard_map/ppermute | solution.py:21
  69.6 8.7 collective-permute-start.5
  97.0 7.3 collective-permute-done.9
  104.3 12.6 %collective-permute-done.10 = bf16[64,2560]{1,0:T(8,128)(2,1)S(1)} collective-permute-done((bf16[64,2560]{1,0:T(8,128)(2,1)S(1)}, bf16[64,2560]{1,0:T(8,128)(2,1)S(1)}, u32[]{:S(2)}, u32[]{:S(2)}) %collective-permute-start.10) | collective-permute-done | bytes 327712 | tf_op jit(solution)/shard_map/ppermute | solution.py:21
  135.5 22.7 %collective-permute-done.13 = bf16[256,640]{1,0:T(8,128)(2,1)S(1)} collective-permute-done((bf16[256,640]{1,0:T(8,128)(2,1)S(1)}, bf16[256,640]{1,0:T(8,128)(2,1)S(1)}, u32[]{:S(2)}, u32[]{:S(2)}) %collective-permute-start.13) | collective-permute-done | bytes 327712 | tf_op jit(solution)/shard_map/ppermute | solution.py:21
  167.7 18.1 %collective-permute-done.40 = bf16[256,640]{1,0:T(8,128)(2,1)S(1)} collective-permute-done((bf16[256,640]{1,0:T(8,128)(2,1)S(1)}, bf16[256,640]{1,0:T(8,128)(2,1)S(1)}, u32[]{:S(2)}, u32[]{:S(2)}) %collective-permute-start.40) | collective-permute-done | bytes 327712 | tf_op jit(solution)/shard_map/ppermute | solution.py:21
  187.7 11.1 broadcast_select_fusion
  198.8 8.4 fusion.1
  207.2 9.4 multiply_convert_fusion.3
  234.6 11.3 collective-permute-done.20
  251.4 8.0 collective-permute-start.22
  265.2 7.5 collective-permute-done.22
  272.7 16.0 %collective-permute-done.23 = bf16[64,3200]{1,0:T(8,128)(2,1)S(1)} collective-permute-done((bf16[64,3200]{1,0:T(8,128)(2,1)S(1)}, bf16[64,3200]{1,0:T(8,128)(2,1)S(1)}, u32[]{:S(2)}, u32[]{:S(2)}) %collective-permute-start.23) | collective-permute-done | bytes 409632 | tf_op jit(solution)/shard_map/ppermute | solution.py:21
  291.1 9.3 collective-permute-start.25
  317.0 8.5 collective-permute-done.29
  325.5 11.9 collective-permute-done.30
  352.3 9.2 concatenate.281
  362.7 16.8 %collective-permute-done.33 = bf16[256,640]{1,0:T(8,128)(2,1)} collective-permute-done((bf16[256,640]{1,0:T(8,128)(2,1)}, bf16[256,640]{1,0:T(8,128)(2,1)}, u32[]{:S(2)}, u32[]{:S(2)}) %collective-permute-start.33) | collective-permute-done | bytes 327712 | tf_op jit(solution)/shard_map/ppermute | solution.py:21
  382.8 7.2 fusion.5
  390.0 9.2 multiply_convert_fusion.2
  411.2 9.3 broadcast_select_fusion.13
  432.0 6.8 fusion.11
  444.8 7.3 collective-permute-done.44
  455.6 10.3 convolution_convert_fusion.1
  465.9 13.8 %collective-permute-done.46 = bf16[256,640]{1,0:T(8,128)(2,1)} collective-permute-done((bf16[256,640]{1,0:T(8,128)(2,1)}, bf16[256,640]{1,0:T(8,128)(2,1)}, u32[]{:S(2)}, u32[]{:S(2)}) %collective-permute-start.46) | collective-permute-done | bytes 327712 | tf_op jit(solution)/shard_map/ppermute | solution.py:21
  479.8 21.1 %collective-permute-done.45 = bf16[256,640]{1,0:T(8,128)(2,1)} collective-permute-done((bf16[256,640]{1,0:T(8,128)(2,1)}, bf16[256,640]{1,0:T(8,128)(2,1)}, u32[]{:S(2)}, u32[]{:S(2)}) %collective-permute-start.45) | collective-permute-done | bytes 327712 | tf_op jit(solution)/shard_map/ppermute | solution.py:21
  522.8 13.0 %collective-permute-done.53 = bf16[64,2560]{1,0:T(8,128)(2,1)} collective-permute-done((bf16[64,2560]{1,0:T(8,128)(2,1)}, bf16[64,2560]{1,0:T(8,128)(2,1)}, u32[]{:S(2)}, u32[]{:S(2)}) %collective-permute-start.53) | collective-permute-done | bytes 327712 | tf_op jit(solution)/shard_map/ppermute | solution.py:21
  551.9 7.4 collective-permute-start.60
  567.3 9.6 collective-permute-done.61
  577.0 13.1 %collective-permute-done.62 = bf16[64,3200]{1,0:T(8,128)(2,1)S(1)} collective-permute-done((bf16[64,3200]{1,0:T(8,128)(2,1)S(1)}, bf16[64,3200]{1,0:T(8,128)(2,1)S(1)}, u32[]{:S(2)}, u32[]{:S(2)}) %collective-permute-start.62) | collective-permute-done | bytes 409632 | tf_op jit(solution)/shard_map/ppermute | solution.py:21
  596.7 9.2 collective-permute-start.64
  614.6 12.6 %collective-permute-done.65 = bf16[256,640]{1,0:T(8,128)(2,1)S(1)} collective-permute-done((bf16[256,640]{1,0:T(8,128)(2,1)S(1)}, bf16[256,640]{1,0:T(8,128)(2,1)S(1)}, u32[]{:S(2)}, u32[]{:S(2)}) %collective-permute-start.65) | collective-permute-done | bytes 327712 | tf_op jit(solution)/shard_map/ppermute | solution.py:21
  630.0 9.5 add_reduce_fusion
  639.5 7.5 collective-permute-start.76
  661.4 6.8 fusion.10
  683.1 9.9 convolution_convert_fusion
  693.0 11.3 collective-permute-done.70
  723.6 13.0 %collective-permute-done.80 = bf16[64,2560]{1,0:T(8,128)(2,1)} collective-permute-done((bf16[64,2560]{1,0:T(8,128)(2,1)}, bf16[64,2560]{1,0:T(8,128)(2,1)}, u32[]{:S(2)}, u32[]{:S(2)}) %collective-permute-start.80) | collective-permute-done | bytes 327712 | tf_op jit(solution)/shard_map/ppermute | solution.py:21
  753.6 10.7 collective-permute-start.87
  773.4 8.9 collective-permute-done.88
  782.3 12.1 %collective-permute-done.89 = bf16[64,3200]{1,0:T(8,128)(2,1)S(1)} collective-permute-done((bf16[64,3200]{1,0:T(8,128)(2,1)S(1)}, bf16[64,3200]{1,0:T(8,128)(2,1)S(1)}, u32[]{:S(2)}, u32[]{:S(2)}) %collective-permute-start.89) | collective-permute-done | bytes 409632 | tf_op jit(solution)/shard_map/ppermute | solution.py:21
  804.9 13.2 %pad_maximum_fusion = bf16[4,960,1920]{2,1,0:T(8,128)(2,1)} fusion(bf16[4,640,1920]{2,1,0:T(8,128)(2,1)} %bitcast.168, bf16[4,320,1920]{2,1,0:T(8,128)(2,1)} %bitcast.176), kind=kLoop, calls=%fused_computation | loop fusion | flops 29491200 | bytes 29491200 | tf_op jit(solution)/shard_map/concatenate | solution.py:380
  822.0 28.6 %psum.7 = f32[2,2,640]{2,1,0:T(2,128)S(1)} all-reduce(f32[2,2,640]{2,1,0:T(2,128)S(1)} %pad_maximum_fusion.28), channel_id=1, replica_groups=mesh['section'=2,'ctx'=4,'wt'=4] {'section','ctx'}, use_global_device_ids=true, to_apply=%region_32.33 | all-reduce | flops 2560 | bytes 20480 | tf_op jit(solution)/shard_map/psum | solution.py:454
  851.3 8.2 reduce-scatter.6.cloned.1.call-done
  862.6 98.3 %reduce-scatter.12.cloned.1.call-done = bf16[640,1920]{1,0:T(8,128)(2,1)} async-done(((bf16[2560,1920]{1,0:T(8,128)(2,1)}), bf16[640,1920]{1,0:T(8,128)(2,1)}) %reduce-scatter.12.cloned.1.call-update) | async-done | bytes 2457616 | tf_op jit(solution)/shard_map/reduce_scatter | solution.py:381
  961.0 141.4 %reduce-scatter.10.cloned.1.call-done = bf16[960,1920]{1,0:T(8,128)(2,1)} async-done(((bf16[3840,1920]{1,0:T(8,128)(2,1)}), bf16[960,1920]{1,0:T(8,128)(2,1)}) %reduce-scatter.10.cloned.1.call-update) | async-done | bytes 3686416 | tf_op jit(solution)/shard_map/reduce_scatter | solution.py:381
  1106.5 58.1 %reduce-scatter.14.cloned.1.call-done = bf16[320,1920]{1,0:T(8,128)(2,1)} async-done(((bf16[1280,1920]{1,0:T(8,128)(2,1)}), bf16[320,1920]{1,0:T(8,128)(2,1)}) %reduce-scatter.14.cloned.1.call-update) | async-done | bytes 1228816 | tf_op jit(solution)/shard_map/reduce_scatter | solution.py:381
  1186.2 7.0 bitcast_convert_fusion
  (729 shorter events, 367.7 us)
Async XLA Ops:
  7.2 109.9 %all-gather.4.cloned.1.call-start = ((), (), s32[]{:S(2)}) async-start(), calls=%async_computation.5 | async-start | bytes 9830400 | tf_op jit(solution)/shard_map/all_gather | solution.py:408
  7.9 190.9 %all-gather.6.cloned.1.call-start = ((), (), s32[]{:S(2)}) async-start(), calls=%async_computation.6 | async-start | bytes 29491200 | tf_op jit(solution)/shard_map/all_gather | solution.py:408
  8.7 198.5 %all-gather.8.cloned.1.call-start = ((), (), s32[]{:S(2)}) async-start(), calls=%async_computation.7 | async-start | bytes 29491200 | tf_op jit(solution)/shard_map/all_gather | solution.py:408
  9.4 841.9 %reduce-scatter.8.cloned.1.call-start = ((), (), s32[]{:S(2)}) async-start(), calls=%async_computation.9 | async-start | bytes 4505600 | tf_op jit(solution)/shard_map/reduce_scatter | solution.py:381
  14.0 173.6 %collective-permute-start.18 = (bf16[1920,2560]{1,0:T(8,128)(2,1)}, bf16[1920,2560]{1,0:T(8,128)(2,1)}, u32[]{:S(2)}, u32[]{:S(2)}) collective-permute-start(bf16[1920,2560]{1,0:T(8,128)(2,1)} %bitcast.169), channel_id=1, source_target_pairs={{0,16},{16,0},{1,17},{17,1},{2,18},{18,2},{3,19},{19,3},{4,20},{20... | collective-permute-start | bytes 29491208 | tf_op jit(solution)/shard_map/ppermute | solution.py:21
  33.8 31.8 %collective-permute-start.2 = (bf16[64,3200]{1,0:T(8,128)(2,1)}, bf16[64,3200]{1,0:T(8,128)(2,1)S(1)}, u32[]{:S(2)}, u32[]{:S(2)}) collective-permute-start(bf16[64,3200]{1,0:T(8,128)(2,1)} %get-tuple-element.224), channel_id=1, source_target_pairs={{0,1},{1,2},{2,3},{3,0},{4,5},{5,6},{6,7},{7,4},{8,9},{9,10},{10,1... | collective-permute-start | bytes 1228808 | tf_op jit(solution)/shard_map/ppermute | solution.py:21
  35.0 30.7 %collective-permute-start.3 = (bf16[64,3200]{1,0:T(8,128)(2,1)}, bf16[64,3200]{1,0:T(8,128)(2,1)}, u32[]{:S(2)}, u32[]{:S(2)}) collective-permute-start(bf16[64,3200]{1,0:T(8,128)(2,1)} %get-tuple-element.225), channel_id=1, source_target_pairs={{0,2},{1,3},{2,0},{3,1},{4,6},{5,7},{6,4},{7,5},{8,10},{9,11},{10,... | collective-permute-start | bytes 1228808 | tf_op jit(solution)/shard_map/ppermute | solution.py:21
  36.8 28.9 %collective-permute-start.4 = (bf16[64,3200]{1,0:T(8,128)(2,1)S(1)}, bf16[64,3200]{1,0:T(8,128)(2,1)}, u32[]{:S(2)}, u32[]{:S(2)}) collective-permute-start(bf16[64,3200]{1,0:T(8,128)(2,1)S(1)} %get-tuple-element.226), channel_id=1, source_target_pairs={{0,3},{1,0},{2,1},{3,2},{4,7},{5,4},{6,5},{7,6},{8,11},{9,8},{10,9... | collective-permute-start | bytes 1228808 | tf_op jit(solution)/shard_map/ppermute | solution.py:21
  40.2 24.9 %collective-permute-start.17 = (f32[4,640]{1,0:T(4,128)S(1)}, f32[4,640]{1,0:T(4,128)S(1)}, u32[]{:S(2)}, u32[]{:S(2)}) collective-permute-start(f32[4,640]{1,0:T(4,128)S(1)} %pad_maximum_fusion.27), channel_id=1, source_target_pairs={{0,1},{1,2},{2,3},{3,0},{4,5},{5,6},{6,7},{7,4},{8,9},{9,10},{10,1... | collective-permute-start | bytes 30728 | tf_op jit(solution)/shard_map/ppermute | solution.py:21
  93.3 23.6 %collective-permute-start.10 = (bf16[64,2560]{1,0:T(8,128)(2,1)S(1)}, bf16[64,2560]{1,0:T(8,128)(2,1)S(1)}, u32[]{:S(2)}, u32[]{:S(2)}) collective-permute-start(bf16[64,2560]{1,0:T(8,128)(2,1)S(1)} %reshape.465), channel_id=1, source_target_pairs={{0,2},{1,3},{2,0},{3,1},{4,6},{5,7},{6,4},{7,5},{8,10},{9,11},{10,... | collective-permute-start | bytes 983048 | tf_op jit(solution)/shard_map/ppermute | solution.py:21
  127.4 30.7 %collective-permute-start.13 = (bf16[256,640]{1,0:T(8,128)(2,1)S(1)}, bf16[256,640]{1,0:T(8,128)(2,1)S(1)}, u32[]{:S(2)}, u32[]{:S(2)}) collective-permute-start(bf16[256,640]{1,0:T(8,128)(2,1)S(1)} %get-tuple-element.350), channel_id=1, source_target_pairs={{0,2},{1,3},{2,0},{3,1},{4,6},{5,7},{6,4},{7,5},{8,10},{9,11},{10,... | collective-permute-start | bytes 983048 | tf_op jit(solution)/shard_map/ppermute | solution.py:21
  129.4 28.7 %collective-permute-start.14 = (bf16[256,640]{1,0:T(8,128)(2,1)S(1)}, bf16[256,640]{1,0:T(8,128)(2,1)S(1)}, u32[]{:S(2)}, u32[]{:S(2)}) collective-permute-start(bf16[256,640]{1,0:T(8,128)(2,1)S(1)} %get-tuple-element.350), channel_id=1, source_target_pairs={{0,1},{1,2},{2,3},{3,0},{4,5},{5,6},{6,7},{7,4},{8,9},{9,10},{10,1... | collective-permute-start | bytes 983048 | tf_op jit(solution)/shard_map/ppermute | solution.py:21
  158.6 27.2 %collective-permute-start.40 = (bf16[256,640]{1,0:T(8,128)(2,1)S(1)}, bf16[256,640]{1,0:T(8,128)(2,1)S(1)}, u32[]{:S(2)}, u32[]{:S(2)}) collective-permute-start(bf16[256,640]{1,0:T(8,128)(2,1)S(1)} %bitcast.178), channel_id=1, source_target_pairs={{0,2},{1,3},{2,0},{3,1},{4,6},{5,7},{6,4},{7,5},{8,10},{9,11},{10,... | collective-permute-start | bytes 983048 | tf_op jit(solution)/shard_map/ppermute | solution.py:21
  158.6 27.2 %collective-permute-start.41 = (bf16[256,640]{1,0:T(8,128)(2,1)S(1)}, bf16[256,640]{1,0:T(8,128)(2,1)S(1)}, u32[]{:S(2)}, u32[]{:S(2)}) collective-permute-start(bf16[256,640]{1,0:T(8,128)(2,1)S(1)} %bitcast.179), channel_id=1, source_target_pairs={{0,1},{1,2},{2,3},{3,0},{4,5},{5,6},{6,7},{7,4},{8,9},{9,10},{10,1... | collective-permute-start | bytes 983048 | tf_op jit(solution)/shard_map/ppermute | solution.py:21
  259.4 29.3 %collective-permute-start.23 = (bf16[64,3200]{1,0:T(8,128)(2,1)S(1)}, bf16[64,3200]{1,0:T(8,128)(2,1)S(1)}, u32[]{:S(2)}, u32[]{:S(2)}) collective-permute-start(bf16[64,3200]{1,0:T(8,128)(2,1)S(1)} %get-tuple-element.222), channel_id=1, source_target_pairs={{0,2},{1,3},{2,0},{3,1},{4,6},{5,7},{6,4},{7,5},{8,10},{9,11},{10,... | collective-permute-start | bytes 1228808 | tf_op jit(solution)/shard_map/ppermute | solution.py:21
  262.8 25.9 %collective-permute-start.24 = (bf16[64,3200]{1,0:T(8,128)(2,1)S(1)}, bf16[64,3200]{1,0:T(8,128)(2,1)S(1)}, u32[]{:S(2)}, u32[]{:S(2)}) collective-permute-start(bf16[64,3200]{1,0:T(8,128)(2,1)S(1)} %get-tuple-element.223), channel_id=1, source_target_pairs={{0,3},{1,0},{2,1},{3,2},{4,7},{5,4},{6,5},{7,6},{8,11},{9,8},{10,9... | collective-permute-start | bytes 1228808 | tf_op jit(solution)/shard_map/ppermute | solution.py:21
  264.1 140.7 %collective-permute-start.42 = (bf16[256,1280]{1,0:T(8,128)(2,1)}, bf16[256,1280]{1,0:T(8,128)(2,1)}, u32[]{:S(2)}, u32[]{:S(2)}) collective-permute-start(bf16[256,1280]{1,0:T(8,128)(2,1)} %get-tuple-element.269), channel_id=1, source_target_pairs={{0,16},{16,0},{1,17},{17,1},{2,18},{18,2},{3,19},{19,3},{4,20},{20... | collective-permute-start | bytes 1966088 | tf_op jit(solution)/shard_map/ppermute | solution.py:21
  349.0 30.5 %collective-permute-start.33 = (bf16[256,640]{1,0:T(8,128)(2,1)}, bf16[256,640]{1,0:T(8,128)(2,1)}, u32[]{:S(2)}, u32[]{:S(2)}) collective-permute-start(bf16[256,640]{1,0:T(8,128)(2,1)} %get-tuple-element.356), channel_id=1, source_target_pairs={{0,2},{1,3},{2,0},{3,1},{4,6},{5,7},{6,4},{7,5},{8,10},{9,11},{10,... | collective-permute-start | bytes 983048 | tf_op jit(solution)/shard_map/ppermute | solution.py:21
  351.0 28.5 %collective-permute-start.34 = (bf16[256,640]{1,0:T(8,128)(2,1)}, bf16[256,640]{1,0:T(8,128)(2,1)}, u32[]{:S(2)}, u32[]{:S(2)}) collective-permute-start(bf16[256,640]{1,0:T(8,128)(2,1)} %get-tuple-element.356), channel_id=1, source_target_pairs={{0,1},{1,2},{2,3},{3,0},{4,5},{5,6},{6,7},{7,4},{8,9},{9,10},{10,1... | collective-permute-start | bytes 983048 | tf_op jit(solution)/shard_map/ppermute | solution.py:21
  382.8 69.3 %collective-permute-start.47 = (bf16[256,2560]{1,0:T(8,128)(2,1)}, bf16[256,2560]{1,0:T(8,128)(2,1)}, u32[]{:S(2)}, u32[]{:S(2)}) collective-permute-start(bf16[256,2560]{1,0:T(8,128)(2,1)} %fusion.19), channel_id=1, source_target_pairs={{0,16},{16,0},{1,17},{17,1},{2,18},{18,2},{3,19},{19,3},{4,20},{20... | collective-permute-start | bytes 3932168 | tf_op jit(solution)/shard_map/ppermute | solution.py:21
  426.4 27.3 %collective-permute-start.48 = (bf16[256,1920]{1,0:T(8,128)(2,1)S(1)}, bf16[256,1920]{1,0:T(8,128)(2,1)S(1)}, u32[]{:S(2)}, u32[]{:S(2)}) collective-permute-start(bf16[256,1920]{1,0:T(8,128)(2,1)S(1)} %broadcast_select_fusion.12), channel_id=1, source_target_pairs={{0,16},{16,0},{1,17},{17,1},{2,18},{18,2},{3,19},{19,3},{4,20},{20... | collective-permute-start | bytes 2949128 | tf_op jit(solution)/shard_map/ppermute | solution.py:21
  441.0 62.2 %collective-permute-start.35 = (bf16[256,640]{1,0:T(8,128)(2,1)}, bf16[256,640]{1,0:T(8,128)(2,1)S(1)}, u32[]{:S(2)}, u32[]{:S(2)}) collective-permute-start(bf16[256,640]{1,0:T(8,128)(2,1)} %get-tuple-element.274), channel_id=1, source_target_pairs={{0,1},{1,2},{2,3},{3,0},{4,5},{5,6},{6,7},{7,4},{8,9},{9,10},{10,1... | collective-permute-start | bytes 983048 | tf_op jit(solution)/shard_map/ppermute | solution.py:21
  443.0 60.2 %collective-permute-start.36 = (bf16[256,640]{1,0:T(8,128)(2,1)}, bf16[256,640]{1,0:T(8,128)(2,1)}, u32[]{:S(2)}, u32[]{:S(2)}) collective-permute-start(bf16[256,640]{1,0:T(8,128)(2,1)} %get-tuple-element.275), channel_id=1, source_target_pairs={{0,2},{1,3},{2,0},{3,1},{4,6},{5,7},{6,4},{7,5},{8,10},{9,11},{10,... | collective-permute-start | bytes 983048 | tf_op jit(solution)/shard_map/ppermute | solution.py:21
  452.1 51.1 %collective-permute-start.37 = (bf16[256,640]{1,0:T(8,128)(2,1)}, bf16[256,640]{1,0:T(8,128)(2,1)}, u32[]{:S(2)}, u32[]{:S(2)}) collective-permute-start(bf16[256,640]{1,0:T(8,128)(2,1)} %select_select_fusion.14), channel_id=1, source_target_pairs={{0,3},{1,0},{2,1},{3,2},{4,7},{5,4},{6,5},{7,6},{8,11},{9,8},{10,9... | collective-permute-start | bytes 983048 | tf_op jit(solution)/shard_map/ppermute | solution.py:21
  452.1 27.6 %collective-permute-start.46 = (bf16[256,640]{1,0:T(8,128)(2,1)}, bf16[256,640]{1,0:T(8,128)(2,1)}, u32[]{:S(2)}, u32[]{:S(2)}) collective-permute-start(bf16[256,640]{1,0:T(8,128)(2,1)} %get-tuple-element.266), channel_id=1, source_target_pairs={{0,3},{1,0},{2,1},{3,2},{4,7},{5,4},{6,5},{7,6},{8,11},{9,8},{10,9... | collective-permute-start | bytes 983048 | tf_op jit(solution)/shard_map/ppermute | solution.py:21
  453.7 47.2 %collective-permute-start.45 = (bf16[256,640]{1,0:T(8,128)(2,1)}, bf16[256,640]{1,0:T(8,128)(2,1)}, u32[]{:S(2)}, u32[]{:S(2)}) collective-permute-start(bf16[256,640]{1,0:T(8,128)(2,1)} %select_select_fusion.8), channel_id=1, source_target_pairs={{0,2},{1,3},{2,0},{3,1},{4,6},{5,7},{6,4},{7,5},{8,10},{9,11},{10,... | collective-permute-start | bytes 983048 | tf_op jit(solution)/shard_map/ppermute | solution.py:21
  479.7 37.2 %collective-permute-start.55 = (bf16[256,1280]{1,0:T(8,128)(2,1)}, bf16[256,1280]{1,0:T(8,128)(2,1)}, u32[]{:S(2)}, u32[]{:S(2)}) collective-permute-start(bf16[256,1280]{1,0:T(8,128)(2,1)} %get-tuple-element.254), channel_id=1, source_target_pairs={{0,16},{16,0},{1,17},{17,1},{2,18},{18,2},{3,19},{19,3},{4,20},{20... | collective-permute-start | bytes 1966088 | tf_op jit(solution)/shard_map/ppermute | solution.py:21
  509.9 25.9 %collective-permute-start.53 = (bf16[64,2560]{1,0:T(8,128)(2,1)}, bf16[64,2560]{1,0:T(8,128)(2,1)}, u32[]{:S(2)}, u32[]{:S(2)}) collective-permute-start(bf16[64,2560]{1,0:T(8,128)(2,1)} %get-tuple-element.264), channel_id=1, source_target_pairs={{0,2},{1,3},{2,0},{3,1},{4,6},{5,7},{6,4},{7,5},{8,10},{9,11},{10,... | collective-permute-start | bytes 983048 | tf_op jit(solution)/shard_map/ppermute | solution.py:21
  511.5 24.3 %collective-permute-start.54 = (bf16[64,2560]{1,0:T(8,128)(2,1)}, bf16[64,2560]{1,0:T(8,128)(2,1)}, u32[]{:S(2)}, u32[]{:S(2)}) collective-permute-start(bf16[64,2560]{1,0:T(8,128)(2,1)} %get-tuple-element.263), channel_id=1, source_target_pairs={{0,3},{1,0},{2,1},{3,2},{4,7},{5,4},{6,5},{7,6},{8,11},{9,8},{10,9... | collective-permute-start | bytes 983048 | tf_op jit(solution)/shard_map/ppermute | solution.py:21
  564.7 25.3 %collective-permute-start.62 = (bf16[64,3200]{1,0:T(8,128)(2,1)S(1)}, bf16[64,3200]{1,0:T(8,128)(2,1)S(1)}, u32[]{:S(2)}, u32[]{:S(2)}) collective-permute-start(bf16[64,3200]{1,0:T(8,128)(2,1)S(1)} %constant_dynamic-update-slice_fusion.14), channel_id=1, source_target_pairs={{0,2},{1,3},{2,0},{3,1},{4,6},{5,7},{6,4},{7,5},{8,10},{9,11},{10,... | collective-permute-start | bytes 1228808 | tf_op jit(solution)/shard_map/ppermute | solution.py:21
  564.7 25.4 %collective-permute-start.63 = (bf16[64,3200]{1,0:T(8,128)(2,1)S(1)}, bf16[64,3200]{1,0:T(8,128)(2,1)S(1)}, u32[]{:S(2)}, u32[]{:S(2)}) collective-permute-start(bf16[64,3200]{1,0:T(8,128)(2,1)S(1)} %constant_dynamic-update-slice_fusion.14), channel_id=1, source_target_pairs={{0,3},{1,0},{2,1},{3,2},{4,7},{5,4},{6,5},{7,6},{8,11},{9,8},{10,9... | collective-permute-start | bytes 1228808 | tf_op jit(solution)/shard_map/ppermute | solution.py:21
  609.9 73.1 %collective-permute-start.74 = (bf16[256,2560]{1,0:T(8,128)(2,1)}, bf16[256,2560]{1,0:T(8,128)(2,1)}, u32[]{:S(2)}, u32[]{:S(2)}) collective-permute-start(bf16[256,2560]{1,0:T(8,128)(2,1)} %fusion.16), channel_id=1, source_target_pairs={{0,16},{16,0},{1,17},{17,1},{2,18},{18,2},{3,19},{19,3},{4,20},{20... | collective-permute-start | bytes 3932168 | tf_op jit(solution)/shard_map/ppermute | solution.py:21
  610.0 62.7 %collective-permute-start.73 = (bf16[256,1920]{1,0:T(8,128)(2,1)}, bf16[256,1920]{1,0:T(8,128)(2,1)}, u32[]{:S(2)}, u32[]{:S(2)}) collective-permute-start(bf16[256,1920]{1,0:T(8,128)(2,1)} %get-tuple-element.352), channel_id=1, source_target_pairs={{0,16},{16,0},{1,17},{17,1},{2,18},{18,2},{3,19},{19,3},{4,20},{20... | collective-permute-start | bytes 2949128 | tf_op jit(solution)/shard_map/ppermute | solution.py:21
  639.5 28.8 %collective-permute-start.76 = (f32[256]{0:T(256)S(1)}, f32[256]{0:T(256)S(1)}, u32[]{:S(2)}, u32[]{:S(2)}) collective-permute-start(f32[256]{0:T(256)S(1)} %get-tuple-element.145), channel_id=1, source_target_pairs={{0,1},{1,2},{2,3},{3,0},{4,5},{5,6},{6,7},{7,4},{8,9},{9,10},{10,1... | collective-permute-start | bytes 3080 | tf_op jit(solution)/shard_map/ppermute | solution.py:21
  652.8 30.3 %collective-permute-start.75 = (bf16[256,1920]{1,0:T(8,128)(2,1)}, bf16[256,1920]{1,0:T(8,128)(2,1)}, u32[]{:S(2)}, u32[]{:S(2)}) collective-permute-start(bf16[256,1920]{1,0:T(8,128)(2,1)} %get-tuple-element.188), channel_id=1, source_target_pairs={{0,16},{16,0},{1,17},{17,1},{2,18},{18,2},{3,19},{19,3},{4,20},{20... | collective-permute-start | bytes 2949128 | tf_op jit(solution)/shard_map/ppermute | solution.py:21
  672.7 44.2 %collective-permute-start.82 = (bf16[256,1280]{1,0:T(8,128)(2,1)S(1)}, bf16[256,1280]{1,0:T(8,128)(2,1)}, u32[]{:S(2)}, u32[]{:S(2)}) collective-permute-start(bf16[256,1280]{1,0:T(8,128)(2,1)S(1)} %copy-done.66), channel_id=1, source_target_pairs={{0,16},{16,0},{1,17},{17,1},{2,18},{18,2},{3,19},{19,3},{4,20},{20... | collective-permute-start | bytes 1966088 | tf_op jit(solution)/shard_map/ppermute | solution.py:21
  710.7 25.9 %collective-permute-start.80 = (bf16[64,2560]{1,0:T(8,128)(2,1)}, bf16[64,2560]{1,0:T(8,128)(2,1)}, u32[]{:S(2)}, u32[]{:S(2)}) collective-permute-start(bf16[64,2560]{1,0:T(8,128)(2,1)} %get-tuple-element.243), channel_id=1, source_target_pairs={{0,2},{1,3},{2,0},{3,1},{4,6},{5,7},{6,4},{7,5},{8,10},{9,11},{10,... | collective-permute-start | bytes 983048 | tf_op jit(solution)/shard_map/ppermute | solution.py:21
  713.1 23.6 %collective-permute-start.81 = (bf16[64,2560]{1,0:T(8,128)(2,1)}, bf16[64,2560]{1,0:T(8,128)(2,1)}, u32[]{:S(2)}, u32[]{:S(2)}) collective-permute-start(bf16[64,2560]{1,0:T(8,128)(2,1)} %get-tuple-element.242), channel_id=1, source_target_pairs={{0,3},{1,0},{2,1},{3,2},{4,7},{5,4},{6,5},{7,6},{8,11},{9,8},{10,9... | collective-permute-start | bytes 983048 | tf_op jit(solution)/shard_map/ppermute | solution.py:21
  716.8 142.8 %reduce-scatter.6.cloned.1.call-start = ((), (), s32[]{:S(2)}) async-start(), calls=%async_computation.8 | async-start | bytes 4505600 | tf_op jit(solution)/shard_map/reduce_scatter | solution.py:381
  770.6 23.8 %collective-permute-start.89 = (bf16[64,3200]{1,0:T(8,128)(2,1)S(1)}, bf16[64,3200]{1,0:T(8,128)(2,1)S(1)}, u32[]{:S(2)}, u32[]{:S(2)}) collective-permute-start(bf16[64,3200]{1,0:T(8,128)(2,1)S(1)} %constant_dynamic-update-slice_fusion.19), channel_id=1, source_target_pairs={{0,2},{1,3},{2,0},{3,1},{4,6},{5,7},{6,4},{7,5},{8,10},{9,11},{10,... | collective-permute-start | bytes 1228808 | tf_op jit(solution)/shard_map/ppermute | solution.py:21
  770.6 23.9 %collective-permute-start.90 = (bf16[64,3200]{1,0:T(8,128)(2,1)S(1)}, bf16[64,3200]{1,0:T(8,128)(2,1)S(1)}, u32[]{:S(2)}, u32[]{:S(2)}) collective-permute-start(bf16[64,3200]{1,0:T(8,128)(2,1)S(1)} %constant_dynamic-update-slice_fusion.19), channel_id=1, source_target_pairs={{0,3},{1,0},{2,1},{3,2},{4,7},{5,4},{6,5},{7,6},{8,11},{9,8},{10,9... | collective-permute-start | bytes 1228808 | tf_op jit(solution)/shard_map/ppermute | solution.py:21
  804.3 156.6 %reduce-scatter.12.cloned.1.call-start = ((), (), s32[]{:S(2)}) async-start(), calls=%async_computation.11 | async-start | bytes 12288000 | tf_op jit(solution)/shard_map/reduce_scatter | solution.py:381
  804.9 297.5 %reduce-scatter.10.cloned.1.call-start = ((), (), s32[]{:S(2)}) async-start(), calls=%async_computation.10 | async-start | bytes 18432000 | tf_op jit(solution)/shard_map/reduce_scatter | solution.py:381
  818.1 346.4 %reduce-scatter.14.cloned.1.call-start = ((), (), s32[]{:S(2)}) async-start(), calls=%async_computation.12 | async-start | bytes 6144000 | tf_op jit(solution)/shard_map/reduce_scatter | solution.py:381
  821.7 29.5 %collective-permute-start.91 = (f32[256,640]{1,0:T(8,128)S(1)}, f32[256,640]{1,0:T(8,128)S(1)}, u32[]{:S(2)}, u32[]{:S(2)}) collective-permute-start(f32[256,640]{1,0:T(8,128)S(1)} %get-tuple-element.228), channel_id=1, source_target_pairs={{0,16},{16,0},{1,17},{17,1},{2,18},{18,2},{3,19},{19,3},{4,20},{20... | collective-permute-start | bytes 1966088 | tf_op jit(solution)/shard_map/ppermute | solution.py:21
  860.7 307.8 %collective-permute-start.95 = (bf16[320,640]{1,0:T(8,128)(2,1)S(1)}, bf16[320,640]{1,0:T(8,128)(2,1)S(1)}, u32[]{:S(2)}, u32[]{:S(2)}) collective-permute-start(bf16[320,640]{1,0:T(8,128)(2,1)S(1)} %broadcast_select_fusion.30), channel_id=1, source_target_pairs={{0,16},{16,0},{1,17},{17,1},{2,18},{18,2},{3,19},{19,3},{4,20},{20... | collective-permute-start | bytes 1228808 | tf_op jit(solution)/shard_map/ppermute | solution.py:21
  862.1 308.6 %collective-permute-start.94 = (bf16[384,640]{1,0:T(8,128)(2,1)S(1)}, bf16[384,640]{1,0:T(8,128)(2,1)S(1)}, u32[]{:S(2)}, u32[]{:S(2)}) collective-permute-start(bf16[384,640]{1,0:T(8,128)(2,1)S(1)} %broadcast_select_fusion.28), channel_id=1, source_target_pairs={{0,16},{16,0},{1,17},{17,1},{2,18},{18,2},{3,19},{19,3},{4,20},{20... | collective-permute-start | bytes 1474568 | tf_op jit(solution)/shard_map/ppermute | solution.py:21
  1106.5 79.7 %collective-permute-start.96 = (bf16[640,1920]{1,0:T(8,128)(2,1)}, bf16[640,1920]{1,0:T(8,128)(2,1)}, u32[]{:S(2)}, u32[]{:S(2)}) collective-permute-start(bf16[640,1920]{1,0:T(8,128)(2,1)} %broadcast_select_fusion.4), channel_id=1, source_target_pairs={{0,16},{16,0},{1,17},{17,1},{2,18},{18,2},{3,19},{19,3},{4,20},{20... | collective-permute-start | bytes 7372808 | tf_op jit(solution)/shard_map/ppermute | solution.py:21
  (191 other events, 2947.6 us)
Sparse Core Ops, SparseCore 0:
  9.5 23.9 all-gather.3
  35.1 35.5 all-gather.5
  72.3 35.5 all-gather.7
  716.9 47.8 reduce-scatter.7
  804.4 55.0 reduce-scatter.5
  862.5 98.3 reduce-scatter.11
  964.0 138.2 reduce-scatter.9
  1106.0 58.5 reduce-scatter.13

commit v3 on v2

--- a/solution.py
+++ b/solution.py
@@ -53,8 +53,12 @@
 
 def gather_cols(value, axis, fillers=()):
     count = lax.axis_size(axis)
+    return join_cols([value] + after([shift(value, axis, s) for s in range(1, count)], fillers), axis)
+
+
+def join_cols(parts, axis):
     me = lax.axis_index(axis)
-    parts = [value] + after([shift(value, axis, s) for s in range(1, count)], fillers)
+    count = len(parts)
     return natural(jnp.concatenate([pick((me - place) % count, parts) for place in range(count)], axis=1))
 
 
@@ -171,7 +175,7 @@
         return total
 
 
-def layer_forward(source, layout, params, early=None):
+def layer_forward(source, layout, params, early=None, fillers=(), last=False):
     gain_first, gain_second, w_proj, w_out, w_gate, w_up, w_down = params
     query_width = w_out.shape[0]
     head_size = (w_proj.shape[1] - query_width) // 2
@@ -181,7 +185,7 @@
     square = jnp.sum(source * source, axis=1)
     scaled = (source * gain_first).astype(BF)
     partial = jnp.concatenate([mm(scaled, w_proj).astype(BF), side_columns([square])], axis=1)
-    total = reduce_rows(partial, "wt")
+    total = reduce_rows(partial, "wt", fillers)
     proj_width = query_width + 2 * head_size
     square_all = total[:, proj_width] + total[:, proj_width + 1]
     inv_first = lax.rsqrt(square_all / width_all + EPS)
@@ -210,14 +214,17 @@
     middle_full = gather_cols(middle.astype(BF), "wt")
     if early is not None:
         middle_full, early = lax.optimization_barrier((middle_full, early))
-        early = gather_cols(early, "wt")
+        early = [early] + [shift(early, "wt", s) for s in range(1, layout.n_wt)]
     middle_full = middle_full.astype(F32)
     inv_second = lax.rsqrt(jnp.sum(middle_full * middle_full, axis=1) / width_all + EPS)
     normed_second = (middle_full * inv_second[:, None] * gain_second).astype(BF)
     gate_pre = mm(normed_second, w_gate)
     up_pre = mm(normed_second, w_up)
     hidden_act = (gelu_tanh(gate_pre) * up_pre).astype(BF)
-    update = reduce_cols(mm(hidden_act, w_down).astype(BF), "wt")
+    if early is not None:
+        hidden_act, *early = lax.optimization_barrier((hidden_act, *early))
+        early = join_cols(early, "wt")
+    update = mm(hidden_act, w_down).astype(BF)
     saved = (
         source,
         inv_first,
@@ -236,10 +243,12 @@
         cosine,
         sine,
     )
-    return middle + update, saved, early
-
-
-def layer_backward(grad_out, grad_full, layout, saved, params, pending, merge):
+    if last:
+        return update, saved, early
+    return middle + reduce_cols(update, "wt"), saved, early
+
+
+def layer_backward(grad_out, grad_full, layout, saved, params, behind=None):
     gain_first, gain_second, w_proj, w_out, w_gate, w_up, w_down = params
     (
         source,
@@ -268,15 +277,17 @@
     width_all = source.shape[1] * layout.n_wt
     rows = layout.rows
     score_scale = head_size ** (-0.5)
-    pending_grads = pending() if pending else []
-    if grad_full is None:
-        grad_full = gather_cols(grad_out.astype(BF), "wt", pending_grads)
-    pending_kept = keep(*pending_grads) if pending_grads else None
+    attention_kept = None
+    if behind is not None:
+        attention_grads, sums = behind
+        attention_grads = attention_grads()
+        attention_kept = keep(*attention_grads)
+        grad_full = gather_cols(grad_out.astype(BF), "wt", attention_grads + [sums])
     down = weight_grad(
         both_halves(section_id, *row_halves(grad_full, n_ctx)), both_sections(hidden_act)
     )
-    if not merge:
-        down_kept = keep(down)
+    down_kept = keep(down)
+    if behind is None:
         (grad_full,) = after([grad_full], [down])
     d_hidden = mm_nt(grad_full, w_down)
     activated, pull_back = jax.vjp(gelu_tanh, gate_pre)
@@ -285,9 +296,9 @@
     inner_part = jnp.sum(d_gate.astype(F32) * gate_pre + d_up.astype(F32) * up_pre, axis=1)
     inner = sum_small(inner_part, "wt") / (inv_second * width_all)
     gate_up = weight_grad(both_sections(normed_second), both_halves(section_id, d_gate, d_up))
-    feed_kept = keep(down, gate_up) if merge else (down_kept, keep(gate_up))
+    gate_up_kept = keep(gate_up)
     d_normed = reduce_cols(
-        (mm_nt(d_gate, w_gate) + mm_nt(d_up, w_up)).astype(BF), "wt", [down, gate_up] if merge else [gate_up]
+        (mm_nt(d_gate, w_gate) + mm_nt(d_up, w_up)).astype(BF), "wt", [gate_up] if behind is None else [down, gate_up]
     )
     gain_local = lax.dynamic_slice_in_dim(gain_second, lax.axis_index("wt") * source.shape[1], source.shape[1], 0)
     d_middle = (
@@ -300,7 +311,8 @@
     out_grad = weight_grad(
         both_halves(section_id, *row_halves(attended_full, n_ctx)), both_sections(d_middle_low)
     )
-    d_attended = reduce_rows(mm_nt(d_middle_low, w_out).astype(BF), "wt", [out_grad]).astype(BF)
+    waits = [down_kept if behind is None else attention_kept]
+    d_attended = reduce_rows(mm_nt(d_middle_low, w_out).astype(BF), "wt", [out_grad] + waits).astype(BF)
     d_rows = d_attended.reshape(rows * head_count, head_size)
     probs_low = probs.astype(BF)
     d_values_all = mm_tn(probs_low, d_rows)
@@ -333,7 +345,7 @@
         )
         return [out_grad, proj_grad]
 
-    return d_source, feed_kept, attention_grads, pending_kept, d_gain_first, d_gain_second
+    return d_source, (down_kept, gate_up_kept), attention_grads, attention_kept, d_gain_first, d_gain_second
 
 
 def both_sections(value):
@@ -372,17 +384,11 @@
 
 def keep(*partials):
     n_ctx = lax.axis_size("ctx")
-    heights = [partial.shape[0] // n_ctx for partial in partials]
-    width = partials[0].shape[1]
     joined = partials[0]
     if len(partials) > 1:
-        blocks = [partial.reshape(n_ctx, height, width) for partial, height in zip(partials, heights)]
-        joined = jnp.concatenate(blocks, axis=1).reshape(n_ctx * sum(heights), width)
-    mine = lax.psum_scatter(joined, "ctx", scatter_dimension=0, tiled=True)
-    if len(partials) == 1:
-        return mine
-    ends = [sum(heights[: k + 1]) for k in range(len(heights))]
-    return tuple(mine[end - height : end] for end, height in zip(ends, heights))
+        blocks = [partial.reshape(n_ctx, -1, partial.shape[1]) for partial in partials]
+        joined = jnp.concatenate(blocks, axis=1).reshape(-1, joined.shape[1])
+    return lax.psum_scatter(joined, "ctx", scatter_dimension=0, tiled=True)
 
 
 def home(section_id, first_block, second_block):
@@ -431,16 +437,20 @@
         return lax.dynamic_slice_in_dim(value, first_micro, micro_own, 0).reshape(micro_own * row_count, width)
 
     cotangent = own_rows(out_grad)
-    state, saved_0, grad_full = layer_forward(own_rows(hidden_in).astype(F32), layout, params[0], cotangent)
-    state, saved_1, _ = layer_forward(state, layout, params[1])
-    out_own = state.astype(BF)
+    state, saved_0, grad_full = layer_forward(
+        own_rows(hidden_in).astype(F32), layout, params[0], cotangent, [params[0][6]]
+    )
+    update, saved_1, _ = layer_forward(state, layout, params[1], last=True)
     grad, feed_1, pending, _, d_first_1, d_second_1 = layer_backward(
-        cotangent.astype(F32), grad_full, layout, saved_1, params[1], None, False
+        cotangent.astype(F32), grad_full, layout, saved_1, params[1]
     )
     in_grad_own, feed_0, pending, attention_1, d_first_0, d_second_0 = layer_backward(
-        grad, None, layout, saved_0, params[0], pending, True
-    )
-    attention_0 = keep(*pending())
+        grad, None, layout, saved_0, params[0], (pending, feed_1[1])
+    )
+    attention_grads = pending()
+    (update,) = after([update], attention_grads)
+    out_own = (saved_1[8] + reduce_cols(update, "wt")).astype(BF)
+    attention_0 = keep(*after(attention_grads, feed_0))
 
     def everywhere(own):
         low, high = own, shift(own, "section", 1)
@@ -456,11 +466,13 @@
     )
     gain_mine = jnp.where(section_id == 0, gain_sum[0], gain_sum[1])
     down, gate_up = (home(section_id, a, b) for a, b in zip(feed_0, feed_1))
-    out_w, proj = (home(section_id, a, b) for a, b in zip(attention_0, attention_1))
     grad_down = jnp.concatenate(down, axis=0).T.astype(F32)
     grad_gate, grad_up = (half.astype(F32) for half in gate_up)
-    grad_wo = jnp.concatenate(out_w, axis=0).astype(F32)
-    grad_proj = jnp.concatenate(proj, axis=0).T.astype(F32)
+    (attention_0,) = after([attention_0], [grad_down, grad_gate, grad_up, out, in_grad, gain_mine])
+    low, high = home(section_id, attention_0, attention_1)
+    out_rows = query_width // n_ctx // 2
+    grad_wo = jnp.concatenate([low[:out_rows], high[:out_rows]], axis=0).astype(F32)
+    grad_proj = jnp.concatenate([low[out_rows:], high[out_rows:]], axis=0).T.astype(F32)
     query_part = query_width // n_ctx
     head_part = head_size // n_ctx
     return (

time: 1210 us -> 913 us (0.75)
  waiting for transfers between devices: 659 us -> 391 us
  other arithmetic: 111 us -> 79.5 us
    reduce_scatter x5 -> x6, waiting for transfers between devices: 306 us -> 0.04 us  [keep(): return lax.psum_scatter(joined, 'ctx', scatter_dimension=0, tiled=True)]
    ppermute x98 -> x97, waiting for transfers between devices: 350 us -> 389 us  [shift(): return lax.ppermute(value, axis, pairs)]
    ppermute x98 -> x97, starting transfers between devices: 167 us -> 179 us  [shift(): return lax.ppermute(value, axis, pairs)]
  transfers between devices with their start and end apart: 106 -> 106, of which waited for: 51 -> 56; matrix products, arithmetic and copies ran while one was open for 23% -> 25% of each run, Pallas kernels for 0% -> 0%
where the time goes in v3:
time: 913 us; the launch traced here: 904 us
  waiting for transfers between devices  391 us (43%)
  starting transfers between devices  180 us (20%)
  matrix products  148 us (16%)
  other arithmetic  79.5 us (9%)
  local copies, waits for them, and re-layouts  59.8 us (7%)
  blocking collectives  28.9 us (3%)
  between operations  17.3 us (2%)
    ppermute x97, waiting for transfers between devices, shift(): return lax.ppermute(value, axis, pairs)  389 us
    ppermute x97, starting transfers between devices, shift(): return lax.ppermute(value, axis, pairs)  179 us
    dot_general x14, matrix products, mm(): return jnp.dot(a, b, preferred_element_type=F32)  56 us
    dot_general x14, matrix products, mm_nt(): lax.dot_general(a, b, (((1,), (1,)), ((), ())), preferred_element_type=F32)  54.4 us
    dot_general x12, matrix products, mm_tn(): lax.dot_general(a, b, (((0,), (0,)), ((), ())), preferred_element_type=F32)  38 us
    psum x1, blocking collectives, local(): lax.psum(jnp.stack([jnp.stack([d_first_0, d_second_0]), jnp.stack([d_firs...  28.9 us
    unnamed x283, local copies, waits for them, and re-layouts  21.6 us
    select_n x2, other arithmetic, fetch_fast(): jnp.where(section_id == 0, received, weight)  18.5 us
  transfers between devices with their start and end apart: 106, of which 56 were waited for; matrix products, arithmetic and copies ran while one was open for 25% of the time, Pallas kernels for 0%

profile of v3, /device:TPU:0, one launch (start us, length us, event | category | flops | bytes accessed | tf_op | source)
XLA Modules:
  0.0 904.5 jit_solution(8864587160603254681)
XLA Ops:
  18.0 7.1 collective-permute-done
  49.5 13.3 %broadcast_select_fusion = (bf16[1920,2560]{1,0:T(8,128)(2,1)}, bf16[1920,2560]{1,0:T(8,128)(2,1)}) fusion(bf16[1920,2560]{1,0:T(8,128)(2,1)} %collective-permute-done.5, pred[]{:T(512)S(6)} %eq.224, bf16[1,1920,2560]{2,1,0:T(8,128)(2,1)S(1)} %bitcast.162), kind=kLoop, calls=%fused_computation.6 | loop fusion | flops 9830400 | bytes 39321600 | tf_op jit(solution)/shard_map/jit(_where)/select_n | solution.py:419
  62.7 12.2 %collective-permute-done.3 = bf16[64,3200]{1,0:T(8,128)(2,1)S(1)} collective-permute-done((bf16[64,3200]{1,0:T(8,128)(2,1)S(1)}, bf16[64,3200]{1,0:T(8,128)(2,1)S(1)}, u32[]{:S(2)}, u32[]{:S(2)}) %collective-permute-start.3) | collective-permute-done | bytes 409632 | tf_op jit(solution)/shard_map/ppermute | solution.py:21
  77.2 9.2 %collective-permute-start.6 = (bf16[64,512]{1,0:T(8,128)(2,1)}, bf16[64,512]{1,0:T(8,128)(2,1)S(1)}, u32[]{:S(2)}, u32[]{:S(2)}) collective-permute-start(bf16[64,512]{1,0:T(8,128)(2,1)} %get-tuple-element.348), channel_id=1, source_target_pairs={{0,1},{1,0},{2,3},{3,2},{4,5},{5,4},{6,7},{7,6},{8,9},{9,8},{10,11... | collective-permute-start | bytes 196616 | tf_op jit(solution)/shard_map/ppermute | solution.py:21
  104.2 8.4 collective-permute-done.10
  112.6 12.6 %collective-permute-done.11 = bf16[64,2560]{1,0:T(8,128)(2,1)S(1)} collective-permute-done((bf16[64,2560]{1,0:T(8,128)(2,1)S(1)}, bf16[64,2560]{1,0:T(8,128)(2,1)S(1)}, u32[]{:S(2)}, u32[]{:S(2)}) %collective-permute-start.11) | collective-permute-done | bytes 327712 | tf_op jit(solution)/shard_map/ppermute | solution.py:21
  129.1 6.6 collective-permute-start.13
  143.8 22.1 %collective-permute-done.14 = bf16[256,640]{1,0:T(8,128)(2,1)S(1)} collective-permute-done((bf16[256,640]{1,0:T(8,128)(2,1)S(1)}, bf16[256,640]{1,0:T(8,128)(2,1)S(1)}, u32[]{:S(2)}, u32[]{:S(2)}) %collective-permute-start.14) | collective-permute-done | bytes 327712 | tf_op jit(solution)/shard_map/ppermute | solution.py:21
  171.1 8.4 fusion.1
  179.5 8.8 multiply_convert_fusion.3
  190.7 7.0 convolution_convert_fusion.9
  197.8 6.9 collective-permute-start.24
  212.8 21.0 %collective-permute-done.23 = bf16[256,640]{1,0:T(8,128)(2,1)S(1)} collective-permute-done((bf16[256,640]{1,0:T(8,128)(2,1)S(1)}, bf16[256,640]{1,0:T(8,128)(2,1)S(1)}, u32[]{:S(2)}, u32[]{:S(2)}) %collective-permute-start.23) | collective-permute-done | bytes 327712 | tf_op jit(solution)/shard_map/ppermute | solution.py:21
  246.6 25.9 %collective-permute-done.26 = bf16[64,3200]{1,0:T(8,128)(2,1)S(1)} collective-permute-done((bf16[64,3200]{1,0:T(8,128)(2,1)S(1)}, bf16[64,3200]{1,0:T(8,128)(2,1)S(1)}, u32[]{:S(2)}, u32[]{:S(2)}) %collective-permute-start.26) | collective-permute-done | bytes 409632 | tf_op jit(solution)/shard_map/ppermute | solution.py:21
  293.4 7.9 collective-permute-done.32
  301.3 10.0 %collective-permute-done.33 = bf16[64,2560]{1,0:T(8,128)(2,1)S(1)} collective-permute-done((bf16[64,2560]{1,0:T(8,128)(2,1)S(1)}, bf16[64,2560]{1,0:T(8,128)(2,1)S(1)}, u32[]{:S(2)}, u32[]{:S(2)}) %collective-permute-start.33) | collective-permute-done | bytes 327712 | tf_op jit(solution)/shard_map/ppermute | solution.py:21
  315.7 8.7 collective-permute-start.35
  332.9 20.7 %collective-permute-done.36 = bf16[256,640]{1,0:T(8,128)(2,1)} collective-permute-done((bf16[256,640]{1,0:T(8,128)(2,1)}, bf16[256,640]{1,0:T(8,128)(2,1)}, u32[]{:S(2)}, u32[]{:S(2)}) %collective-permute-start.36) | collective-permute-done | bytes 327712 | tf_op jit(solution)/shard_map/ppermute | solution.py:21
  355.9 7.4 fusion.5
  380.5 9.2 %broadcast_select_fusion.13 = (bf16[256,1920]{1,0:T(8,128)(2,1)S(1)}, bf16[256,1920]{1,0:T(8,128)(2,1)S(1)}, bf16[256,1920]{1,0:T(8,128)(2,1)S(1)}) fusion(pred[]{:T(512)S(6)} %eq.224, f32[256,1920]{1,0:T(8,128)S(1)} %copy-done.48, f32[256,1920]{1,0:T(8,128)} %get-tuple-element.379, bf16[256,2560]{1,0:T(8,128)(2,1)S(1)} %pad_maximum_fusion.5, ...), kind=kOutput, calls=%fused_computation.197 | convolution fusion | flops 2528870400 | bytes 18022400 | tf_op jit(solution)/shard_map/dot_general | solution.py:40
  393.6 8.1 convolution_convert_fusion.1
  414.8 6.4 fusion.4
  421.2 7.0 fusion.11
  434.4 6.6 collective-permute-done.41
  441.0 12.4 %collective-permute-done.42 = bf16[256,640]{1,0:T(8,128)(2,1)S(1)} collective-permute-done((bf16[256,640]{1,0:T(8,128)(2,1)S(1)}, bf16[256,640]{1,0:T(8,128)(2,1)S(1)}, u32[]{:S(2)}, u32[]{:S(2)}) %collective-permute-start.42) | collective-permute-done | bytes 327712 | tf_op jit(solution)/shard_map/ppermute | solution.py:21
  456.1 7.1 collective-permute-start.49
  472.9 13.8 %collective-permute-done.50 = bf16[64,2560]{1,0:T(8,128)(2,1)S(1)} collective-permute-done((bf16[64,2560]{1,0:T(8,128)(2,1)S(1)}, bf16[64,2560]{1,0:T(8,128)(2,1)S(1)}, u32[]{:S(2)}, u32[]{:S(2)}) %collective-permute-start.50) | collective-permute-done | bytes 327712 | tf_op jit(solution)/shard_map/ppermute | solution.py:21
  506.7 12.6 %collective-permute-start.57 = (bf16[64,512]{1,0:T(8,128)(2,1)S(1)}, bf16[64,512]{1,0:T(8,128)(2,1)S(1)}, u32[]{:S(2)}, u32[]{:S(2)}) collective-permute-start(bf16[64,512]{1,0:T(8,128)(2,1)S(1)} %slice.1126), channel_id=1, source_target_pairs={{0,1},{1,0},{2,3},{3,2},{4,5},{5,4},{6,7},{7,6},{8,9},{9,8},{10,11... | collective-permute-start | bytes 196616 | tf_op jit(solution)/shard_map/ppermute | solution.py:21
  527.4 9.6 %collective-permute-done.58 = bf16[64,3200]{1,0:T(8,128)(2,1)S(1)} collective-permute-done((bf16[64,3200]{1,0:T(8,128)(2,1)S(1)}, bf16[64,3200]{1,0:T(8,128)(2,1)S(1)}, u32[]{:S(2)}, u32[]{:S(2)}) %collective-permute-start.58) | collective-permute-done | bytes 409632 | tf_op jit(solution)/shard_map/ppermute | solution.py:21
  537.0 14.3 %collective-permute-done.59 = bf16[64,3200]{1,0:T(8,128)(2,1)S(1)} collective-permute-done((bf16[64,3200]{1,0:T(8,128)(2,1)S(1)}, bf16[64,3200]{1,0:T(8,128)(2,1)S(1)}, u32[]{:S(2)}, u32[]{:S(2)}) %collective-permute-start.59) | collective-permute-done | bytes 409632 | tf_op jit(solution)/shard_map/ppermute | solution.py:21
  562.3 9.2 %collective-permute-start.61 = (bf16[256,640]{1,0:T(8,128)(2,1)S(1)}, bf16[256,640]{1,0:T(8,128)(2,1)S(1)}, u32[]{:S(2)}, u32[]{:S(2)}) collective-permute-start(bf16[256,640]{1,0:T(8,128)(2,1)S(1)} %get-tuple-element.174), channel_id=1, source_target_pairs={{0,1},{1,2},{2,3},{3,0},{4,5},{5,6},{6,7},{7,4},{8,9},{9,10},{10,1... | collective-permute-start | bytes 983048 | tf_op jit(solution)/shard_map/ppermute | solution.py:21
  580.3 13.5 %collective-permute-done.62 = bf16[256,640]{1,0:T(8,128)(2,1)S(1)} collective-permute-done((bf16[256,640]{1,0:T(8,128)(2,1)S(1)}, bf16[256,640]{1,0:T(8,128)(2,1)S(1)}, u32[]{:S(2)}, u32[]{:S(2)}) %collective-permute-start.62) | collective-permute-done | bytes 327712 | tf_op jit(solution)/shard_map/ppermute | solution.py:21
  608.8 9.4 %add_reduce_fusion = (f32[256]{0:T(256)S(1)}, bf16[256,1920]{1,0:T(8,128)(2,1)S(1)}, bf16[256,1920]{1,0:T(8,128)(2,1)S(1)}) fusion(f32[256,1920]{1,0:T(8,128)} %get-tuple-element.373, f32[256,1920]{1,0:T(8,128)} %fusion.1, bf16[1920,2560]{1,0:T(8,128)(2,1)} %get-tuple-element.46, bf16[256,640]{1,0:T(8,128)(2,1)S(1)} %get-tuple-element.264, ...), kind=kOutput, calls=%fused_computation.105 | convolution fusion | flops 2536570624 | bytes 17040384 | tf_op jit(solution)/shard_map/dot_general | solution.py:40
  622.1 8.1 convolution_convert_fusion
  634.3 9.1 %collective-permute-start.75 = (f32[256]{0:T(256)S(1)}, f32[256]{0:T(256)S(1)}, u32[]{:S(2)}, u32[]{:S(2)}) collective-permute-start(f32[256]{0:T(256)S(1)} %get-tuple-element.169), channel_id=1, source_target_pairs={{0,3},{1,0},{2,1},{3,2},{4,7},{5,4},{6,5},{7,6},{8,11},{9,8},{10,9... | collective-permute-start | bytes 3080 | tf_op jit(solution)/shard_map/ppermute | solution.py:21
  650.1 7.0 fusion.10
  663.1 6.9 collective-permute-done.66
  670.0 12.8 %collective-permute-done.67 = bf16[256,640]{1,0:T(8,128)(2,1)S(1)} collective-permute-done((bf16[256,640]{1,0:T(8,128)(2,1)S(1)}, bf16[256,640]{1,0:T(8,128)(2,1)S(1)}, u32[]{:S(2)}, u32[]{:S(2)}) %collective-permute-start.67) | collective-permute-done | bytes 327712 | tf_op jit(solution)/shard_map/ppermute | solution.py:21
  686.6 7.5 collective-permute-start.77
  703.7 13.9 %collective-permute-done.78 = bf16[64,2560]{1,0:T(8,128)(2,1)} collective-permute-done((bf16[64,2560]{1,0:T(8,128)(2,1)}, bf16[64,2560]{1,0:T(8,128)(2,1)}, u32[]{:S(2)}, u32[]{:S(2)}) %collective-permute-start.78) | collective-permute-done | bytes 327712 | tf_op jit(solution)/shard_map/ppermute | solution.py:21
  728.1 6.8 collective-permute-done.82
  737.8 7.6 collective-permute-start.83
  753.7 9.4 %collective-permute-done.84 = bf16[64,3200]{1,0:T(8,128)(2,1)S(1)} collective-permute-done((bf16[64,3200]{1,0:T(8,128)(2,1)S(1)}, bf16[64,3200]{1,0:T(8,128)(2,1)S(1)}, u32[]{:S(2)}, u32[]{:S(2)}) %collective-permute-start.84) | collective-permute-done | bytes 409632 | tf_op jit(solution)/shard_map/ppermute | solution.py:21
  763.2 15.5 %collective-permute-done.85 = bf16[64,3200]{1,0:T(8,128)(2,1)S(1)} collective-permute-done((bf16[64,3200]{1,0:T(8,128)(2,1)S(1)}, bf16[64,3200]{1,0:T(8,128)(2,1)S(1)}, u32[]{:S(2)}, u32[]{:S(2)}) %collective-permute-start.85) | collective-permute-done | bytes 409632 | tf_op jit(solution)/shard_map/ppermute | solution.py:21
  790.2 7.0 convolution_convert_fusion.8
  797.4 28.9 %psum.7 = f32[2,2,640]{2,1,0:T(2,128)S(1)} all-reduce(f32[2,2,640]{2,1,0:T(2,128)S(1)} %pad_maximum_fusion.27), channel_id=1, replica_groups=mesh['section'=2,'ctx'=4,'wt'=4] {'section','ctx'}, use_global_device_ids=true, to_apply=%region_33.34 | all-reduce | flops 2560 | bytes 20480 | tf_op jit(solution)/shard_map/psum | solution.py:464
  828.9 9.0 collective-permute-start.91
  846.1 21.7 %collective-permute-done.90 = bf16[256,640]{1,0:T(8,128)(2,1)S(1)} collective-permute-done((bf16[256,640]{1,0:T(8,128)(2,1)S(1)}, bf16[256,640]{1,0:T(8,128)(2,1)S(1)}, u32[]{:S(2)}, u32[]{:S(2)}) %collective-permute-start.90) | collective-permute-done | bytes 327712 | tf_op jit(solution)/shard_map/ppermute | solution.py:21
  (734 shorter events, 352.5 us)
Async XLA Ops:
  7.2 118.2 %all-gather.4.cloned.1.call-start = ((), (), s32[]{:S(2)}) async-start(), calls=%async_computation.6 | async-start | bytes 9830400 | tf_op jit(solution)/shard_map/all_gather | solution.py:414
  7.9 163.2 %all-gather.6.cloned.1.call-start = ((), (), s32[]{:S(2)}) async-start(), calls=%async_computation.7 | async-start | bytes 29491200 | tf_op jit(solution)/shard_map/all_gather | solution.py:414
  8.7 170.8 %all-gather.8.cloned.1.call-start = ((), (), s32[]{:S(2)}) async-start(), calls=%async_computation.8 | async-start | bytes 29491200 | tf_op jit(solution)/shard_map/all_gather | solution.py:414
  8.8 40.7 %collective-permute-start.5 = (bf16[1920,2560]{1,0:T(8,128)(2,1)}, bf16[1920,2560]{1,0:T(8,128)(2,1)}, u32[]{:S(2)}, u32[]{:S(2)}) collective-permute-start(bf16[1920,2560]{1,0:T(8,128)(2,1)} %bitcast.160), channel_id=1, source_target_pairs={{0,16},{16,0},{1,17},{17,1},{2,18},{18,2},{3,19},{19,3},{4,20},{20... | collective-permute-start | bytes 29491208 | tf_op jit(solution)/shard_map/ppermute | solution.py:21
  9.4 478.1 %reduce-scatter.7.cloned.1.call-start = ((), (), s32[]{:S(2)}) async-start(), calls=%async_computation.9 | async-start | bytes 6144000 | tf_op jit(solution)/shard_map/reduce_scatter | solution.py:391
  13.7 23.7 %collective-permute-start.1 = (bf16[640,3072]{1,0:T(8,128)(2,1)}, bf16[640,3072]{1,0:T(8,128)(2,1)}, u32[]{:S(2)}, u32[]{:S(2)}) collective-permute-start(bf16[640,3072]{1,0:T(8,128)(2,1)} %pad_maximum_fusion), channel_id=1, source_target_pairs={{0,16},{16,0},{1,17},{17,1},{2,18},{18,2},{3,19},{19,3},{4,20},{20... | collective-permute-start | bytes 11796488 | tf_op jit(solution)/shard_map/ppermute | solution.py:21
  45.3 29.7 %collective-permute-start.3 = (bf16[64,3200]{1,0:T(8,128)(2,1)S(1)}, bf16[64,3200]{1,0:T(8,128)(2,1)S(1)}, u32[]{:S(2)}, u32[]{:S(2)}) collective-permute-start(bf16[64,3200]{1,0:T(8,128)(2,1)S(1)} %get-tuple-element.248), channel_id=1, source_target_pairs={{0,2},{1,3},{2,0},{3,1},{4,6},{5,7},{6,4},{7,5},{8,10},{9,11},{10,... | collective-permute-start | bytes 1228808 | tf_op jit(solution)/shard_map/ppermute | solution.py:21
  48.1 26.9 %collective-permute-start.4 = (bf16[64,3200]{1,0:T(8,128)(2,1)S(1)}, bf16[64,3200]{1,0:T(8,128)(2,1)S(1)}, u32[]{:S(2)}, u32[]{:S(2)}) collective-permute-start(bf16[64,3200]{1,0:T(8,128)(2,1)S(1)} %get-tuple-element.246), channel_id=1, source_target_pairs={{0,3},{1,0},{2,1},{3,2},{4,7},{5,4},{6,5},{7,6},{8,11},{9,8},{10,9... | collective-permute-start | bytes 1228808 | tf_op jit(solution)/shard_map/ppermute | solution.py:21
  101.6 23.6 %collective-permute-start.11 = (bf16[64,2560]{1,0:T(8,128)(2,1)S(1)}, bf16[64,2560]{1,0:T(8,128)(2,1)S(1)}, u32[]{:S(2)}, u32[]{:S(2)}) collective-permute-start(bf16[64,2560]{1,0:T(8,128)(2,1)S(1)} %reshape.456), channel_id=1, source_target_pairs={{0,2},{1,3},{2,0},{3,1},{4,6},{5,7},{6,4},{7,5},{8,10},{9,11},{10,... | collective-permute-start | bytes 983048 | tf_op jit(solution)/shard_map/ppermute | solution.py:21
  103.1 22.2 %collective-permute-start.12 = (bf16[64,2560]{1,0:T(8,128)(2,1)S(1)}, bf16[64,2560]{1,0:T(8,128)(2,1)S(1)}, u32[]{:S(2)}, u32[]{:S(2)}) collective-permute-start(bf16[64,2560]{1,0:T(8,128)(2,1)S(1)} %reshape.456), channel_id=1, source_target_pairs={{0,3},{1,0},{2,1},{3,2},{4,7},{5,4},{6,5},{7,6},{8,11},{9,8},{10,9... | collective-permute-start | bytes 983048 | tf_op jit(solution)/shard_map/ppermute | solution.py:21
  135.6 30.3 %collective-permute-start.14 = (bf16[256,640]{1,0:T(8,128)(2,1)S(1)}, bf16[256,640]{1,0:T(8,128)(2,1)S(1)}, u32[]{:S(2)}, u32[]{:S(2)}) collective-permute-start(bf16[256,640]{1,0:T(8,128)(2,1)S(1)} %get-tuple-element.370), channel_id=1, source_target_pairs={{0,2},{1,3},{2,0},{3,1},{4,6},{5,7},{6,4},{7,5},{8,10},{9,11},{10,... | collective-permute-start | bytes 983048 | tf_op jit(solution)/shard_map/ppermute | solution.py:21
  137.6 28.3 %collective-permute-start.15 = (bf16[256,640]{1,0:T(8,128)(2,1)S(1)}, bf16[256,640]{1,0:T(8,128)(2,1)S(1)}, u32[]{:S(2)}, u32[]{:S(2)}) collective-permute-start(bf16[256,640]{1,0:T(8,128)(2,1)S(1)} %get-tuple-element.370), channel_id=1, source_target_pairs={{0,1},{1,2},{2,3},{3,0},{4,5},{5,6},{6,7},{7,4},{8,9},{9,10},{10,1... | collective-permute-start | bytes 983048 | tf_op jit(solution)/shard_map/ppermute | solution.py:21
  166.3 22.1 %collective-permute-start.19 = (bf16[256,640]{1,0:T(8,128)(2,1)S(1)}, bf16[256,640]{1,0:T(8,128)(2,1)S(1)}, u32[]{:S(2)}, u32[]{:S(2)}) collective-permute-start(bf16[256,640]{1,0:T(8,128)(2,1)S(1)} %bitcast.165), channel_id=1, source_target_pairs={{0,1},{1,2},{2,3},{3,0},{4,5},{5,6},{6,7},{7,4},{8,9},{9,10},{10,1... | collective-permute-start | bytes 983048 | tf_op jit(solution)/shard_map/ppermute | solution.py:21
  166.3 24.4 %collective-permute-start.20 = (bf16[256,640]{1,0:T(8,128)(2,1)S(1)}, bf16[256,640]{1,0:T(8,128)(2,1)S(1)}, u32[]{:S(2)}, u32[]{:S(2)}) collective-permute-start(bf16[256,640]{1,0:T(8,128)(2,1)S(1)} %bitcast.166), channel_id=1, source_target_pairs={{0,2},{1,3},{2,0},{3,1},{4,6},{5,7},{6,4},{7,5},{8,10},{9,11},{10,... | collective-permute-start | bytes 983048 | tf_op jit(solution)/shard_map/ppermute | solution.py:21
  166.4 24.3 %collective-permute-start.21 = (bf16[256,640]{1,0:T(8,128)(2,1)S(1)}, bf16[256,640]{1,0:T(8,128)(2,1)S(1)}, u32[]{:S(2)}, u32[]{:S(2)}) collective-permute-start(bf16[256,640]{1,0:T(8,128)(2,1)S(1)} %bitcast.167), channel_id=1, source_target_pairs={{0,3},{1,0},{2,1},{3,2},{4,7},{5,4},{6,5},{7,6},{8,11},{9,8},{10,9... | collective-permute-start | bytes 983048 | tf_op jit(solution)/shard_map/ppermute | solution.py:21
  204.7 29.1 %collective-permute-start.23 = (bf16[256,640]{1,0:T(8,128)(2,1)S(1)}, bf16[256,640]{1,0:T(8,128)(2,1)S(1)}, u32[]{:S(2)}, u32[]{:S(2)}) collective-permute-start(bf16[256,640]{1,0:T(8,128)(2,1)S(1)} %get-tuple-element.303), channel_id=1, source_target_pairs={{0,2},{1,3},{2,0},{3,1},{4,6},{5,7},{6,4},{7,5},{8,10},{9,11},{10,... | collective-permute-start | bytes 983048 | tf_op jit(solution)/shard_map/ppermute | solution.py:21
  206.1 27.7 %collective-permute-start.22 = (bf16[256,640]{1,0:T(8,128)(2,1)S(1)}, bf16[256,640]{1,0:T(8,128)(2,1)S(1)}, u32[]{:S(2)}, u32[]{:S(2)}) collective-permute-start(bf16[256,640]{1,0:T(8,128)(2,1)S(1)} %get-tuple-element.302), channel_id=1, source_target_pairs={{0,1},{1,2},{2,3},{3,0},{4,5},{5,6},{6,7},{7,4},{8,9},{9,10},{10,1... | collective-permute-start | bytes 983048 | tf_op jit(solution)/shard_map/ppermute | solution.py:21
  236.3 36.3 %collective-permute-start.26 = (bf16[64,3200]{1,0:T(8,128)(2,1)S(1)}, bf16[64,3200]{1,0:T(8,128)(2,1)S(1)}, u32[]{:S(2)}, u32[]{:S(2)}) collective-permute-start(bf16[64,3200]{1,0:T(8,128)(2,1)S(1)} %get-tuple-element.244), channel_id=1, source_target_pairs={{0,2},{1,3},{2,0},{3,1},{4,6},{5,7},{6,4},{7,5},{8,10},{9,11},{10,... | collective-permute-start | bytes 1228808 | tf_op jit(solution)/shard_map/ppermute | solution.py:21
  237.3 35.3 %collective-permute-start.25 = (bf16[64,3200]{1,0:T(8,128)(2,1)S(1)}, bf16[64,3200]{1,0:T(8,128)(2,1)S(1)}, u32[]{:S(2)}, u32[]{:S(2)}) collective-permute-start(bf16[64,3200]{1,0:T(8,128)(2,1)S(1)} %get-tuple-element.243), channel_id=1, source_target_pairs={{0,1},{1,2},{2,3},{3,0},{4,5},{5,6},{6,7},{7,4},{8,9},{9,10},{10,1... | collective-permute-start | bytes 1228808 | tf_op jit(solution)/shard_map/ppermute | solution.py:21
  288.8 22.4 %collective-permute-start.33 = (bf16[64,2560]{1,0:T(8,128)(2,1)S(1)}, bf16[64,2560]{1,0:T(8,128)(2,1)S(1)}, u32[]{:S(2)}, u32[]{:S(2)}) collective-permute-start(bf16[64,2560]{1,0:T(8,128)(2,1)S(1)} %reshape.459), channel_id=1, source_target_pairs={{0,2},{1,3},{2,0},{3,1},{4,6},{5,7},{6,4},{7,5},{8,10},{9,11},{10,... | collective-permute-start | bytes 983048 | tf_op jit(solution)/shard_map/ppermute | solution.py:21
  324.4 29.2 %collective-permute-start.36 = (bf16[256,640]{1,0:T(8,128)(2,1)}, bf16[256,640]{1,0:T(8,128)(2,1)}, u32[]{:S(2)}, u32[]{:S(2)}) collective-permute-start(bf16[256,640]{1,0:T(8,128)(2,1)} %get-tuple-element.376), channel_id=1, source_target_pairs={{0,2},{1,3},{2,0},{3,1},{4,6},{5,7},{6,4},{7,5},{8,10},{9,11},{10,... | collective-permute-start | bytes 983048 | tf_op jit(solution)/shard_map/ppermute | solution.py:21
  324.6 29.0 %collective-permute-start.37 = (bf16[256,640]{1,0:T(8,128)(2,1)}, bf16[256,640]{1,0:T(8,128)(2,1)}, u32[]{:S(2)}, u32[]{:S(2)}) collective-permute-start(bf16[256,640]{1,0:T(8,128)(2,1)} %get-tuple-element.376), channel_id=1, source_target_pairs={{0,1},{1,2},{2,3},{3,0},{4,5},{5,6},{6,7},{7,4},{8,9},{9,10},{10,1... | collective-permute-start | bytes 983048 | tf_op jit(solution)/shard_map/ppermute | solution.py:21
  377.8 216.0 %reduce-scatter.9.cloned.1.call-start = ((), (), s32[]{:S(2)}) async-start(), calls=%async_computation.10 | async-start | bytes 12288000 | tf_op jit(solution)/shard_map/reduce_scatter | solution.py:391
  401.7 297.1 %reduce-scatter.11.cloned.1.call-start = ((), (), s32[]{:S(2)}) async-start(), calls=%async_computation.11 | async-start | bytes 4505600 | tf_op jit(solution)/shard_map/reduce_scatter | solution.py:391
  412.2 22.1 %collective-permute-start.47 = (f32[256]{0:T(256)S(1)}, f32[256]{0:T(256)S(1)}, u32[]{:S(2)}, u32[]{:S(2)}) collective-permute-start(f32[256]{0:T(256)S(1)} %add_reduce_fusion.1), channel_id=1, source_target_pairs={{0,2},{1,3},{2,0},{3,1},{4,6},{5,7},{6,4},{7,5},{8,10},{9,11},{10,... | collective-permute-start | bytes 3080 | tf_op jit(solution)/shard_map/ppermute | solution.py:21
  429.4 24.0 %collective-permute-start.42 = (bf16[256,640]{1,0:T(8,128)(2,1)S(1)}, bf16[256,640]{1,0:T(8,128)(2,1)S(1)}, u32[]{:S(2)}, u32[]{:S(2)}) collective-permute-start(bf16[256,640]{1,0:T(8,128)(2,1)S(1)} %select_select_fusion.11), channel_id=1, source_target_pairs={{0,2},{1,3},{2,0},{3,1},{4,6},{5,7},{6,4},{7,5},{8,10},{9,11},{10,... | collective-permute-start | bytes 983048 | tf_op jit(solution)/shard_map/ppermute | solution.py:21
  431.0 22.4 %collective-permute-start.43 = (bf16[256,640]{1,0:T(8,128)(2,1)S(1)}, bf16[256,640]{1,0:T(8,128)(2,1)S(1)}, u32[]{:S(2)}, u32[]{:S(2)}) collective-permute-start(bf16[256,640]{1,0:T(8,128)(2,1)S(1)} %get-tuple-element.280), channel_id=1, source_target_pairs={{0,3},{1,0},{2,1},{3,2},{4,7},{5,4},{6,5},{7,6},{8,11},{9,8},{10,9... | collective-permute-start | bytes 983048 | tf_op jit(solution)/shard_map/ppermute | solution.py:21
  434.3 31.8 %collective-permute-start.52 = (bf16[256,1280]{1,0:T(8,128)(2,1)S(1)}, bf16[256,1280]{1,0:T(8,128)(2,1)S(1)}, u32[]{:S(2)}, u32[]{:S(2)}) collective-permute-start(bf16[256,1280]{1,0:T(8,128)(2,1)S(1)} %get-tuple-element.268), channel_id=1, source_target_pairs={{0,16},{16,0},{1,17},{17,1},{2,18},{18,2},{3,19},{19,3},{4,20},{20... | collective-permute-start | bytes 1966088 | tf_op jit(solution)/shard_map/ppermute | solution.py:21
  463.2 23.5 %collective-permute-start.50 = (bf16[64,2560]{1,0:T(8,128)(2,1)S(1)}, bf16[64,2560]{1,0:T(8,128)(2,1)S(1)}, u32[]{:S(2)}, u32[]{:S(2)}) collective-permute-start(bf16[64,2560]{1,0:T(8,128)(2,1)S(1)} %get-tuple-element.278), channel_id=1, source_target_pairs={{0,2},{1,3},{2,0},{3,1},{4,6},{5,7},{6,4},{7,5},{8,10},{9,11},{10,... | collective-permute-start | bytes 983048 | tf_op jit(solution)/shard_map/ppermute | solution.py:21
  464.8 21.9 %collective-permute-start.51 = (bf16[64,2560]{1,0:T(8,128)(2,1)S(1)}, bf16[64,2560]{1,0:T(8,128)(2,1)}, u32[]{:S(2)}, u32[]{:S(2)}) collective-permute-start(bf16[64,2560]{1,0:T(8,128)(2,1)S(1)} %get-tuple-element.277), channel_id=1, source_target_pairs={{0,3},{1,0},{2,1},{3,2},{4,7},{5,4},{6,5},{7,6},{8,11},{9,8},{10,9... | collective-permute-start | bytes 983048 | tf_op jit(solution)/shard_map/ppermute | solution.py:21
  524.8 26.5 %collective-permute-start.59 = (bf16[64,3200]{1,0:T(8,128)(2,1)S(1)}, bf16[64,3200]{1,0:T(8,128)(2,1)S(1)}, u32[]{:S(2)}, u32[]{:S(2)}) collective-permute-start(bf16[64,3200]{1,0:T(8,128)(2,1)S(1)} %constant_dynamic-update-slice_fusion.14), channel_id=1, source_target_pairs={{0,2},{1,3},{2,0},{3,1},{4,6},{5,7},{6,4},{7,5},{8,10},{9,11},{10,... | collective-permute-start | bytes 1228808 | tf_op jit(solution)/shard_map/ppermute | solution.py:21
  525.5 25.8 %collective-permute-start.60 = (bf16[64,3200]{1,0:T(8,128)(2,1)S(1)}, bf16[64,3200]{1,0:T(8,128)(2,1)S(1)}, u32[]{:S(2)}, u32[]{:S(2)}) collective-permute-start(bf16[64,3200]{1,0:T(8,128)(2,1)S(1)} %constant_dynamic-update-slice_fusion.14), channel_id=1, source_target_pairs={{0,3},{1,0},{2,1},{3,2},{4,7},{5,4},{6,5},{7,6},{8,11},{9,8},{10,9... | collective-permute-start | bytes 1228808 | tf_op jit(solution)/shard_map/ppermute | solution.py:21
  562.3 224.3 %reduce-scatter.13.cloned.1.call-start = ((), (), s32[]{:S(2)}) async-start(), calls=%async_computation.12 | async-start | bytes 6144000 | tf_op jit(solution)/shard_map/reduce_scatter | solution.py:391
  571.6 22.2 %collective-permute-start.62 = (bf16[256,640]{1,0:T(8,128)(2,1)S(1)}, bf16[256,640]{1,0:T(8,128)(2,1)S(1)}, u32[]{:S(2)}, u32[]{:S(2)}) collective-permute-start(bf16[256,640]{1,0:T(8,128)(2,1)S(1)} %get-tuple-element.174), channel_id=1, source_target_pairs={{0,2},{1,3},{2,0},{3,1},{4,6},{5,7},{6,4},{7,5},{8,10},{9,11},{10,... | collective-permute-start | bytes 983048 | tf_op jit(solution)/shard_map/ppermute | solution.py:21
  574.0 26.1 %collective-permute-start.70 = (bf16[256,1920]{1,0:T(8,128)(2,1)}, bf16[256,1920]{1,0:T(8,128)(2,1)}, u32[]{:S(2)}, u32[]{:S(2)}) collective-permute-start(bf16[256,1920]{1,0:T(8,128)(2,1)} %get-tuple-element.52), channel_id=1, source_target_pairs={{0,16},{16,0},{1,17},{17,1},{2,18},{18,2},{3,19},{19,3},{4,20},{20... | collective-permute-start | bytes 2949128 | tf_op jit(solution)/shard_map/ppermute | solution.py:21
  608.4 178.2 %reduce-scatter.15.cloned.1.call-start = ((), (), s32[]{:S(2)}) async-start(), calls=%async_computation.13 | async-start | bytes 12288000 | tf_op jit(solution)/shard_map/reduce_scatter | solution.py:391
  630.1 249.1 %reduce-scatter.17.cloned.1.call-start = ((), (), s32[]{:S(2)}) async-start(), calls=%async_computation.14 | async-start | bytes 4505600 | tf_op jit(solution)/shard_map/reduce_scatter | solution.py:391
  634.3 26.9 %collective-permute-start.75 = (f32[256]{0:T(256)S(1)}, f32[256]{0:T(256)S(1)}, u32[]{:S(2)}, u32[]{:S(2)}) collective-permute-start(f32[256]{0:T(256)S(1)} %get-tuple-element.169), channel_id=1, source_target_pairs={{0,3},{1,0},{2,1},{3,2},{4,7},{5,4},{6,5},{7,6},{8,11},{9,8},{10,9... | collective-permute-start | bytes 3080 | tf_op jit(solution)/shard_map/ppermute | solution.py:21
  660.2 22.6 %collective-permute-start.67 = (bf16[256,640]{1,0:T(8,128)(2,1)S(1)}, bf16[256,640]{1,0:T(8,128)(2,1)S(1)}, u32[]{:S(2)}, u32[]{:S(2)}) collective-permute-start(bf16[256,640]{1,0:T(8,128)(2,1)S(1)} %select_select_fusion.4), channel_id=1, source_target_pairs={{0,2},{1,3},{2,0},{3,1},{4,6},{5,7},{6,4},{7,5},{8,10},{9,11},{10,... | collective-permute-start | bytes 983048 | tf_op jit(solution)/shard_map/ppermute | solution.py:21
  663.0 33.4 %collective-permute-start.38 = (bf16[256,1280]{1,0:T(8,128)(2,1)S(1)}, bf16[256,1280]{1,0:T(8,128)(2,1)S(1)}, u32[]{:S(2)}, u32[]{:S(2)}) collective-permute-start(bf16[256,1280]{1,0:T(8,128)(2,1)S(1)} %get-tuple-element.289), channel_id=1, source_target_pairs={{0,16},{16,0},{1,17},{17,1},{2,18},{18,2},{3,19},{19,3},{4,20},{20... | collective-permute-start | bytes 1966088 | tf_op jit(solution)/shard_map/ppermute | solution.py:21
  694.0 23.6 %collective-permute-start.78 = (bf16[64,2560]{1,0:T(8,128)(2,1)}, bf16[64,2560]{1,0:T(8,128)(2,1)}, u32[]{:S(2)}, u32[]{:S(2)}) collective-permute-start(bf16[64,2560]{1,0:T(8,128)(2,1)} %get-tuple-element.257), channel_id=1, source_target_pairs={{0,2},{1,3},{2,0},{3,1},{4,6},{5,7},{6,4},{7,5},{8,10},{9,11},{10,... | collective-permute-start | bytes 983048 | tf_op jit(solution)/shard_map/ppermute | solution.py:21
  695.4 22.3 %collective-permute-start.79 = (bf16[64,2560]{1,0:T(8,128)(2,1)S(1)}, bf16[64,2560]{1,0:T(8,128)(2,1)}, u32[]{:S(2)}, u32[]{:S(2)}) collective-permute-start(bf16[64,2560]{1,0:T(8,128)(2,1)S(1)} %get-tuple-element.256), channel_id=1, source_target_pairs={{0,3},{1,0},{2,1},{3,2},{4,7},{5,4},{6,5},{7,6},{8,11},{9,8},{10,9... | collective-permute-start | bytes 983048 | tf_op jit(solution)/shard_map/ppermute | solution.py:21
  750.9 27.8 %collective-permute-start.85 = (bf16[64,3200]{1,0:T(8,128)(2,1)S(1)}, bf16[64,3200]{1,0:T(8,128)(2,1)S(1)}, u32[]{:S(2)}, u32[]{:S(2)}) collective-permute-start(bf16[64,3200]{1,0:T(8,128)(2,1)S(1)} %constant_dynamic-update-slice_fusion.19), channel_id=1, source_target_pairs={{0,2},{1,3},{2,0},{3,1},{4,6},{5,7},{6,4},{7,5},{8,10},{9,11},{10,... | collective-permute-start | bytes 1228808 | tf_op jit(solution)/shard_map/ppermute | solution.py:21
  752.4 26.3 %collective-permute-start.86 = (bf16[64,3200]{1,0:T(8,128)(2,1)S(1)}, bf16[64,3200]{1,0:T(8,128)(2,1)S(1)}, u32[]{:S(2)}, u32[]{:S(2)}) collective-permute-start(bf16[64,3200]{1,0:T(8,128)(2,1)S(1)} %constant_dynamic-update-slice_fusion.19), channel_id=1, source_target_pairs={{0,3},{1,0},{2,1},{3,2},{4,7},{5,4},{6,5},{7,6},{8,11},{9,8},{10,9... | collective-permute-start | bytes 1228808 | tf_op jit(solution)/shard_map/ppermute | solution.py:21
  797.2 71.1 %collective-permute-start.93 = (f32[256,640]{1,0:T(8,128)S(1)}, f32[256,640]{1,0:T(8,128)}, u32[]{:S(2)}, u32[]{:S(2)}) collective-permute-start(f32[256,640]{1,0:T(8,128)S(1)} %get-tuple-element.250), channel_id=1, source_target_pairs={{0,16},{16,0},{1,17},{17,1},{2,18},{18,2},{3,19},{19,3},{4,20},{20... | collective-permute-start | bytes 1966088 | tf_op jit(solution)/shard_map/ppermute | solution.py:21
  828.3 45.9 %collective-permute-start.95 = (bf16[640,1920]{1,0:T(8,128)(2,1)S(1)}, bf16[640,1920]{1,0:T(8,128)(2,1)S(1)}, u32[]{:S(2)}, u32[]{:S(2)}) collective-permute-start(bf16[640,1920]{1,0:T(8,128)(2,1)S(1)} %broadcast_select_fusion.4), channel_id=1, source_target_pairs={{0,16},{16,0},{1,17},{17,1},{2,18},{18,2},{3,19},{19,3},{4,20},{20... | collective-permute-start | bytes 7372808 | tf_op jit(solution)/shard_map/ppermute | solution.py:21
  838.1 29.8 %collective-permute-start.90 = (bf16[256,640]{1,0:T(8,128)(2,1)S(1)}, bf16[256,640]{1,0:T(8,128)(2,1)S(1)}, u32[]{:S(2)}, u32[]{:S(2)}) collective-permute-start(bf16[256,640]{1,0:T(8,128)(2,1)S(1)} %get-tuple-element.255), channel_id=1, source_target_pairs={{0,2},{1,3},{2,0},{3,1},{4,6},{5,7},{6,4},{7,5},{8,10},{9,11},{10,... | collective-permute-start | bytes 983048 | tf_op jit(solution)/shard_map/ppermute | solution.py:21
  839.4 28.5 %collective-permute-start.89 = (bf16[256,640]{1,0:T(8,128)(2,1)S(1)}, bf16[256,640]{1,0:T(8,128)(2,1)S(1)}, u32[]{:S(2)}, u32[]{:S(2)}) collective-permute-start(bf16[256,640]{1,0:T(8,128)(2,1)S(1)} %get-tuple-element.254), channel_id=1, source_target_pairs={{0,1},{1,2},{2,3},{3,0},{4,5},{5,6},{6,7},{7,4},{8,9},{9,10},{10,1... | collective-permute-start | bytes 983048 | tf_op jit(solution)/shard_map/ppermute | solution.py:21
  (192 other events, 2260.9 us)
Sparse Core Ops, SparseCore 0:
  9.5 23.9 all-gather.3
  35.1 35.5 all-gather.5
  72.3 35.5 all-gather.7
  377.9 55.9 reduce-scatter.6
  436.8 98.0 reduce-scatter.8
  562.4 52.6 reduce-scatter.10
  618.7 58.5 reduce-scatter.12
  680.5 103.7 reduce-scatter.14
  790.3 56.1 reduce-scatter.16

commit v4 on v3

--- a/solution.py
+++ b/solution.py
@@ -82,14 +82,22 @@
     return sum((part.astype(F32) for part in received), blocks[0].astype(F32))
 
 
-def reduce_cols(value, axis, fillers=()):
+def send_cols(value, axis):
     count = lax.axis_size(axis)
     me = lax.axis_index(axis)
     width = value.shape[1] // count
     blocks = [value[:, p * width : (p + 1) * width] for p in range(count)]
     chosen = [pick((me + s) % count, blocks) for s in range(count)]
-    received = after([shift(chosen[s], axis, s) for s in range(1, count)], fillers)
-    return sum((part.astype(F32) for part in received), chosen[0].astype(F32))
+    return [chosen[0]] + [shift(chosen[s], axis, s) for s in range(1, count)]
+
+
+def add_up(parts):
+    return sum((part.astype(F32) for part in parts[1:]), parts[0].astype(F32))
+
+
+def reduce_cols(value, axis, fillers=()):
+    own, *received = send_cols(value, axis)
+    return add_up([own] + after(received, fillers))
 
 
 def sum_small(value, axis):
@@ -185,6 +193,8 @@
     square = jnp.sum(source * source, axis=1)
     scaled = (source * gain_first).astype(BF)
     partial = jnp.concatenate([mm(scaled, w_proj).astype(BF), side_columns([square])], axis=1)
+    if callable(gain_second):
+        partial, gain_second = gain_second(partial)
     total = reduce_rows(partial, "wt", fillers)
     proj_width = query_width + 2 * head_size
     square_all = total[:, proj_width] + total[:, proj_width + 1]
@@ -278,11 +288,13 @@
     rows = layout.rows
     score_scale = head_size ** (-0.5)
     attention_kept = None
+    output_parts = None
     if behind is not None:
-        attention_grads, sums = behind
+        attention_grads, sums, update = behind
         attention_grads = attention_grads()
-        attention_kept = keep(*attention_grads)
+        attention_kept = keep_fast(attention_grads)
         grad_full = gather_cols(grad_out.astype(BF), "wt", attention_grads + [sums])
+        output_parts = send_cols(*after([update], [grad_full]), "wt")
     down = weight_grad(
         both_halves(section_id, *row_halves(grad_full, n_ctx)), both_sections(hidden_act)
     )
@@ -294,12 +306,16 @@
     d_gate = pull_back(d_hidden * up_pre)[0].astype(BF)
     d_up = (d_hidden * activated).astype(BF)
     inner_part = jnp.sum(d_gate.astype(F32) * gate_pre + d_up.astype(F32) * up_pre, axis=1)
+    d_normed_part = (mm_nt(d_gate, w_gate) + mm_nt(d_up, w_up)).astype(BF)
+    if output_parts is not None:
+        d_normed_part, *output_parts = lax.optimization_barrier((d_normed_part, *output_parts))
+    inner_part, normed_other = after([inner_part, shift(normed_second, "section", 1)], [d_normed_part])
     inner = sum_small(inner_part, "wt") / (inv_second * width_all)
-    gate_up = weight_grad(both_sections(normed_second), both_halves(section_id, d_gate, d_up))
+    gate_up = weight_grad(
+        jnp.concatenate([normed_second, normed_other], axis=0), both_halves(section_id, d_gate, d_up)
+    )
     gate_up_kept = keep(gate_up)
-    d_normed = reduce_cols(
-        (mm_nt(d_gate, w_gate) + mm_nt(d_up, w_up)).astype(BF), "wt", [gate_up] if behind is None else [down, gate_up]
-    )
+    d_normed = reduce_cols(d_normed_part, "wt", [gate_up] if behind is None else [down, gate_up])
     gain_local = lax.dynamic_slice_in_dim(gain_second, lax.axis_index("wt") * source.shape[1], source.shape[1], 0)
     d_middle = (
         grad_out
@@ -321,16 +337,19 @@
     d_scores = (probs * (d_probs - delta) * score_scale).astype(BF)
     d_query_rows = mm(d_scores, all_keys)
     d_keys_all = mm_tn(d_scores, query_rows)
-    d_pairs = layout.reduce_keys(jnp.concatenate([d_keys_all, d_values_all], axis=1))
     d_query = rotate(
         d_query_rows.reshape(rows, head_count, head_size), cosine[:, None], -sine[:, None]
-    ).reshape(rows, query_width)
+    ).reshape(rows, query_width).astype(BF)
+    d_query_full = gather_rows(d_query, "wt")
+    d_pairs = layout.reduce_keys(jnp.concatenate([d_keys_all, d_values_all], axis=1))
     d_key = rotate(d_pairs[:, :head_size], cosine, -sine)
-    d_projected = jnp.concatenate([d_query, d_key, d_pairs[:, head_size:]], axis=1).astype(BF)
-    inner_own = jnp.sum(d_projected.astype(F32) * projected, axis=1) * inv_first * inv_first / width_all
-    packed = gather_rows(jnp.concatenate([d_projected, side_columns([inv_first, inner_own])], axis=1), "wt")
-    d_projected_full = packed[:, :proj_width]
-    side = packed[:, proj_width : proj_width + 4].astype(F32)
+    d_pairs = jnp.concatenate([d_key, d_pairs[:, head_size:]], axis=1).astype(BF)
+    inner_own = jnp.sum(d_query.astype(F32) * projected[:, :query_width], axis=1)
+    inner_own = inner_own + jnp.sum(d_pairs.astype(F32) * projected[:, query_width:], axis=1)
+    inner_own = inner_own * inv_first * inv_first / width_all
+    packed = gather_rows(jnp.concatenate([d_pairs, side_columns([inv_first, inner_own])], axis=1), "wt")
+    d_projected_full = natural(jnp.concatenate([d_query_full, packed[:, : 2 * head_size]], axis=1))
+    side = packed[:, 2 * head_size : 2 * head_size + 4].astype(F32)
     inv_full = side[:, 0:1] + side[:, 1:2]
     inner_full = side[:, 2:3] + side[:, 3:4]
     d_first = mm_nt(d_projected_full, w_proj)
@@ -345,7 +364,8 @@
         )
         return [out_grad, proj_grad]
 
-    return d_source, (down_kept, gate_up_kept), attention_grads, attention_kept, d_gain_first, d_gain_second
+    output = None if output_parts is None else add_up(output_parts)
+    return d_source, (down_kept, gate_up_kept), attention_grads, attention_kept, d_gain_first, d_gain_second, output
 
 
 def both_sections(value):
@@ -382,13 +402,15 @@
     return natural(mm_tn(left, right).astype(BF))
 
 
-def keep(*partials):
+def keep(partial):
+    return lax.psum_scatter(partial, "ctx", scatter_dimension=0, tiled=True)
+
+
+def keep_fast(partials):
     n_ctx = lax.axis_size("ctx")
-    joined = partials[0]
-    if len(partials) > 1:
-        blocks = [partial.reshape(n_ctx, -1, partial.shape[1]) for partial in partials]
-        joined = jnp.concatenate(blocks, axis=1).reshape(-1, joined.shape[1])
-    return lax.psum_scatter(joined, "ctx", scatter_dimension=0, tiled=True)
+    blocks = [partial.reshape(n_ctx, -1, partial.shape[1]) for partial in partials]
+    joined = jnp.concatenate(blocks, axis=1)
+    return reduce_rows(joined.reshape(-1, joined.shape[2]), "ctx").astype(BF)
 
 
 def home(section_id, first_block, second_block):
@@ -419,17 +441,25 @@
             (jnp.where(section_id == 0, weight, received), jnp.where(section_id == 0, received, weight))
         )
 
-    w_proj = fetch_fast(jnp.concatenate([wq[0], wk[0], wv[0]], axis=1))
-    weights = (w_proj, fetch(wo[0]), fetch(w_gate[0]), fetch(w_up[0]), fetch_fast(w_down[0]))
     gains = jnp.concatenate([norm1_gain, norm2_gain], axis=0)
     other_gains = shift(gains, "section", 1)
-    gains = jnp.concatenate(
-        [jnp.where(section_id == 0, gains, other_gains), jnp.where(section_id == 0, other_gains, gains)], axis=0
-    )
-    gains_full = gather_cols(gains, "wt")
-    params = [
-        (gains[2 * l], gains_full[2 * l + 1]) + tuple(w[l] for w in weights) for l in range(n_section)
-    ]
+    other_proj = jnp.concatenate(
+        [shift(wq[0], "section", 1), shift(jnp.concatenate([wk[0], wv[0]], axis=1), "section", 1)], axis=1
+    )
+    own_proj = jnp.concatenate([wq[0], wk[0], wv[0]], axis=1)
+    w_proj = lax.optimization_barrier(
+        (jnp.where(section_id == 0, own_proj, other_proj), jnp.where(section_id == 0, other_proj, own_proj))
+    )
+    weights = (w_proj, fetch(wo[0]), fetch(w_gate[0]), fetch(w_up[0]), fetch_fast(after([w_down[0]], [other_proj])[0]))
+    gains = [jnp.where(section_id == 0, gains, other_gains), jnp.where(section_id == 0, other_gains, gains)]
+    second_full = []
+
+    def gather_second(partial):
+        own, partial = lax.optimization_barrier((jnp.stack([gains[0][1], gains[1][1]]), partial))
+        second_full.append(gather_cols(own, "wt"))
+        return partial, second_full[0][0]
+
+    params = [[gains[l][0], gather_second] + [w[l] for w in weights] for l in range(n_section)]
     first_micro = section_id * micro_own
     layout = Layout(block_pos, first_micro, micro_own, row_count)
 
@@ -440,17 +470,17 @@
     state, saved_0, grad_full = layer_forward(
         own_rows(hidden_in).astype(F32), layout, params[0], cotangent, [params[0][6]]
     )
+    for l in range(n_section):
+        params[l][1] = second_full[0][l]
     update, saved_1, _ = layer_forward(state, layout, params[1], last=True)
-    grad, feed_1, pending, _, d_first_1, d_second_1 = layer_backward(
+    grad, feed_1, pending, _, d_first_1, d_second_1, _ = layer_backward(
         cotangent.astype(F32), grad_full, layout, saved_1, params[1]
     )
-    in_grad_own, feed_0, pending, attention_1, d_first_0, d_second_0 = layer_backward(
-        grad, None, layout, saved_0, params[0], (pending, feed_1[1])
-    )
-    attention_grads = pending()
-    (update,) = after([update], attention_grads)
-    out_own = (saved_1[8] + reduce_cols(update, "wt")).astype(BF)
-    attention_0 = keep(*after(attention_grads, feed_0))
+    in_grad_own, feed_0, pending, attention_1, d_first_0, d_second_0, update = layer_backward(
+        grad, None, layout, saved_0, params[0], (pending, feed_1[1], update)
+    )
+    out_own = (saved_1[8] + update).astype(BF)
+    attention_0 = keep_fast(pending())
 
     def everywhere(own):
         low, high = own, shift(own, "section", 1)

time: 913 us -> 997 us (1.092)
  waiting for transfers between devices: 391 us -> 435 us
  starting transfers between devices: 180 us -> 206 us
  matrix products: 148 us -> 158 us
    ppermute x97 -> x110, waiting for transfers between devices: 389 us -> 434 us  [shift(): return lax.ppermute(value, axis, pairs)]
    ppermute x97 -> x110, starting transfers between devices: 179 us -> 205 us  [shift(): return lax.ppermute(value, axis, pairs)]
    unnamed x283 -> x220, local copies, waits for them, and re-layouts: 21.6 us -> 25.3 us
  transfers between devices with their start and end apart: 106 -> 117, of which waited for: 56 -> 49; matrix products, arithmetic and copies ran while one was open for 25% -> 24% of each run, Pallas kernels for 0% -> 0%
where the time goes in v4:
time: 997 us; the launch traced here: 988 us
  waiting for transfers between devices  435 us (44%)
  starting transfers between devices  206 us (21%)
  matrix products  158 us (16%)
  other arithmetic  76.9 us (8%)
  local copies, waits for them, and re-layouts  68.1 us (7%)
  blocking collectives  26.6 us (3%)
  between operations  17.4 us (2%)
    ppermute x110, waiting for transfers between devices, shift(): return lax.ppermute(value, axis, pairs)  434 us
    ppermute x110, starting transfers between devices, shift(): return lax.ppermute(value, axis, pairs)  205 us
    dot_general x14, matrix products, mm(): return jnp.dot(a, b, preferred_element_type=F32)  57.8 us
    dot_general x14, matrix products, mm_nt(): lax.dot_general(a, b, (((1,), (1,)), ((), ())), preferred_element_type=F32)  56.7 us
    dot_general x12, matrix products, mm_tn(): lax.dot_general(a, b, (((0,), (0,)), ((), ())), preferred_element_type=F32)  43.4 us
    psum x1, blocking collectives, local(): lax.psum(jnp.stack([jnp.stack([d_first_0, d_second_0]), jnp.stack([d_firs...  26.6 us
    unnamed x220, local copies, waits for them, and re-layouts  25.3 us
  transfers between devices with their start and end apart: 117, of which 49 were waited for; matrix products, arithmetic and copies ran while one was open for 24% of the time, Pallas kernels for 0%

profile of v4, /device:TPU:0, one launch (start us, length us, event | category | flops | bytes accessed | tf_op | source)
XLA Modules:
  0.0 987.9 jit_solution(11980285825630191112)
XLA Ops:
  21.8 16.2 %collective-permute-done = f32[2,640]{1,0:T(2,128)S(1)} collective-permute-done((f32[2,640]{1,0:T(2,128)S(1)}, f32[2,640]{1,0:T(2,128)S(1)}, u32[]{:S(2)}, u32[]{:S(2)}) %collective-permute-start) | collective-permute-done | bytes 5152 | tf_op jit(solution)/shard_map/ppermute | solution.py:21
  57.7 11.9 %broadcast_select_fusion = (bf16[1920,2560]{1,0:T(8,128)(2,1)}, bf16[1920,2560]{1,0:T(8,128)(2,1)}) fusion(bf16[1920,2560]{1,0:T(8,128)(2,1)} %collective-permute-done.6, bf16[1920,2560]{1,0:T(8,128)(2,1)S(1)} %bitcast.163, pred[]{:T(512)S(6)} %eq.462), kind=kLoop, calls=%fused_computation.6 | loop fusion | flops 9830400 | bytes 39321600 | tf_op jit(solution)/shard_map/jit(_where)/select_n | solution.py:441
  69.6 13.3 %collective-permute-done.4 = bf16[64,3200]{1,0:T(8,128)(2,1)S(1)} collective-permute-done((bf16[64,3200]{1,0:T(8,128)(2,1)S(1)}, bf16[64,3200]{1,0:T(8,128)(2,1)S(1)}, u32[]{:S(2)}, u32[]{:S(2)}) %collective-permute-start.4) | collective-permute-done | bytes 409632 | tf_op jit(solution)/shard_map/ppermute | solution.py:21
  85.0 9.3 collective-permute-start.7
  112.0 8.4 collective-permute-done.11
  120.5 12.6 %collective-permute-done.12 = bf16[64,2560]{1,0:T(8,128)(2,1)S(1)} collective-permute-done((bf16[64,2560]{1,0:T(8,128)(2,1)S(1)}, bf16[64,2560]{1,0:T(8,128)(2,1)S(1)}, u32[]{:S(2)}, u32[]{:S(2)}) %collective-permute-start.12) | collective-permute-done | bytes 327712 | tf_op jit(solution)/shard_map/ppermute | solution.py:21
  136.9 6.6 collective-permute-start.14
  151.7 22.1 %collective-permute-done.15 = bf16[256,640]{1,0:T(8,128)(2,1)S(1)} collective-permute-done((bf16[256,640]{1,0:T(8,128)(2,1)S(1)}, bf16[256,640]{1,0:T(8,128)(2,1)S(1)}, u32[]{:S(2)}, u32[]{:S(2)}) %collective-permute-start.15) | collective-permute-done | bytes 327712 | tf_op jit(solution)/shard_map/ppermute | solution.py:21
  180.0 8.4 fusion.1
  188.4 9.3 multiply_convert_fusion.3
  198.6 7.0 convolution_convert_fusion.9
  205.7 6.7 collective-permute-start.23
  221.2 12.5 %collective-permute-done.24 = bf16[256,640]{1,0:T(8,128)(2,1)S(1)} collective-permute-done((bf16[256,640]{1,0:T(8,128)(2,1)S(1)}, bf16[256,640]{1,0:T(8,128)(2,1)S(1)}, u32[]{:S(2)}, u32[]{:S(2)}) %collective-permute-start.24) | collective-permute-done | bytes 327712 | tf_op jit(solution)/shard_map/ppermute | solution.py:21
  235.9 7.5 collective-permute-start.26
  247.5 8.1 collective-permute-done.26
  255.6 15.5 %collective-permute-done.27 = bf16[64,3200]{1,0:T(8,128)(2,1)S(1)} collective-permute-done((bf16[64,3200]{1,0:T(8,128)(2,1)S(1)}, bf16[64,3200]{1,0:T(8,128)(2,1)S(1)}, u32[]{:S(2)}, u32[]{:S(2)}) %collective-permute-start.27) | collective-permute-done | bytes 409632 | tf_op jit(solution)/shard_map/ppermute | solution.py:21
  273.0 9.3 collective-permute-start.29
  301.1 8.1 collective-permute-done.33
  309.1 11.8 %collective-permute-done.34 = bf16[64,2560]{1,0:T(8,128)(2,1)S(1)} collective-permute-done((bf16[64,2560]{1,0:T(8,128)(2,1)S(1)}, bf16[64,2560]{1,0:T(8,128)(2,1)S(1)}, u32[]{:S(2)}, u32[]{:S(2)}) %collective-permute-start.34) | collective-permute-done | bytes 327712 | tf_op jit(solution)/shard_map/ppermute | solution.py:21
  325.4 6.4 collective-permute-start.36
  340.2 22.2 %collective-permute-done.37 = bf16[256,640]{1,0:T(8,128)(2,1)} collective-permute-done((bf16[256,640]{1,0:T(8,128)(2,1)}, bf16[256,640]{1,0:T(8,128)(2,1)}, u32[]{:S(2)}, u32[]{:S(2)}) %collective-permute-start.37) | collective-permute-done | bytes 327712 | tf_op jit(solution)/shard_map/ppermute | solution.py:21
  364.7 7.4 fusion.5
  388.3 9.2 broadcast_select_fusion.13
  404.5 7.1 fusion.11
  411.6 8.1 convolution_convert_fusion.1
  436.6 23.7 %collective-permute-done.47 = f32[256]{0:T(256)S(1)} collective-permute-done((f32[256]{0:T(256)S(1)}, f32[256]{0:T(256)S(1)}, u32[]{:S(2)}, u32[]{:S(2)}) %collective-permute-start.47) | collective-permute-done | bytes 1056 | tf_op jit(solution)/shard_map/ppermute | solution.py:21
  472.0 6.2 collective-permute-done.49
  478.2 13.0 %collective-permute-done.50 = bf16[64,2560]{1,0:T(8,128)(2,1)S(1)} collective-permute-done((bf16[64,2560]{1,0:T(8,128)(2,1)S(1)}, bf16[64,2560]{1,0:T(8,128)(2,1)S(1)}, u32[]{:S(2)}, u32[]{:S(2)}) %collective-permute-start.50) | collective-permute-done | bytes 327712 | tf_op jit(solution)/shard_map/ppermute | solution.py:21
  498.3 6.8 convolution_convert_fusion.7
  526.3 20.0 %collective-permute-done.58 = bf16[64,640]{1,0:T(8,128)(2,1)S(1)} collective-permute-done((bf16[64,640]{1,0:T(8,128)(2,1)S(1)}, bf16[64,640]{1,0:T(8,128)(2,1)S(1)}, u32[]{:S(2)}, u32[]{:S(2)}) %collective-permute-start.58) | collective-permute-done | bytes 81952 | tf_op jit(solution)/shard_map/ppermute | solution.py:21
  546.3 9.6 collective-permute-done.59
  576.5 15.9 %collective-permute-start.70 = (bf16[256,640]{1,0:T(8,128)(2,1)}, bf16[256,640]{1,0:T(8,128)(2,1)}, u32[]{:S(2)}, u32[]{:S(2)}) collective-permute-start(bf16[256,640]{1,0:T(8,128)(2,1)} %get-tuple-element.259), channel_id=1, source_target_pairs={{0,2},{1,3},{2,0},{3,1},{4,6},{5,7},{6,4},{7,5},{8,10},{9,11},{10,... | collective-permute-start | bytes 983048 | tf_op jit(solution)/shard_map/ppermute | solution.py:21
  593.1 18.6 %collective-permute-start.71 = (bf16[256,640]{1,0:T(8,128)(2,1)}, bf16[256,640]{1,0:T(8,128)(2,1)}, u32[]{:S(2)}, u32[]{:S(2)}) collective-permute-start(bf16[256,640]{1,0:T(8,128)(2,1)} %get-tuple-element.257), channel_id=1, source_target_pairs={{0,3},{1,0},{2,1},{3,2},{4,7},{5,4},{6,5},{7,6},{8,11},{9,8},{10,9... | collective-permute-start | bytes 983048 | tf_op jit(solution)/shard_map/ppermute | solution.py:21
  613.3 8.8 broadcast_select_fusion.11
  627.9 6.8 fusion.10
  635.5 10.4 %convolution_convert_fusion = bf16[2560,1920]{1,0:T(8,128)(2,1)} fusion(bf16[256,2560]{1,0:T(8,128)(2,1)} %collective-permute-done.78, bf16[256,2560]{1,0:T(8,128)(2,1)} %fusion.16, bf16[256,1920]{1,0:T(8,128)(2,1)S(1)} %collective-permute-done.79, bf16[256,1920]{1,0:T(8,128)(2,1)S(1)} %get-tuple-element.185), kind=kOutput, calls=%fused_computation | convolution fusion | flops 5047255040 | bytes 14417920 | tf_op jit(solution)/shard_map/dot_general | solution.py:44
  661.5 33.7 %collective-permute-done.88 = bf16[704,640]{1,0:T(8,128)(2,1)} collective-permute-done((bf16[704,640]{1,0:T(8,128)(2,1)}, bf16[704,640]{1,0:T(8,128)(2,1)}, u32[]{:S(2)}, u32[]{:S(2)}) %collective-permute-start.88) | collective-permute-done | bytes 901152 | tf_op jit(solution)/shard_map/ppermute | solution.py:21
  695.2 19.3 %collective-permute-done.89 = bf16[704,640]{1,0:T(8,128)(2,1)} collective-permute-done((bf16[704,640]{1,0:T(8,128)(2,1)}, bf16[704,640]{1,0:T(8,128)(2,1)}, u32[]{:S(2)}, u32[]{:S(2)}) %collective-permute-start.89) | collective-permute-done | bytes 901152 | tf_op jit(solution)/shard_map/ppermute | solution.py:21
  714.5 19.1 %collective-permute-done.90 = bf16[704,640]{1,0:T(8,128)(2,1)} collective-permute-done((bf16[704,640]{1,0:T(8,128)(2,1)}, bf16[704,640]{1,0:T(8,128)(2,1)}, u32[]{:S(2)}, u32[]{:S(2)}) %collective-permute-start.90) | collective-permute-done | bytes 901152 | tf_op jit(solution)/shard_map/ppermute | solution.py:21
  754.8 6.2 convolution_convert_fusion.2
  768.4 15.2 %collective-permute-done.74 = bf16[256,640]{1,0:T(8,128)(2,1)} collective-permute-done((bf16[256,640]{1,0:T(8,128)(2,1)}, bf16[256,640]{1,0:T(8,128)(2,1)}, u32[]{:S(2)}, u32[]{:S(2)}) %collective-permute-start.74) | collective-permute-done | bytes 327712 | tf_op jit(solution)/shard_map/ppermute | solution.py:21
  803.3 13.0 %collective-permute-done.84 = bf16[64,2560]{1,0:T(8,128)(2,1)} collective-permute-done((bf16[64,2560]{1,0:T(8,128)(2,1)}, bf16[64,2560]{1,0:T(8,128)(2,1)}, u32[]{:S(2)}, u32[]{:S(2)}) %collective-permute-start.84) | collective-permute-done | bytes 327712 | tf_op jit(solution)/shard_map/ppermute | solution.py:21
  826.2 7.2 collective-permute-start.98
  838.8 16.1 %collective-permute-done.94 = bf16[64,512]{1,0:T(8,128)(2,1)S(1)} collective-permute-done((bf16[64,512]{1,0:T(8,128)(2,1)S(1)}, bf16[64,512]{1,0:T(8,128)(2,1)S(1)}, u32[]{:S(2)}, u32[]{:S(2)}) %collective-permute-start.94) | collective-permute-done | bytes 65568 | tf_op jit(solution)/shard_map/ppermute | solution.py:21
  879.0 26.6 %psum.7 = f32[2,2,640]{2,1,0:T(2,128)S(1)} all-reduce(f32[2,2,640]{2,1,0:T(2,128)S(1)} %pad_maximum_fusion.28), channel_id=1, replica_groups=mesh['section'=2,'ctx'=4,'wt'=4] {'section','ctx'}, use_global_device_ids=true, to_apply=%region_33.34 | all-reduce | flops 2560 | bytes 20480 | tf_op jit(solution)/shard_map/psum | solution.py:494
  920.3 16.8 %collective-permute-done.104 = bf16[704,640]{1,0:T(8,128)(2,1)} collective-permute-done((bf16[704,640]{1,0:T(8,128)(2,1)}, bf16[704,640]{1,0:T(8,128)(2,1)}, u32[]{:S(2)}, u32[]{:S(2)}) %collective-permute-start.104) | collective-permute-done | bytes 901152 | tf_op jit(solution)/shard_map/ppermute | solution.py:21
  937.2 17.8 %collective-permute-done.105 = bf16[704,640]{1,0:T(8,128)(2,1)} collective-permute-done((bf16[704,640]{1,0:T(8,128)(2,1)}, bf16[704,640]{1,0:T(8,128)(2,1)}, u32[]{:S(2)}, u32[]{:S(2)}) %collective-permute-start.105) | collective-permute-done | bytes 901152 | tf_op jit(solution)/shard_map/ppermute | solution.py:21
  958.6 6.9 select_convert_fusion
  (712 shorter events, 367.9 us)
Async XLA Ops:
  7.2 126.0 %all-gather.4.cloned.1.call-start = ((), (), s32[]{:S(2)}) async-start(), calls=%async_computation.4 | async-start | bytes 9830400 | tf_op jit(solution)/shard_map/all_gather | solution.py:436
  7.9 172.1 %all-gather.6.cloned.1.call-start = ((), (), s32[]{:S(2)}) async-start(), calls=%async_computation.5 | async-start | bytes 29491200 | tf_op jit(solution)/shard_map/all_gather | solution.py:436
  8.7 179.7 %all-gather.8.cloned.1.call-start = ((), (), s32[]{:S(2)}) async-start(), calls=%async_computation.6 | async-start | bytes 29491200 | tf_op jit(solution)/shard_map/all_gather | solution.py:436
  17.8 39.9 %collective-permute-start.6 = (bf16[1920,2560]{1,0:T(8,128)(2,1)}, bf16[1920,2560]{1,0:T(8,128)(2,1)}, u32[]{:S(2)}, u32[]{:S(2)}) collective-permute-start(bf16[1920,2560]{1,0:T(8,128)(2,1)} %bitcast.160), channel_id=1, source_target_pairs={{0,16},{16,0},{1,17},{17,1},{2,18},{18,2},{3,19},{19,3},{4,20},{20... | collective-permute-start | bytes 29491208 | tf_op jit(solution)/shard_map/ppermute | solution.py:21
  18.2 473.0 %reduce-scatter.5.cloned.1.call-start = ((), (), s32[]{:S(2)}) async-start(), calls=%async_computation.7 | async-start | bytes 6144000 | tf_op jit(solution)/shard_map/reduce_scatter | solution.py:406
  55.2 27.7 %collective-permute-start.4 = (bf16[64,3200]{1,0:T(8,128)(2,1)S(1)}, bf16[64,3200]{1,0:T(8,128)(2,1)S(1)}, u32[]{:S(2)}, u32[]{:S(2)}) collective-permute-start(bf16[64,3200]{1,0:T(8,128)(2,1)S(1)} %get-tuple-element.225), channel_id=1, source_target_pairs={{0,2},{1,3},{2,0},{3,1},{4,6},{5,7},{6,4},{7,5},{8,10},{9,11},{10,... | collective-permute-start | bytes 1228808 | tf_op jit(solution)/shard_map/ppermute | solution.py:21
  56.1 26.8 %collective-permute-start.5 = (bf16[64,3200]{1,0:T(8,128)(2,1)S(1)}, bf16[64,3200]{1,0:T(8,128)(2,1)S(1)}, u32[]{:S(2)}, u32[]{:S(2)}) collective-permute-start(bf16[64,3200]{1,0:T(8,128)(2,1)S(1)} %get-tuple-element.224), channel_id=1, source_target_pairs={{0,3},{1,0},{2,1},{3,2},{4,7},{5,4},{6,5},{7,6},{8,11},{9,8},{10,9... | collective-permute-start | bytes 1228808 | tf_op jit(solution)/shard_map/ppermute | solution.py:21
  143.5 30.3 %collective-permute-start.15 = (bf16[256,640]{1,0:T(8,128)(2,1)S(1)}, bf16[256,640]{1,0:T(8,128)(2,1)S(1)}, u32[]{:S(2)}, u32[]{:S(2)}) collective-permute-start(bf16[256,640]{1,0:T(8,128)(2,1)S(1)} %get-tuple-element.395), channel_id=1, source_target_pairs={{0,2},{1,3},{2,0},{3,1},{4,6},{5,7},{6,4},{7,5},{8,10},{9,11},{10,... | collective-permute-start | bytes 983048 | tf_op jit(solution)/shard_map/ppermute | solution.py:21
  145.5 28.3 %collective-permute-start.16 = (bf16[256,640]{1,0:T(8,128)(2,1)S(1)}, bf16[256,640]{1,0:T(8,128)(2,1)S(1)}, u32[]{:S(2)}, u32[]{:S(2)}) collective-permute-start(bf16[256,640]{1,0:T(8,128)(2,1)S(1)} %get-tuple-element.395), channel_id=1, source_target_pairs={{0,1},{1,2},{2,3},{3,0},{4,5},{5,6},{6,7},{7,4},{8,9},{9,10},{10,1... | collective-permute-start | bytes 983048 | tf_op jit(solution)/shard_map/ppermute | solution.py:21
  243.5 27.6 %collective-permute-start.27 = (bf16[64,3200]{1,0:T(8,128)(2,1)S(1)}, bf16[64,3200]{1,0:T(8,128)(2,1)S(1)}, u32[]{:S(2)}, u32[]{:S(2)}) collective-permute-start(bf16[64,3200]{1,0:T(8,128)(2,1)S(1)} %get-tuple-element.222), channel_id=1, source_target_pairs={{0,2},{1,3},{2,0},{3,1},{4,6},{5,7},{6,4},{7,5},{8,10},{9,11},{10,... | collective-permute-start | bytes 1228808 | tf_op jit(solution)/shard_map/ppermute | solution.py:21
  331.8 30.6 %collective-permute-start.37 = (bf16[256,640]{1,0:T(8,128)(2,1)}, bf16[256,640]{1,0:T(8,128)(2,1)}, u32[]{:S(2)}, u32[]{:S(2)}) collective-permute-start(bf16[256,640]{1,0:T(8,128)(2,1)} %get-tuple-element.401), channel_id=1, source_target_pairs={{0,2},{1,3},{2,0},{3,1},{4,6},{5,7},{6,4},{7,5},{8,10},{9,11},{10,... | collective-permute-start | bytes 983048 | tf_op jit(solution)/shard_map/ppermute | solution.py:21
  333.9 28.5 %collective-permute-start.38 = (bf16[256,640]{1,0:T(8,128)(2,1)}, bf16[256,640]{1,0:T(8,128)(2,1)}, u32[]{:S(2)}, u32[]{:S(2)}) collective-permute-start(bf16[256,640]{1,0:T(8,128)(2,1)} %get-tuple-element.401), channel_id=1, source_target_pairs={{0,1},{1,2},{2,3},{3,0},{4,5},{5,6},{6,7},{7,4},{8,9},{9,10},{10,1... | collective-permute-start | bytes 983048 | tf_op jit(solution)/shard_map/ppermute | solution.py:21
  386.5 225.2 %reduce-scatter.7.cloned.1.call-start = ((), (), s32[]{:S(2)}) async-start(), calls=%async_computation.8 | async-start | bytes 12288000 | tf_op jit(solution)/shard_map/reduce_scatter | solution.py:406
  419.8 455.8 %reduce-scatter.11.cloned.1.call-start = ((), (), s32[]{:S(2)}) async-start(), calls=%async_computation.10 | async-start | bytes 12288000 | tf_op jit(solution)/shard_map/reduce_scatter | solution.py:406
  427.3 33.0 %collective-permute-start.41 = (bf16[256,640]{1,0:T(8,128)(2,1)S(1)}, bf16[256,640]{1,0:T(8,128)(2,1)S(1)}, u32[]{:S(2)}, u32[]{:S(2)}) collective-permute-start(bf16[256,640]{1,0:T(8,128)(2,1)S(1)} %get-tuple-element.287), channel_id=1, source_target_pairs={{0,1},{1,2},{2,3},{3,0},{4,5},{5,6},{6,7},{7,4},{8,9},{9,10},{10,1... | collective-permute-start | bytes 983048 | tf_op jit(solution)/shard_map/ppermute | solution.py:21
  427.4 33.0 %collective-permute-start.43 = (bf16[256,640]{1,0:T(8,128)(2,1)S(1)}, bf16[256,640]{1,0:T(8,128)(2,1)S(1)}, u32[]{:S(2)}, u32[]{:S(2)}) collective-permute-start(bf16[256,640]{1,0:T(8,128)(2,1)S(1)} %get-tuple-element.286), channel_id=1, source_target_pairs={{0,3},{1,0},{2,1},{3,2},{4,7},{5,4},{6,5},{7,6},{8,11},{9,8},{10,9... | collective-permute-start | bytes 983048 | tf_op jit(solution)/shard_map/ppermute | solution.py:21
  431.2 29.1 %collective-permute-start.42 = (bf16[256,640]{1,0:T(8,128)(2,1)S(1)}, bf16[256,640]{1,0:T(8,128)(2,1)S(1)}, u32[]{:S(2)}, u32[]{:S(2)}) collective-permute-start(bf16[256,640]{1,0:T(8,128)(2,1)S(1)} %select_select_fusion.12), channel_id=1, source_target_pairs={{0,2},{1,3},{2,0},{3,1},{4,6},{5,7},{6,4},{7,5},{8,10},{9,11},{10,... | collective-permute-start | bytes 983048 | tf_op jit(solution)/shard_map/ppermute | solution.py:21
  431.7 28.6 %collective-permute-start.47 = (f32[256]{0:T(256)S(1)}, f32[256]{0:T(256)S(1)}, u32[]{:S(2)}, u32[]{:S(2)}) collective-permute-start(f32[256]{0:T(256)S(1)} %add_reduce_fusion.1), channel_id=1, source_target_pairs={{0,2},{1,3},{2,0},{3,1},{4,6},{5,7},{6,4},{7,5},{8,10},{9,11},{10,... | collective-permute-start | bytes 3080 | tf_op jit(solution)/shard_map/ppermute | solution.py:21
  434.1 26.2 %collective-permute-start.48 = (f32[256]{0:T(256)S(1)}, f32[256]{0:T(256)S(1)}, u32[]{:S(2)}, u32[]{:S(2)}) collective-permute-start(f32[256]{0:T(256)S(1)} %add_reduce_fusion.1), channel_id=1, source_target_pairs={{0,3},{1,0},{2,1},{3,2},{4,7},{5,4},{6,5},{7,6},{8,11},{9,8},{10,9... | collective-permute-start | bytes 3080 | tf_op jit(solution)/shard_map/ppermute | solution.py:21
  465.8 25.4 %collective-permute-start.50 = (bf16[64,2560]{1,0:T(8,128)(2,1)S(1)}, bf16[64,2560]{1,0:T(8,128)(2,1)S(1)}, u32[]{:S(2)}, u32[]{:S(2)}) collective-permute-start(bf16[64,2560]{1,0:T(8,128)(2,1)S(1)} %get-tuple-element.284), channel_id=1, source_target_pairs={{0,2},{1,3},{2,0},{3,1},{4,6},{5,7},{6,4},{7,5},{8,10},{9,11},{10,... | collective-permute-start | bytes 983048 | tf_op jit(solution)/shard_map/ppermute | solution.py:21
  518.5 38.6 %collective-permute-start.61 = (bf16[64,2560]{1,0:T(8,128)(2,1)S(1)}, bf16[64,2560]{1,0:T(8,128)(2,1)S(1)}, u32[]{:S(2)}, u32[]{:S(2)}) collective-permute-start(bf16[64,2560]{1,0:T(8,128)(2,1)S(1)} %bitcast.173), channel_id=1, source_target_pairs={{0,1},{1,2},{2,3},{3,0},{4,5},{5,6},{6,7},{7,4},{8,9},{9,10},{10,1... | collective-permute-start | bytes 983048 | tf_op jit(solution)/shard_map/ppermute | solution.py:21
  520.5 36.7 %collective-permute-start.62 = (bf16[64,2560]{1,0:T(8,128)(2,1)S(1)}, bf16[64,2560]{1,0:T(8,128)(2,1)S(1)}, u32[]{:S(2)}, u32[]{:S(2)}) collective-permute-start(bf16[64,2560]{1,0:T(8,128)(2,1)S(1)} %bitcast.174), channel_id=1, source_target_pairs={{0,2},{1,3},{2,0},{3,1},{4,6},{5,7},{6,4},{7,5},{8,10},{9,11},{10,... | collective-permute-start | bytes 983048 | tf_op jit(solution)/shard_map/ppermute | solution.py:21
  522.0 35.2 %collective-permute-start.63 = (bf16[64,2560]{1,0:T(8,128)(2,1)S(1)}, bf16[64,2560]{1,0:T(8,128)(2,1)S(1)}, u32[]{:S(2)}, u32[]{:S(2)}) collective-permute-start(bf16[64,2560]{1,0:T(8,128)(2,1)S(1)} %bitcast.175), channel_id=1, source_target_pairs={{0,3},{1,0},{2,1},{3,2},{4,7},{5,4},{6,5},{7,6},{8,11},{9,8},{10,9... | collective-permute-start | bytes 983048 | tf_op jit(solution)/shard_map/ppermute | solution.py:21
  524.8 31.1 %collective-permute-start.59 = (bf16[64,640]{1,0:T(8,128)(2,1)S(1)}, bf16[64,640]{1,0:T(8,128)(2,1)S(1)}, u32[]{:S(2)}, u32[]{:S(2)}) collective-permute-start(bf16[64,640]{1,0:T(8,128)(2,1)S(1)} %get-tuple-element.364), channel_id=1, source_target_pairs={{0,2},{1,3},{2,0},{3,1},{4,6},{5,7},{6,4},{7,5},{8,10},{9,11},{10,... | collective-permute-start | bytes 245768 | tf_op jit(solution)/shard_map/ppermute | solution.py:21
  566.3 26.1 %collective-permute-start.65 = (bf16[256,640]{1,0:T(8,128)(2,1)S(1)}, bf16[256,640]{1,0:T(8,128)(2,1)S(1)}, u32[]{:S(2)}, u32[]{:S(2)}) collective-permute-start(bf16[256,640]{1,0:T(8,128)(2,1)S(1)} %get-tuple-element.190), channel_id=1, source_target_pairs={{0,2},{1,3},{2,0},{3,1},{4,6},{5,7},{6,4},{7,5},{8,10},{9,11},{10,... | collective-permute-start | bytes 983048 | tf_op jit(solution)/shard_map/ppermute | solution.py:21
  567.8 44.0 %collective-permute-start.66 = (bf16[256,640]{1,0:T(8,128)(2,1)S(1)}, bf16[256,640]{1,0:T(8,128)(2,1)}, u32[]{:S(2)}, u32[]{:S(2)}) collective-permute-start(bf16[256,640]{1,0:T(8,128)(2,1)S(1)} %get-tuple-element.190), channel_id=1, source_target_pairs={{0,3},{1,0},{2,1},{3,2},{4,7},{5,4},{6,5},{7,6},{8,11},{9,8},{10,9... | collective-permute-start | bytes 983048 | tf_op jit(solution)/shard_map/ppermute | solution.py:21
  571.7 63.8 %collective-permute-start.78 = (bf16[256,2560]{1,0:T(8,128)(2,1)}, bf16[256,2560]{1,0:T(8,128)(2,1)}, u32[]{:S(2)}, u32[]{:S(2)}) collective-permute-start(bf16[256,2560]{1,0:T(8,128)(2,1)} %fusion.16), channel_id=1, source_target_pairs={{0,16},{16,0},{1,17},{17,1},{2,18},{18,2},{3,19},{19,3},{4,20},{20... | collective-permute-start | bytes 3932168 | tf_op jit(solution)/shard_map/ppermute | solution.py:21
  571.7 63.0 %collective-permute-start.69 = (bf16[256,640]{1,0:T(8,128)(2,1)}, bf16[256,640]{1,0:T(8,128)(2,1)S(1)}, u32[]{:S(2)}, u32[]{:S(2)}) collective-permute-start(bf16[256,640]{1,0:T(8,128)(2,1)} %get-tuple-element.260), channel_id=1, source_target_pairs={{0,1},{1,2},{2,3},{3,0},{4,5},{5,6},{6,7},{7,4},{8,9},{9,10},{10,1... | collective-permute-start | bytes 983048 | tf_op jit(solution)/shard_map/ppermute | solution.py:21
  576.5 58.2 %collective-permute-start.70 = (bf16[256,640]{1,0:T(8,128)(2,1)}, bf16[256,640]{1,0:T(8,128)(2,1)}, u32[]{:S(2)}, u32[]{:S(2)}) collective-permute-start(bf16[256,640]{1,0:T(8,128)(2,1)} %get-tuple-element.259), channel_id=1, source_target_pairs={{0,2},{1,3},{2,0},{3,1},{4,6},{5,7},{6,4},{7,5},{8,10},{9,11},{10,... | collective-permute-start | bytes 983048 | tf_op jit(solution)/shard_map/ppermute | solution.py:21
  593.1 41.6 %collective-permute-start.71 = (bf16[256,640]{1,0:T(8,128)(2,1)}, bf16[256,640]{1,0:T(8,128)(2,1)}, u32[]{:S(2)}, u32[]{:S(2)}) collective-permute-start(bf16[256,640]{1,0:T(8,128)(2,1)} %get-tuple-element.257), channel_id=1, source_target_pairs={{0,3},{1,0},{2,1},{3,2},{4,7},{5,4},{6,5},{7,6},{8,11},{9,8},{10,9... | collective-permute-start | bytes 983048 | tf_op jit(solution)/shard_map/ppermute | solution.py:21
  645.9 273.0 %reduce-scatter.9.cloned.1.call-start = ((), (), s32[]{:S(2)}) async-start(), calls=%async_computation.9 | async-start | bytes 6144000 | tf_op jit(solution)/shard_map/reduce_scatter | solution.py:406
  651.8 43.4 %collective-permute-start.88 = (bf16[704,640]{1,0:T(8,128)(2,1)}, bf16[704,640]{1,0:T(8,128)(2,1)}, u32[]{:S(2)}, u32[]{:S(2)}) collective-permute-start(bf16[704,640]{1,0:T(8,128)(2,1)} %get-tuple-element.214), channel_id=1, source_target_pairs={{0,4},{4,8},{8,12},{12,0},{1,5},{5,9},{9,13},{13,1},{2,6},{6,10},{... | collective-permute-start | bytes 2703368 | tf_op jit(solution)/shard_map/ppermute | solution.py:21
  653.3 61.2 %collective-permute-start.89 = (bf16[704,640]{1,0:T(8,128)(2,1)}, bf16[704,640]{1,0:T(8,128)(2,1)}, u32[]{:S(2)}, u32[]{:S(2)}) collective-permute-start(bf16[704,640]{1,0:T(8,128)(2,1)} %get-tuple-element.216), channel_id=1, source_target_pairs={{0,8},{4,12},{8,0},{12,4},{1,9},{5,13},{9,1},{13,5},{2,10},{6,14},... | collective-permute-start | bytes 2703368 | tf_op jit(solution)/shard_map/ppermute | solution.py:21
  654.6 79.0 %collective-permute-start.90 = (bf16[704,640]{1,0:T(8,128)(2,1)}, bf16[704,640]{1,0:T(8,128)(2,1)}, u32[]{:S(2)}, u32[]{:S(2)}) collective-permute-start(bf16[704,640]{1,0:T(8,128)(2,1)} %get-tuple-element.215), channel_id=1, source_target_pairs={{0,12},{4,0},{8,4},{12,8},{1,13},{5,1},{9,5},{13,9},{2,14},{6,2},{... | collective-permute-start | bytes 2703368 | tf_op jit(solution)/shard_map/ppermute | solution.py:21
  661.4 93.0 %collective-permute-start.77 = (bf16[256,1920]{1,0:T(8,128)(2,1)}, bf16[256,1920]{1,0:T(8,128)(2,1)}, u32[]{:S(2)}, u32[]{:S(2)}) collective-permute-start(bf16[256,1920]{1,0:T(8,128)(2,1)} %get-tuple-element.65), channel_id=1, source_target_pairs={{0,16},{16,0},{1,17},{17,1},{2,18},{18,2},{3,19},{19,3},{4,20},{20... | collective-permute-start | bytes 2949128 | tf_op jit(solution)/shard_map/ppermute | solution.py:21
  750.5 45.7 %collective-permute-start.86 = (bf16[256,1280]{1,0:T(8,128)(2,1)}, bf16[256,1280]{1,0:T(8,128)(2,1)}, u32[]{:S(2)}, u32[]{:S(2)}) collective-permute-start(bf16[256,1280]{1,0:T(8,128)(2,1)} %get-tuple-element.241), channel_id=1, source_target_pairs={{0,16},{16,0},{1,17},{17,1},{2,18},{18,2},{3,19},{19,3},{4,20},{20... | collective-permute-start | bytes 1966088 | tf_op jit(solution)/shard_map/ppermute | solution.py:21
  754.4 29.1 %collective-permute-start.74 = (bf16[256,640]{1,0:T(8,128)(2,1)}, bf16[256,640]{1,0:T(8,128)(2,1)}, u32[]{:S(2)}, u32[]{:S(2)}) collective-permute-start(bf16[256,640]{1,0:T(8,128)(2,1)} %select_select_fusion.1), channel_id=1, source_target_pairs={{0,2},{1,3},{2,0},{3,1},{4,6},{5,7},{6,4},{7,5},{8,10},{9,11},{10,... | collective-permute-start | bytes 983048 | tf_op jit(solution)/shard_map/ppermute | solution.py:21
  754.7 37.6 %collective-permute-start.72 = (bf16[256,640]{1,0:T(8,128)(2,1)S(1)}, bf16[256,640]{1,0:T(8,128)(2,1)}, u32[]{:S(2)}, u32[]{:S(2)}) collective-permute-start(bf16[256,640]{1,0:T(8,128)(2,1)S(1)} %add_convert_fusion.3), channel_id=1, source_target_pairs={{0,16},{16,0},{1,17},{17,1},{2,18},{18,2},{3,19},{19,3},{4,20},{20... | collective-permute-start | bytes 983048 | tf_op jit(solution)/shard_map/ppermute | solution.py:21
  790.4 25.9 %collective-permute-start.84 = (bf16[64,2560]{1,0:T(8,128)(2,1)}, bf16[64,2560]{1,0:T(8,128)(2,1)}, u32[]{:S(2)}, u32[]{:S(2)}) collective-permute-start(bf16[64,2560]{1,0:T(8,128)(2,1)} %get-tuple-element.251), channel_id=1, source_target_pairs={{0,2},{1,3},{2,0},{3,1},{4,6},{5,7},{6,4},{7,5},{8,10},{9,11},{10,... | collective-permute-start | bytes 983048 | tf_op jit(solution)/shard_map/ppermute | solution.py:21
  826.2 41.8 %collective-permute-start.98 = (bf16[64,2560]{1,0:T(8,128)(2,1)S(1)}, bf16[64,2560]{1,0:T(8,128)(2,1)S(1)}, u32[]{:S(2)}, u32[]{:S(2)}) collective-permute-start(bf16[64,2560]{1,0:T(8,128)(2,1)S(1)} %bitcast.168), channel_id=1, source_target_pairs={{0,1},{1,2},{2,3},{3,0},{4,5},{5,6},{6,7},{7,4},{8,9},{9,10},{10,1... | collective-permute-start | bytes 983048 | tf_op jit(solution)/shard_map/ppermute | solution.py:21
  833.4 34.7 %collective-permute-start.99 = (bf16[64,2560]{1,0:T(8,128)(2,1)S(1)}, bf16[64,2560]{1,0:T(8,128)(2,1)S(1)}, u32[]{:S(2)}, u32[]{:S(2)}) collective-permute-start(bf16[64,2560]{1,0:T(8,128)(2,1)S(1)} %bitcast.169), channel_id=1, source_target_pairs={{0,2},{1,3},{2,0},{3,1},{4,6},{5,7},{6,4},{7,5},{8,10},{9,11},{10,... | collective-permute-start | bytes 983048 | tf_op jit(solution)/shard_map/ppermute | solution.py:21
  833.4 34.7 %collective-permute-start.100 = (bf16[64,2560]{1,0:T(8,128)(2,1)S(1)}, bf16[64,2560]{1,0:T(8,128)(2,1)S(1)}, u32[]{:S(2)}, u32[]{:S(2)}) collective-permute-start(bf16[64,2560]{1,0:T(8,128)(2,1)S(1)} %bitcast.170), channel_id=1, source_target_pairs={{0,3},{1,0},{2,1},{3,2},{4,7},{5,4},{6,5},{7,6},{8,11},{9,8},{10,9... | collective-permute-start | bytes 983048 | tf_op jit(solution)/shard_map/ppermute | solution.py:21
  875.0 31.9 %collective-permute-start.102 = (bf16[256,1536]{1,0:T(8,128)(2,1)}, bf16[256,1536]{1,0:T(8,128)(2,1)}, u32[]{:S(2)}, u32[]{:S(2)}) collective-permute-start(bf16[256,1536]{1,0:T(8,128)(2,1)} %broadcast_select_fusion.18), channel_id=1, source_target_pairs={{0,16},{16,0},{1,17},{17,1},{2,18},{18,2},{3,19},{19,3},{4,20},{20... | collective-permute-start | bytes 2359304 | tf_op jit(solution)/shard_map/ppermute | solution.py:21
  875.0 31.9 %collective-permute-start.103 = (bf16[256,640]{1,0:T(8,128)(2,1)}, bf16[256,640]{1,0:T(8,128)(2,1)}, u32[]{:S(2)}, u32[]{:S(2)}) collective-permute-start(bf16[256,640]{1,0:T(8,128)(2,1)} %get-tuple-element.317), channel_id=1, source_target_pairs={{0,16},{16,0},{1,17},{17,1},{2,18},{18,2},{3,19},{19,3},{4,20},{20... | collective-permute-start | bytes 983048 | tf_op jit(solution)/shard_map/ppermute | solution.py:21
  877.3 81.4 %collective-permute-start.108 = (bf16[640,1920]{1,0:T(8,128)(2,1)}, bf16[640,1920]{1,0:T(8,128)(2,1)}, u32[]{:S(2)}, u32[]{:S(2)}) collective-permute-start(bf16[640,1920]{1,0:T(8,128)(2,1)} %broadcast_select_fusion.4), channel_id=1, source_target_pairs={{0,16},{16,0},{1,17},{17,1},{2,18},{18,2},{3,19},{19,3},{4,20},{20... | collective-permute-start | bytes 7372808 | tf_op jit(solution)/shard_map/ppermute | solution.py:21
  913.0 41.9 %collective-permute-start.105 = (bf16[704,640]{1,0:T(8,128)(2,1)}, bf16[704,640]{1,0:T(8,128)(2,1)}, u32[]{:S(2)}, u32[]{:S(2)}) collective-permute-start(bf16[704,640]{1,0:T(8,128)(2,1)} %get-tuple-element.213), channel_id=1, source_target_pairs={{0,8},{4,12},{8,0},{12,4},{1,9},{5,13},{9,1},{13,5},{2,10},{6,14},... | collective-permute-start | bytes 2703368 | tf_op jit(solution)/shard_map/ppermute | solution.py:21
  914.7 41.5 %collective-permute-start.106 = (bf16[704,640]{1,0:T(8,128)(2,1)}, bf16[704,640]{1,0:T(8,128)(2,1)}, u32[]{:S(2)}, u32[]{:S(2)}) collective-permute-start(bf16[704,640]{1,0:T(8,128)(2,1)} %get-tuple-element.212), channel_id=1, source_target_pairs={{0,12},{4,0},{8,4},{12,8},{1,13},{5,1},{9,5},{13,9},{2,14},{6,2},{... | collective-permute-start | bytes 2703368 | tf_op jit(solution)/shard_map/ppermute | solution.py:21
  920.3 46.3 %collective-permute-start.107 = (bf16[320,1920]{1,0:T(8,128)(2,1)S(1)}, bf16[320,1920]{1,0:T(8,128)(2,1)S(1)}, u32[]{:S(2)}, u32[]{:S(2)}) collective-permute-start(bf16[320,1920]{1,0:T(8,128)(2,1)S(1)} %broadcast_select_fusion.8), channel_id=1, source_target_pairs={{0,16},{16,0},{1,17},{17,1},{2,18},{18,2},{3,19},{19,3},{4,20},{20... | collective-permute-start | bytes 3686408 | tf_op jit(solution)/shard_map/ppermute | solution.py:21
  (173 other events, 2261.7 us)
Sparse Core Ops, SparseCore 0:
  9.5 23.9 all-gather.3
  35.1 35.5 all-gather.5
  72.3 35.5 all-gather.7
  386.6 56.4 reduce-scatter.4
  446.2 103.7 reduce-scatter.6
  646.0 134.3 reduce-scatter.10
  796.3 60.2 reduce-scatter.8

commit v5 on v4

--- a/solution.py
+++ b/solution.py
@@ -74,12 +74,16 @@
 
 
 def reduce_rows(value, axis, fillers=()):
+    own, *received = send_rows(value, axis)
+    return add_up([own] + after(received, fillers))
+
+
+def send_rows(value, axis):
     count = lax.axis_size(axis)
     me = lax.axis_index(axis)
     rows = value.shape[0] // count
     blocks = [lax.dynamic_slice_in_dim(value, (me + s) % count * rows, rows, 0) for s in range(count)]
-    received = after([shift(blocks[s], axis, s) for s in range(1, count)], fillers)
-    return sum((part.astype(F32) for part in received), blocks[0].astype(F32))
+    return [blocks[0]] + [shift(blocks[s], axis, s) for s in range(1, count)]
 
 
 def send_cols(value, axis):
@@ -105,6 +109,13 @@
     for s in range(1, lax.axis_size(axis)):
         total = total + shift(value, axis, s)
     return total
+
+
+def sum_in_order(value, axis):
+    count = lax.axis_size(axis)
+    me = lax.axis_index(axis)
+    parts = [value] + [shift(value, axis, s) for s in range(1, count)]
+    return sum(pick((me - place) % count, parts) for place in range(count))
 
 
 def split_two(value):
@@ -193,9 +204,9 @@
     square = jnp.sum(source * source, axis=1)
     scaled = (source * gain_first).astype(BF)
     partial = jnp.concatenate([mm(scaled, w_proj).astype(BF), side_columns([square])], axis=1)
+    total = reduce_rows(partial, "wt", fillers)
     if callable(gain_second):
-        partial, gain_second = gain_second(partial)
-    total = reduce_rows(partial, "wt", fillers)
+        total, gain_second = gain_second(total)
     proj_width = query_width + 2 * head_size
     square_all = total[:, proj_width] + total[:, proj_width + 1]
     inv_first = lax.rsqrt(square_all / width_all + EPS)
@@ -288,13 +299,11 @@
     rows = layout.rows
     score_scale = head_size ** (-0.5)
     attention_kept = None
-    output_parts = None
     if behind is not None:
-        attention_grads, sums, update = behind
+        attention_grads, sums = behind
         attention_grads = attention_grads()
-        attention_kept = keep_fast(attention_grads)
+        attention_kept = keep(*attention_grads)
         grad_full = gather_cols(grad_out.astype(BF), "wt", attention_grads + [sums])
-        output_parts = send_cols(*after([update], [grad_full]), "wt")
     down = weight_grad(
         both_halves(section_id, *row_halves(grad_full, n_ctx)), both_sections(hidden_act)
     )
@@ -307,8 +316,6 @@
     d_up = (d_hidden * activated).astype(BF)
     inner_part = jnp.sum(d_gate.astype(F32) * gate_pre + d_up.astype(F32) * up_pre, axis=1)
     d_normed_part = (mm_nt(d_gate, w_gate) + mm_nt(d_up, w_up)).astype(BF)
-    if output_parts is not None:
-        d_normed_part, *output_parts = lax.optimization_barrier((d_normed_part, *output_parts))
     inner_part, normed_other = after([inner_part, shift(normed_second, "section", 1)], [d_normed_part])
     inner = sum_small(inner_part, "wt") / (inv_second * width_all)
     gate_up = weight_grad(
@@ -364,8 +371,7 @@
         )
         return [out_grad, proj_grad]
 
-    output = None if output_parts is None else add_up(output_parts)
-    return d_source, (down_kept, gate_up_kept), attention_grads, attention_kept, d_gain_first, d_gain_second, output
+    return d_source, (down_kept, gate_up_kept), attention_grads, attention_kept, d_gain_first, d_gain_second
 
 
 def both_sections(value):
@@ -402,15 +408,16 @@
     return natural(mm_tn(left, right).astype(BF))
 
 
-def keep(partial):
-    return lax.psum_scatter(partial, "ctx", scatter_dimension=0, tiled=True)
-
-
-def keep_fast(partials):
+def keep(*partials):
     n_ctx = lax.axis_size("ctx")
+    return lax.psum_scatter(stack_rows(partials, n_ctx), "ctx", scatter_dimension=0, tiled=True)
+
+
+def stack_rows(partials, n_ctx):
+    if len(partials) == 1:
+        return partials[0]
     blocks = [partial.reshape(n_ctx, -1, partial.shape[1]) for partial in partials]
-    joined = jnp.concatenate(blocks, axis=1)
-    return reduce_rows(joined.reshape(-1, joined.shape[2]), "ctx").astype(BF)
+    return jnp.concatenate(blocks, axis=1).reshape(-1, partials[0].shape[1])
 
 
 def home(section_id, first_block, second_block):
@@ -447,10 +454,11 @@
         [shift(wq[0], "section", 1), shift(jnp.concatenate([wk[0], wv[0]], axis=1), "section", 1)], axis=1
     )
     own_proj = jnp.concatenate([wq[0], wk[0], wv[0]], axis=1)
+    other_proj, other_gains, w_down_late = lax.optimization_barrier((other_proj, other_gains, w_down[0]))
     w_proj = lax.optimization_barrier(
         (jnp.where(section_id == 0, own_proj, other_proj), jnp.where(section_id == 0, other_proj, own_proj))
     )
-    weights = (w_proj, fetch(wo[0]), fetch(w_gate[0]), fetch(w_up[0]), fetch_fast(after([w_down[0]], [other_proj])[0]))
+    weights = (w_proj, fetch(wo[0]), fetch(w_gate[0]), fetch(w_up[0]), fetch_fast(w_down_late))
     gains = [jnp.where(section_id == 0, gains, other_gains), jnp.where(section_id == 0, other_gains, gains)]
     second_full = []
 
@@ -473,14 +481,20 @@
     for l in range(n_section):
         params[l][1] = second_full[0][l]
     update, saved_1, _ = layer_forward(state, layout, params[1], last=True)
-    grad, feed_1, pending, _, d_first_1, d_second_1, _ = layer_backward(
+    grad, feed_1, pending, _, d_first_1, d_second_1 = layer_backward(
         cotangent.astype(F32), grad_full, layout, saved_1, params[1]
     )
-    in_grad_own, feed_0, pending, attention_1, d_first_0, d_second_0, update = layer_backward(
-        grad, None, layout, saved_0, params[0], (pending, feed_1[1], update)
-    )
-    out_own = (saved_1[8] + update).astype(BF)
-    attention_0 = keep_fast(pending())
+    in_grad_own, feed_0, pending, attention_1, d_first_0, d_second_0 = layer_backward(
+        grad, None, layout, saved_0, params[0], (pending, feed_1[1])
+    )
+    joined = stack_rows(pending(), n_ctx)
+    gain_sum = jnp.stack([jnp.stack([d_first_0, d_second_0]), jnp.stack([d_first_1, d_second_1])])
+    update, gain_sum, in_grad_own = after([update, gain_sum, in_grad_own], [joined])
+    parts = send_rows(joined, "ctx") + send_cols(update, "wt")
+    parts = lax.optimization_barrier(tuple(parts))
+    attention_0 = add_up(parts[:n_ctx]).astype(BF)
+    out_own = (saved_1[8] + add_up(parts[n_ctx:])).astype(BF)
+    feed_0 = after(feed_0, [attention_0])
 
     def everywhere(own):
         low, high = own, shift(own, "section", 1)
@@ -491,14 +505,12 @@
 
     out = everywhere(out_own)
     in_grad = everywhere(in_grad_own)
-    gain_sum = lax.psum(
-        jnp.stack([jnp.stack([d_first_0, d_second_0]), jnp.stack([d_first_1, d_second_1])]), ("section", "ctx")
-    )
+    gain_sum = gain_sum + shift(gain_sum, "section", 1)
+    gain_sum = sum_in_order(gain_sum, "ctx")
     gain_mine = jnp.where(section_id == 0, gain_sum[0], gain_sum[1])
     down, gate_up = (home(section_id, a, b) for a, b in zip(feed_0, feed_1))
     grad_down = jnp.concatenate(down, axis=0).T.astype(F32)
     grad_gate, grad_up = (half.astype(F32) for half in gate_up)
-    (attention_0,) = after([attention_0], [grad_down, grad_gate, grad_up, out, in_grad, gain_mine])
     low, high = home(section_id, attention_0, attention_1)
     out_rows = query_width // n_ctx // 2
     grad_wo = jnp.concatenate([low[:out_rows], high[:out_rows]], axis=0).astype(F32)

time: 997 us -> 882 us (0.88)
  waiting for transfers between devices: 435 us -> 386 us
  blocking collectives: 26.6 us -> 0 us
  starting transfers between devices: 206 us -> 181 us
    ppermute x110 -> x111, waiting for transfers between devices: 434 us -> 385 us  [shift(): return lax.ppermute(value, axis, pairs)]
    psum x1 -> x0, blocking collectives: 26.6 us -> none  [local(): lax.psum(jnp.stack([jnp.stack([d_first_0, d_second_0]), jnp.stack([d_firs...]
    ppermute x110 -> x111, starting transfers between devices: 205 us -> 181 us  [shift(): return lax.ppermute(value, axis, pairs)]
    convert_element_type x4 -> x1, other arithmetic: 14 us -> 0.2 us  [local(): out_own = (saved_1[8] + add_up(parts[n_ctx:])).astype(BF)]
    unnamed x220 -> x285, local copies, waits for them, and re-layouts: 25.3 us -> 21.6 us
  transfers between devices with their start and end apart: 117 -> 119, of which waited for: 49 -> 54; matrix products, arithmetic and copies ran while one was open for 24% -> 26% of each run, Pallas kernels for 0% -> 0%
where the time goes in v5:
time: 882 us; the launch traced here: 873 us
  waiting for transfers between devices  386 us (44%)
  starting transfers between devices  181 us (21%)
  matrix products  150 us (17%)
  other arithmetic  73.2 us (8%)
  local copies, waits for them, and re-layouts  63.5 us (7%)
  between operations  18.1 us (2%)
    ppermute x111, waiting for transfers between devices, shift(): return lax.ppermute(value, axis, pairs)  385 us
    ppermute x111, starting transfers between devices, shift(): return lax.ppermute(value, axis, pairs)  181 us
    dot_general x14, matrix products, mm(): return jnp.dot(a, b, preferred_element_type=F32)  57 us
    dot_general x14, matrix products, mm_nt(): lax.dot_general(a, b, (((1,), (1,)), ((), ())), preferred_element_type=F32)  56.9 us
    dot_general x12, matrix products, mm_tn(): lax.dot_general(a, b, (((0,), (0,)), ((), ())), preferred_element_type=F32)  36.1 us
    unnamed x285, local copies, waits for them, and re-layouts  21.6 us
  transfers between devices with their start and end apart: 119, of which 54 were waited for; matrix products, arithmetic and copies ran while one was open for 26% of the time, Pallas kernels for 0%

profile of v5, /device:TPU:0, one launch (start us, length us, event | category | flops | bytes accessed | tf_op | source)
XLA Modules:
  0.0 872.5 jit_solution(2312846152349926092)
XLA Ops:
  22.0 6.5 broadcast_select_fusion.2
  38.7 13.4 %broadcast_select_fusion = (bf16[1920,2560]{1,0:T(8,128)(2,1)}, bf16[1920,2560]{1,0:T(8,128)(2,1)}) fusion(bf16[1920,2560]{1,0:T(8,128)(2,1)} %collective-permute-done.6, bf16[1920,2560]{1,0:T(8,128)(2,1)S(1)} %bitcast.165, pred[]{:T(512)S(6)} %eq.498), kind=kLoop, calls=%fused_computation.6 | loop fusion | flops 9830400 | bytes 39321600 | tf_op jit(solution)/shard_map/jit(_where)/select_n | solution.py:448
  52.2 10.7 %collective-permute-done.4 = bf16[64,3200]{1,0:T(8,128)(2,1)S(1)} collective-permute-done((bf16[64,3200]{1,0:T(8,128)(2,1)S(1)}, bf16[64,3200]{1,0:T(8,128)(2,1)S(1)}, u32[]{:S(2)}, u32[]{:S(2)}) %collective-permute-start.4) | collective-permute-done | bytes 409632 | tf_op jit(solution)/shard_map/ppermute | solution.py:21
  63.1 10.4 %collective-permute-start.17 = (f32[2,640]{1,0:T(2,128)S(1)}, f32[2,640]{1,0:T(2,128)S(1)}, u32[]{:S(2)}, u32[]{:S(2)}) collective-permute-start(f32[2,640]{1,0:T(2,128)S(1)} %pad_maximum_fusion.29), channel_id=1, source_target_pairs={{0,3},{1,0},{2,1},{3,2},{4,7},{5,4},{6,5},{7,6},{8,11},{9,8},{10,9... | collective-permute-start | bytes 15368 | tf_op jit(solution)/shard_map/ppermute | solution.py:21
  96.5 7.8 collective-permute-done.11
  104.4 9.4 %collective-permute-done.12 = bf16[64,2560]{1,0:T(8,128)(2,1)S(1)} collective-permute-done((bf16[64,2560]{1,0:T(8,128)(2,1)S(1)}, bf16[64,2560]{1,0:T(8,128)(2,1)S(1)}, u32[]{:S(2)}, u32[]{:S(2)}) %collective-permute-start.12) | collective-permute-done | bytes 327712 | tf_op jit(solution)/shard_map/ppermute | solution.py:21
  117.6 8.6 collective-permute-start.14
  128.0 6.2 collective-permute-done.14
  134.3 21.0 %collective-permute-done.15 = bf16[256,640]{1,0:T(8,128)(2,1)S(1)} collective-permute-done((bf16[256,640]{1,0:T(8,128)(2,1)S(1)}, bf16[256,640]{1,0:T(8,128)(2,1)S(1)}, u32[]{:S(2)}, u32[]{:S(2)}) %collective-permute-start.15) | collective-permute-done | bytes 327712 | tf_op jit(solution)/shard_map/ppermute | solution.py:21
  160.4 8.4 fusion.1
  168.8 8.9 %multiply_convert_fusion.3 = (bf16[256,1920]{1,0:T(8,128)(2,1)}, f32[256,1920]{1,0:T(8,128)}) fusion(f32[256,1920]{1,0:T(8,128)} %fusion.1, bf16[256,2560]{1,0:T(8,128)(2,1)S(1)} %fusion.16, bf16[2,2560,1920]{2,1,0:T(8,128)(2,1)} %all-gather.8.cloned.1.call-done), kind=kOutput, calls=%fused_computation.111 | convolution fusion | flops 2521497600 | bytes 16056320 | tf_op jit(solution)/shard_map/dot_general | solution.py:36
  180.4 7.1 convolution_convert_fusion.9
  187.6 6.7 collective-permute-start.23
  202.7 12.4 %collective-permute-done.24 = bf16[256,640]{1,0:T(8,128)(2,1)S(1)} collective-permute-done((bf16[256,640]{1,0:T(8,128)(2,1)S(1)}, bf16[256,640]{1,0:T(8,128)(2,1)S(1)}, u32[]{:S(2)}, u32[]{:S(2)}) %collective-permute-start.24) | collective-permute-done | bytes 327712 | tf_op jit(solution)/shard_map/ppermute | solution.py:21
  217.3 7.5 collective-permute-start.26
  229.3 8.3 collective-permute-done.26
  237.6 15.5 %collective-permute-done.27 = bf16[64,3200]{1,0:T(8,128)(2,1)S(1)} collective-permute-done((bf16[64,3200]{1,0:T(8,128)(2,1)S(1)}, bf16[64,3200]{1,0:T(8,128)(2,1)S(1)}, u32[]{:S(2)}, u32[]{:S(2)}) %collective-permute-start.27) | collective-permute-done | bytes 409632 | tf_op jit(solution)/shard_map/ppermute | solution.py:21
  256.7 9.3 %collective-permute-start.29 = (bf16[64,512]{1,0:T(8,128)(2,1)S(1)}, bf16[64,512]{1,0:T(8,128)(2,1)S(1)}, u32[]{:S(2)}, u32[]{:S(2)}) collective-permute-start(bf16[64,512]{1,0:T(8,128)(2,1)S(1)} %get-tuple-element.382), channel_id=1, source_target_pairs={{0,1},{1,0},{2,3},{3,2},{4,5},{5,4},{6,7},{7,6},{8,9},{9,8},{10,11... | collective-permute-start | bytes 196616 | tf_op jit(solution)/shard_map/ppermute | solution.py:21
  286.0 7.3 collective-permute-done.33
  293.3 13.0 %collective-permute-done.34 = bf16[64,2560]{1,0:T(8,128)(2,1)S(1)} collective-permute-done((bf16[64,2560]{1,0:T(8,128)(2,1)S(1)}, bf16[64,2560]{1,0:T(8,128)(2,1)S(1)}, u32[]{:S(2)}, u32[]{:S(2)}) %collective-permute-start.34) | collective-permute-done | bytes 327712 | tf_op jit(solution)/shard_map/ppermute | solution.py:21
  310.7 6.4 collective-permute-start.37
  325.5 22.2 %collective-permute-done.38 = bf16[256,640]{1,0:T(8,128)(2,1)} collective-permute-done((bf16[256,640]{1,0:T(8,128)(2,1)}, bf16[256,640]{1,0:T(8,128)(2,1)}, u32[]{:S(2)}, u32[]{:S(2)}) %collective-permute-start.38) | collective-permute-done | bytes 327712 | tf_op jit(solution)/shard_map/ppermute | solution.py:21
  350.0 7.4 fusion.5
  373.7 9.2 %broadcast_select_fusion.13 = (bf16[256,1920]{1,0:T(8,128)(2,1)S(1)}, bf16[256,1920]{1,0:T(8,128)(2,1)S(1)}, bf16[256,1920]{1,0:T(8,128)(2,1)S(1)}) fusion(pred[]{:T(512)S(6)} %eq.498, f32[256,1920]{1,0:T(8,128)S(1)} %copy-done.56, f32[256,1920]{1,0:T(8,128)} %get-tuple-element.420, bf16[256,2560]{1,0:T(8,128)(2,1)S(1)} %pad_maximum_fusion.6, ...), kind=kOutput, calls=%fused_computation.203 | convolution fusion | flops 2528870400 | bytes 18022400 | tf_op jit(solution)/shard_map/dot_general | solution.py:40
  389.7 7.2 fusion.11
  397.0 8.1 convolution_convert_fusion.1
  422.6 23.8 %collective-permute-done.48 = f32[256]{0:T(256)S(1)} collective-permute-done((f32[256]{0:T(256)S(1)}, f32[256]{0:T(256)S(1)}, u32[]{:S(2)}, u32[]{:S(2)}) %collective-permute-start.48) | collective-permute-done | bytes 1056 | tf_op jit(solution)/shard_map/ppermute | solution.py:21
  457.8 6.3 collective-permute-done.50
  464.1 13.1 %collective-permute-done.51 = bf16[64,2560]{1,0:T(8,128)(2,1)S(1)} collective-permute-done((bf16[64,2560]{1,0:T(8,128)(2,1)S(1)}, bf16[64,2560]{1,0:T(8,128)(2,1)S(1)}, u32[]{:S(2)}, u32[]{:S(2)}) %collective-permute-start.51) | collective-permute-done | bytes 327712 | tf_op jit(solution)/shard_map/ppermute | solution.py:21
  483.4 6.9 collective-permute-done.55
  511.0 19.2 %collective-permute-done.59 = bf16[64,640]{1,0:T(8,128)(2,1)S(1)} collective-permute-done((bf16[64,640]{1,0:T(8,128)(2,1)S(1)}, bf16[64,640]{1,0:T(8,128)(2,1)S(1)}, u32[]{:S(2)}, u32[]{:S(2)}) %collective-permute-start.59) | collective-permute-done | bytes 81952 | tf_op jit(solution)/shard_map/ppermute | solution.py:21
  530.3 9.6 %collective-permute-done.60 = bf16[64,640]{1,0:T(8,128)(2,1)S(1)} collective-permute-done((bf16[64,640]{1,0:T(8,128)(2,1)S(1)}, bf16[64,640]{1,0:T(8,128)(2,1)S(1)}, u32[]{:S(2)}, u32[]{:S(2)}) %collective-permute-start.60) | collective-permute-done | bytes 81952 | tf_op jit(solution)/shard_map/ppermute | solution.py:21
  566.5 13.2 %collective-permute-done.66 = bf16[256,640]{1,0:T(8,128)(2,1)S(1)} collective-permute-done((bf16[256,640]{1,0:T(8,128)(2,1)S(1)}, bf16[256,640]{1,0:T(8,128)(2,1)S(1)}, u32[]{:S(2)}, u32[]{:S(2)}) %collective-permute-start.66) | collective-permute-done | bytes 327712 | tf_op jit(solution)/shard_map/ppermute | solution.py:21
  591.7 8.4 broadcast_select_fusion.11
  607.2 6.8 fusion.10
  614.1 8.2 convolution_convert_fusion
  627.0 7.6 collective-permute-start.77
  642.6 7.5 collective-permute-done.70
  655.9 13.6 %collective-permute-done.71 = bf16[256,640]{1,0:T(8,128)(2,1)S(1)} collective-permute-done((bf16[256,640]{1,0:T(8,128)(2,1)S(1)}, bf16[256,640]{1,0:T(8,128)(2,1)S(1)}, u32[]{:S(2)}, u32[]{:S(2)}) %collective-permute-start.71) | collective-permute-done | bytes 327712 | tf_op jit(solution)/shard_map/ppermute | solution.py:21
  678.9 7.0 convolution_convert_fusion.6
  688.4 12.6 %collective-permute-done.82 = bf16[64,2560]{1,0:T(8,128)(2,1)} collective-permute-done((bf16[64,2560]{1,0:T(8,128)(2,1)}, bf16[64,2560]{1,0:T(8,128)(2,1)}, u32[]{:S(2)}, u32[]{:S(2)}) %collective-permute-start.82) | collective-permute-done | bytes 327712 | tf_op jit(solution)/shard_map/ppermute | solution.py:21
  723.3 7.1 collective-permute-start.90
  737.6 20.1 %collective-permute-done.91 = bf16[64,640]{1,0:T(8,128)(2,1)S(1)} collective-permute-done((bf16[64,640]{1,0:T(8,128)(2,1)S(1)}, bf16[64,640]{1,0:T(8,128)(2,1)S(1)}, u32[]{:S(2)}, u32[]{:S(2)}) %collective-permute-start.91) | collective-permute-done | bytes 81952 | tf_op jit(solution)/shard_map/ppermute | solution.py:21
  758.0 9.4 %collective-permute-done.92 = bf16[64,640]{1,0:T(8,128)(2,1)S(1)} collective-permute-done((bf16[64,640]{1,0:T(8,128)(2,1)S(1)}, bf16[64,640]{1,0:T(8,128)(2,1)S(1)}, u32[]{:S(2)}, u32[]{:S(2)}) %collective-permute-start.92) | collective-permute-done | bytes 81952 | tf_op jit(solution)/shard_map/ppermute | solution.py:21
  788.8 7.2 collective-permute-done.100
  801.0 7.3 collective-permute-done.99
  812.4 13.4 %collective-permute-done.97 = bf16[704,640]{1,0:T(8,128)(2,1)S(1)} collective-permute-done((bf16[704,640]{1,0:T(8,128)(2,1)S(1)}, bf16[704,640]{1,0:T(8,128)(2,1)S(1)}, u32[]{:S(2)}, u32[]{:S(2)}) %collective-permute-start.97) | collective-permute-done | bytes 901152 | tf_op jit(solution)/shard_map/ppermute | solution.py:21
  858.2 7.0 bitcast_convert_fusion
  (780 shorter events, 360.4 us)
Async XLA Ops:
  7.2 106.6 %all-gather.4.cloned.1.call-start = ((), (), s32[]{:S(2)}) async-start(), calls=%async_computation.5 | async-start | bytes 9830400 | tf_op jit(solution)/shard_map/all_gather | solution.py:443
  8.0 152.4 %all-gather.6.cloned.1.call-start = ((), (), s32[]{:S(2)}) async-start(), calls=%async_computation.6 | async-start | bytes 29491200 | tf_op jit(solution)/shard_map/all_gather | solution.py:443
  8.7 160.1 %all-gather.8.cloned.1.call-start = ((), (), s32[]{:S(2)}) async-start(), calls=%async_computation.7 | async-start | bytes 29491200 | tf_op jit(solution)/shard_map/all_gather | solution.py:443
  18.9 458.3 %reduce-scatter.6.cloned.1.call-start = ((), (), s32[]{:S(2)}) async-start(), calls=%async_computation.8 | async-start | bytes 6144000 | tf_op jit(solution)/shard_map/reduce_scatter | solution.py:413
  33.7 29.1 %collective-permute-start.4 = (bf16[64,3200]{1,0:T(8,128)(2,1)S(1)}, bf16[64,3200]{1,0:T(8,128)(2,1)S(1)}, u32[]{:S(2)}, u32[]{:S(2)}) collective-permute-start(bf16[64,3200]{1,0:T(8,128)(2,1)S(1)} %get-tuple-element.242), channel_id=1, source_target_pairs={{0,2},{1,3},{2,0},{3,1},{4,6},{5,7},{6,4},{7,5},{8,10},{9,11},{10,... | collective-permute-start | bytes 1228808 | tf_op jit(solution)/shard_map/ppermute | solution.py:21
  36.1 26.8 %collective-permute-start.5 = (bf16[64,3200]{1,0:T(8,128)(2,1)S(1)}, bf16[64,3200]{1,0:T(8,128)(2,1)S(1)}, u32[]{:S(2)}, u32[]{:S(2)}) collective-permute-start(bf16[64,3200]{1,0:T(8,128)(2,1)S(1)} %get-tuple-element.240), channel_id=1, source_target_pairs={{0,3},{1,0},{2,1},{3,2},{4,7},{5,4},{6,5},{7,6},{8,11},{9,8},{10,9... | collective-permute-start | bytes 1228808 | tf_op jit(solution)/shard_map/ppermute | solution.py:21
  126.2 29.1 %collective-permute-start.15 = (bf16[256,640]{1,0:T(8,128)(2,1)S(1)}, bf16[256,640]{1,0:T(8,128)(2,1)S(1)}, u32[]{:S(2)}, u32[]{:S(2)}) collective-permute-start(bf16[256,640]{1,0:T(8,128)(2,1)S(1)} %get-tuple-element.411), channel_id=1, source_target_pairs={{0,2},{1,3},{2,0},{3,1},{4,6},{5,7},{6,4},{7,5},{8,10},{9,11},{10,... | collective-permute-start | bytes 983048 | tf_op jit(solution)/shard_map/ppermute | solution.py:21
  126.5 28.7 %collective-permute-start.16 = (bf16[256,640]{1,0:T(8,128)(2,1)S(1)}, bf16[256,640]{1,0:T(8,128)(2,1)S(1)}, u32[]{:S(2)}, u32[]{:S(2)}) collective-permute-start(bf16[256,640]{1,0:T(8,128)(2,1)S(1)} %get-tuple-element.411), channel_id=1, source_target_pairs={{0,1},{1,2},{2,3},{3,0},{4,5},{5,6},{6,7},{7,4},{8,9},{9,10},{10,1... | collective-permute-start | bytes 983048 | tf_op jit(solution)/shard_map/ppermute | solution.py:21
  155.6 22.2 %collective-permute-start.20 = (bf16[256,640]{1,0:T(8,128)(2,1)S(1)}, bf16[256,640]{1,0:T(8,128)(2,1)S(1)}, u32[]{:S(2)}, u32[]{:S(2)}) collective-permute-start(bf16[256,640]{1,0:T(8,128)(2,1)S(1)} %bitcast.178), channel_id=1, source_target_pairs={{0,1},{1,2},{2,3},{3,0},{4,5},{5,6},{6,7},{7,4},{8,9},{9,10},{10,1... | collective-permute-start | bytes 983048 | tf_op jit(solution)/shard_map/ppermute | solution.py:21
  155.6 24.7 %collective-permute-start.21 = (bf16[256,640]{1,0:T(8,128)(2,1)S(1)}, bf16[256,640]{1,0:T(8,128)(2,1)S(1)}, u32[]{:S(2)}, u32[]{:S(2)}) collective-permute-start(bf16[256,640]{1,0:T(8,128)(2,1)S(1)} %bitcast.179), channel_id=1, source_target_pairs={{0,2},{1,3},{2,0},{3,1},{4,6},{5,7},{6,4},{7,5},{8,10},{9,11},{10,... | collective-permute-start | bytes 983048 | tf_op jit(solution)/shard_map/ppermute | solution.py:21
  155.7 24.7 %collective-permute-start.22 = (bf16[256,640]{1,0:T(8,128)(2,1)S(1)}, bf16[256,640]{1,0:T(8,128)(2,1)}, u32[]{:S(2)}, u32[]{:S(2)}) collective-permute-start(bf16[256,640]{1,0:T(8,128)(2,1)S(1)} %bitcast.180), channel_id=1, source_target_pairs={{0,3},{1,0},{2,1},{3,2},{4,7},{5,4},{6,5},{7,6},{8,11},{9,8},{10,9... | collective-permute-start | bytes 983048 | tf_op jit(solution)/shard_map/ppermute | solution.py:21
  224.9 28.2 %collective-permute-start.27 = (bf16[64,3200]{1,0:T(8,128)(2,1)S(1)}, bf16[64,3200]{1,0:T(8,128)(2,1)S(1)}, u32[]{:S(2)}, u32[]{:S(2)}) collective-permute-start(bf16[64,3200]{1,0:T(8,128)(2,1)S(1)} %get-tuple-element.238), channel_id=1, source_target_pairs={{0,2},{1,3},{2,0},{3,1},{4,6},{5,7},{6,4},{7,5},{8,10},{9,11},{10,... | collective-permute-start | bytes 1228808 | tf_op jit(solution)/shard_map/ppermute | solution.py:21
  227.7 25.4 %collective-permute-start.28 = (bf16[64,3200]{1,0:T(8,128)(2,1)S(1)}, bf16[64,3200]{1,0:T(8,128)(2,1)S(1)}, u32[]{:S(2)}, u32[]{:S(2)}) collective-permute-start(bf16[64,3200]{1,0:T(8,128)(2,1)S(1)} %get-tuple-element.239), channel_id=1, source_target_pairs={{0,3},{1,0},{2,1},{3,2},{4,7},{5,4},{6,5},{7,6},{8,11},{9,8},{10,9... | collective-permute-start | bytes 1228808 | tf_op jit(solution)/shard_map/ppermute | solution.py:21
  282.8 23.5 %collective-permute-start.34 = (bf16[64,2560]{1,0:T(8,128)(2,1)S(1)}, bf16[64,2560]{1,0:T(8,128)(2,1)S(1)}, u32[]{:S(2)}, u32[]{:S(2)}) collective-permute-start(bf16[64,2560]{1,0:T(8,128)(2,1)S(1)} %reshape.479), channel_id=1, source_target_pairs={{0,2},{1,3},{2,0},{3,1},{4,6},{5,7},{6,4},{7,5},{8,10},{9,11},{10,... | collective-permute-start | bytes 983048 | tf_op jit(solution)/shard_map/ppermute | solution.py:21
  317.2 30.5 %collective-permute-start.38 = (bf16[256,640]{1,0:T(8,128)(2,1)}, bf16[256,640]{1,0:T(8,128)(2,1)}, u32[]{:S(2)}, u32[]{:S(2)}) collective-permute-start(bf16[256,640]{1,0:T(8,128)(2,1)} %get-tuple-element.417), channel_id=1, source_target_pairs={{0,2},{1,3},{2,0},{3,1},{4,6},{5,7},{6,4},{7,5},{8,10},{9,11},{10,... | collective-permute-start | bytes 983048 | tf_op jit(solution)/shard_map/ppermute | solution.py:21
  319.2 28.5 %collective-permute-start.39 = (bf16[256,640]{1,0:T(8,128)(2,1)}, bf16[256,640]{1,0:T(8,128)(2,1)}, u32[]{:S(2)}, u32[]{:S(2)}) collective-permute-start(bf16[256,640]{1,0:T(8,128)(2,1)} %get-tuple-element.417), channel_id=1, source_target_pairs={{0,1},{1,2},{2,3},{3,0},{4,5},{5,6},{6,7},{7,4},{8,9},{9,10},{10,1... | collective-permute-start | bytes 983048 | tf_op jit(solution)/shard_map/ppermute | solution.py:21
  371.9 207.8 %reduce-scatter.8.cloned.1.call-start = ((), (), s32[]{:S(2)}) async-start(), calls=%async_computation.9 | async-start | bytes 12288000 | tf_op jit(solution)/shard_map/reduce_scatter | solution.py:413
  372.2 24.7 %collective-permute-start.45 = (bf16[256,2560]{1,0:T(8,128)(2,1)}, bf16[256,2560]{1,0:T(8,128)(2,1)S(1)}, u32[]{:S(2)}, u32[]{:S(2)}) collective-permute-start(bf16[256,2560]{1,0:T(8,128)(2,1)} %copy-done.70), channel_id=1, source_target_pairs={{0,16},{16,0},{1,17},{17,1},{2,18},{18,2},{3,19},{19,3},{4,20},{20... | collective-permute-start | bytes 3932168 | tf_op jit(solution)/shard_map/ppermute | solution.py:21
  405.1 283.3 %reduce-scatter.10.cloned.1.call-start = ((), (), s32[]{:S(2)}) async-start(), calls=%async_computation.10 | async-start | bytes 4505600 | tf_op jit(solution)/shard_map/reduce_scatter | solution.py:413
  413.3 33.1 %collective-permute-start.42 = (bf16[256,640]{1,0:T(8,128)(2,1)S(1)}, bf16[256,640]{1,0:T(8,128)(2,1)S(1)}, u32[]{:S(2)}, u32[]{:S(2)}) collective-permute-start(bf16[256,640]{1,0:T(8,128)(2,1)S(1)} %get-tuple-element.303), channel_id=1, source_target_pairs={{0,1},{1,2},{2,3},{3,0},{4,5},{5,6},{6,7},{7,4},{8,9},{9,10},{10,1... | collective-permute-start | bytes 983048 | tf_op jit(solution)/shard_map/ppermute | solution.py:21
  413.4 33.0 %collective-permute-start.44 = (bf16[256,640]{1,0:T(8,128)(2,1)S(1)}, bf16[256,640]{1,0:T(8,128)(2,1)S(1)}, u32[]{:S(2)}, u32[]{:S(2)}) collective-permute-start(bf16[256,640]{1,0:T(8,128)(2,1)S(1)} %get-tuple-element.302), channel_id=1, source_target_pairs={{0,3},{1,0},{2,1},{3,2},{4,7},{5,4},{6,5},{7,6},{8,11},{9,8},{10,9... | collective-permute-start | bytes 983048 | tf_op jit(solution)/shard_map/ppermute | solution.py:21
  417.3 29.2 %collective-permute-start.43 = (bf16[256,640]{1,0:T(8,128)(2,1)S(1)}, bf16[256,640]{1,0:T(8,128)(2,1)S(1)}, u32[]{:S(2)}, u32[]{:S(2)}) collective-permute-start(bf16[256,640]{1,0:T(8,128)(2,1)S(1)} %select_select_fusion.12), channel_id=1, source_target_pairs={{0,2},{1,3},{2,0},{3,1},{4,6},{5,7},{6,4},{7,5},{8,10},{9,11},{10,... | collective-permute-start | bytes 983048 | tf_op jit(solution)/shard_map/ppermute | solution.py:21
  417.8 28.6 %collective-permute-start.48 = (f32[256]{0:T(256)S(1)}, f32[256]{0:T(256)S(1)}, u32[]{:S(2)}, u32[]{:S(2)}) collective-permute-start(f32[256]{0:T(256)S(1)} %add_reduce_fusion.1), channel_id=1, source_target_pairs={{0,2},{1,3},{2,0},{3,1},{4,6},{5,7},{6,4},{7,5},{8,10},{9,11},{10,... | collective-permute-start | bytes 3080 | tf_op jit(solution)/shard_map/ppermute | solution.py:21
  420.2 26.2 %collective-permute-start.49 = (f32[256]{0:T(256)S(1)}, f32[256]{0:T(256)S(1)}, u32[]{:S(2)}, u32[]{:S(2)}) collective-permute-start(f32[256]{0:T(256)S(1)} %add_reduce_fusion.1), channel_id=1, source_target_pairs={{0,3},{1,0},{2,1},{3,2},{4,7},{5,4},{6,5},{7,6},{8,11},{9,8},{10,9... | collective-permute-start | bytes 3080 | tf_op jit(solution)/shard_map/ppermute | solution.py:21
  452.0 25.2 %collective-permute-start.51 = (bf16[64,2560]{1,0:T(8,128)(2,1)S(1)}, bf16[64,2560]{1,0:T(8,128)(2,1)S(1)}, u32[]{:S(2)}, u32[]{:S(2)}) collective-permute-start(bf16[64,2560]{1,0:T(8,128)(2,1)S(1)} %get-tuple-element.300), channel_id=1, source_target_pairs={{0,2},{1,3},{2,0},{3,1},{4,6},{5,7},{6,4},{7,5},{8,10},{9,11},{10,... | collective-permute-start | bytes 983048 | tf_op jit(solution)/shard_map/ppermute | solution.py:21
  452.0 25.2 %collective-permute-start.52 = (bf16[64,2560]{1,0:T(8,128)(2,1)S(1)}, bf16[64,2560]{1,0:T(8,128)(2,1)S(1)}, u32[]{:S(2)}, u32[]{:S(2)}) collective-permute-start(bf16[64,2560]{1,0:T(8,128)(2,1)S(1)} %get-tuple-element.299), channel_id=1, source_target_pairs={{0,3},{1,0},{2,1},{3,2},{4,7},{5,4},{6,5},{7,6},{8,11},{9,8},{10,9... | collective-permute-start | bytes 983048 | tf_op jit(solution)/shard_map/ppermute | solution.py:21
  503.0 39.1 %collective-permute-start.62 = (bf16[64,2560]{1,0:T(8,128)(2,1)S(1)}, bf16[64,2560]{1,0:T(8,128)(2,1)S(1)}, u32[]{:S(2)}, u32[]{:S(2)}) collective-permute-start(bf16[64,2560]{1,0:T(8,128)(2,1)S(1)} %bitcast.173), channel_id=1, source_target_pairs={{0,1},{1,2},{2,3},{3,0},{4,5},{5,6},{6,7},{7,4},{8,9},{9,10},{10,1... | collective-permute-start | bytes 983048 | tf_op jit(solution)/shard_map/ppermute | solution.py:21
  505.1 37.1 %collective-permute-start.63 = (bf16[64,2560]{1,0:T(8,128)(2,1)S(1)}, bf16[64,2560]{1,0:T(8,128)(2,1)S(1)}, u32[]{:S(2)}, u32[]{:S(2)}) collective-permute-start(bf16[64,2560]{1,0:T(8,128)(2,1)S(1)} %bitcast.174), channel_id=1, source_target_pairs={{0,2},{1,3},{2,0},{3,1},{4,6},{5,7},{6,4},{7,5},{8,10},{9,11},{10,... | collective-permute-start | bytes 983048 | tf_op jit(solution)/shard_map/ppermute | solution.py:21
  507.4 34.8 %collective-permute-start.64 = (bf16[64,2560]{1,0:T(8,128)(2,1)S(1)}, bf16[64,2560]{1,0:T(8,128)(2,1)S(1)}, u32[]{:S(2)}, u32[]{:S(2)}) collective-permute-start(bf16[64,2560]{1,0:T(8,128)(2,1)S(1)} %bitcast.175), channel_id=1, source_target_pairs={{0,3},{1,0},{2,1},{3,2},{4,7},{5,4},{6,5},{7,6},{8,11},{9,8},{10,9... | collective-permute-start | bytes 983048 | tf_op jit(solution)/shard_map/ppermute | solution.py:21
  510.3 29.6 %collective-permute-start.60 = (bf16[64,640]{1,0:T(8,128)(2,1)S(1)}, bf16[64,640]{1,0:T(8,128)(2,1)S(1)}, u32[]{:S(2)}, u32[]{:S(2)}) collective-permute-start(bf16[64,640]{1,0:T(8,128)(2,1)S(1)} %get-tuple-element.380), channel_id=1, source_target_pairs={{0,2},{1,3},{2,0},{3,1},{4,6},{5,7},{6,4},{7,5},{8,10},{9,11},{10,... | collective-permute-start | bytes 245768 | tf_op jit(solution)/shard_map/ppermute | solution.py:21
  553.9 275.6 %reduce-scatter.12.cloned.1.call-start = ((), (), s32[]{:S(2)}) async-start(), calls=%async_computation.11 | async-start | bytes 6144000 | tf_op jit(solution)/shard_map/reduce_scatter | solution.py:413
  556.4 23.2 %collective-permute-start.66 = (bf16[256,640]{1,0:T(8,128)(2,1)S(1)}, bf16[256,640]{1,0:T(8,128)(2,1)S(1)}, u32[]{:S(2)}, u32[]{:S(2)}) collective-permute-start(bf16[256,640]{1,0:T(8,128)(2,1)S(1)} %get-tuple-element.208), channel_id=1, source_target_pairs={{0,2},{1,3},{2,0},{3,1},{4,6},{5,7},{6,4},{7,5},{8,10},{9,11},{10,... | collective-permute-start | bytes 983048 | tf_op jit(solution)/shard_map/ppermute | solution.py:21
  558.0 21.7 %collective-permute-start.67 = (bf16[256,640]{1,0:T(8,128)(2,1)S(1)}, bf16[256,640]{1,0:T(8,128)(2,1)S(1)}, u32[]{:S(2)}, u32[]{:S(2)}) collective-permute-start(bf16[256,640]{1,0:T(8,128)(2,1)S(1)} %get-tuple-element.208), channel_id=1, source_target_pairs={{0,3},{1,0},{2,1},{3,2},{4,7},{5,4},{6,5},{7,6},{8,11},{9,8},{10,9... | collective-permute-start | bytes 983048 | tf_op jit(solution)/shard_map/ppermute | solution.py:21
  590.1 239.4 %reduce-scatter.14.cloned.1.call-start = ((), (), s32[]{:S(2)}) async-start(), calls=%async_computation.12 | async-start | bytes 12288000 | tf_op jit(solution)/shard_map/reduce_scatter | solution.py:413
  590.3 23.8 %collective-permute-start.75 = (bf16[256,2560]{1,0:T(8,128)(2,1)}, bf16[256,2560]{1,0:T(8,128)(2,1)S(1)}, u32[]{:S(2)}, u32[]{:S(2)}) collective-permute-start(bf16[256,2560]{1,0:T(8,128)(2,1)} %copy-done.68), channel_id=1, source_target_pairs={{0,16},{16,0},{1,17},{17,1},{2,18},{18,2},{3,19},{19,3},{4,20},{20... | collective-permute-start | bytes 3932168 | tf_op jit(solution)/shard_map/ppermute | solution.py:21
  641.7 27.8 %collective-permute-start.71 = (bf16[256,640]{1,0:T(8,128)(2,1)S(1)}, bf16[256,640]{1,0:T(8,128)(2,1)S(1)}, u32[]{:S(2)}, u32[]{:S(2)}) collective-permute-start(bf16[256,640]{1,0:T(8,128)(2,1)S(1)} %select_select_fusion.5), channel_id=1, source_target_pairs={{0,2},{1,3},{2,0},{3,1},{4,6},{5,7},{6,4},{7,5},{8,10},{9,11},{10,... | collective-permute-start | bytes 983048 | tf_op jit(solution)/shard_map/ppermute | solution.py:21
  641.8 44.1 %collective-permute-start.36 = (bf16[256,1280]{1,0:T(8,128)(2,1)S(1)}, bf16[256,1280]{1,0:T(8,128)(2,1)S(1)}, u32[]{:S(2)}, u32[]{:S(2)}) collective-permute-start(bf16[256,1280]{1,0:T(8,128)(2,1)S(1)} %get-tuple-element.261), channel_id=1, source_target_pairs={{0,16},{16,0},{1,17},{17,1},{2,18},{18,2},{3,19},{19,3},{4,20},{20... | collective-permute-start | bytes 1966088 | tf_op jit(solution)/shard_map/ppermute | solution.py:21
  675.0 25.9 %collective-permute-start.82 = (bf16[64,2560]{1,0:T(8,128)(2,1)}, bf16[64,2560]{1,0:T(8,128)(2,1)}, u32[]{:S(2)}, u32[]{:S(2)}) collective-permute-start(bf16[64,2560]{1,0:T(8,128)(2,1)} %get-tuple-element.271), channel_id=1, source_target_pairs={{0,2},{1,3},{2,0},{3,1},{4,6},{5,7},{6,4},{7,5},{8,10},{9,11},{10,... | collective-permute-start | bytes 983048 | tf_op jit(solution)/shard_map/ppermute | solution.py:21
  676.6 24.3 %collective-permute-start.83 = (bf16[64,2560]{1,0:T(8,128)(2,1)S(1)}, bf16[64,2560]{1,0:T(8,128)(2,1)}, u32[]{:S(2)}, u32[]{:S(2)}) collective-permute-start(bf16[64,2560]{1,0:T(8,128)(2,1)S(1)} %get-tuple-element.270), channel_id=1, source_target_pairs={{0,3},{1,0},{2,1},{3,2},{4,7},{5,4},{6,5},{7,6},{8,11},{9,8},{10,9... | collective-permute-start | bytes 983048 | tf_op jit(solution)/shard_map/ppermute | solution.py:21
  730.6 37.5 %collective-permute-start.84 = (bf16[64,2560]{1,0:T(8,128)(2,1)S(1)}, bf16[64,2560]{1,0:T(8,128)(2,1)}, u32[]{:S(2)}, u32[]{:S(2)}) collective-permute-start(bf16[64,2560]{1,0:T(8,128)(2,1)S(1)} %bitcast.169), channel_id=1, source_target_pairs={{0,1},{1,2},{2,3},{3,0},{4,5},{5,6},{6,7},{7,4},{8,9},{9,10},{10,1... | collective-permute-start | bytes 983048 | tf_op jit(solution)/shard_map/ppermute | solution.py:21
  730.7 38.4 %collective-permute-start.85 = (bf16[64,2560]{1,0:T(8,128)(2,1)S(1)}, bf16[64,2560]{1,0:T(8,128)(2,1)S(1)}, u32[]{:S(2)}, u32[]{:S(2)}) collective-permute-start(bf16[64,2560]{1,0:T(8,128)(2,1)S(1)} %bitcast.170), channel_id=1, source_target_pairs={{0,2},{1,3},{2,0},{3,1},{4,6},{5,7},{6,4},{7,5},{8,10},{9,11},{10,... | collective-permute-start | bytes 983048 | tf_op jit(solution)/shard_map/ppermute | solution.py:21
  731.6 37.6 %collective-permute-start.86 = (bf16[64,2560]{1,0:T(8,128)(2,1)S(1)}, bf16[64,2560]{1,0:T(8,128)(2,1)S(1)}, u32[]{:S(2)}, u32[]{:S(2)}) collective-permute-start(bf16[64,2560]{1,0:T(8,128)(2,1)S(1)} %bitcast.171), channel_id=1, source_target_pairs={{0,3},{1,0},{2,1},{3,2},{4,7},{5,4},{6,5},{7,6},{8,11},{9,8},{10,9... | collective-permute-start | bytes 983048 | tf_op jit(solution)/shard_map/ppermute | solution.py:21
  735.3 22.4 %collective-permute-start.91 = (bf16[64,640]{1,0:T(8,128)(2,1)S(1)}, bf16[64,640]{1,0:T(8,128)(2,1)S(1)}, u32[]{:S(2)}, u32[]{:S(2)}) collective-permute-start(bf16[64,640]{1,0:T(8,128)(2,1)S(1)} %get-tuple-element.378), channel_id=1, source_target_pairs={{0,1},{1,2},{2,3},{3,0},{4,5},{5,6},{6,7},{7,4},{8,9},{9,10},{10,1... | collective-permute-start | bytes 245768 | tf_op jit(solution)/shard_map/ppermute | solution.py:21
  736.4 30.9 %collective-permute-start.92 = (bf16[64,640]{1,0:T(8,128)(2,1)S(1)}, bf16[64,640]{1,0:T(8,128)(2,1)S(1)}, u32[]{:S(2)}, u32[]{:S(2)}) collective-permute-start(bf16[64,640]{1,0:T(8,128)(2,1)S(1)} %get-tuple-element.378), channel_id=1, source_target_pairs={{0,2},{1,3},{2,0},{3,1},{4,6},{5,7},{6,4},{7,5},{8,10},{9,11},{10,... | collective-permute-start | bytes 245768 | tf_op jit(solution)/shard_map/ppermute | solution.py:21
  784.4 28.0 %collective-permute-start.96 = (bf16[704,640]{1,0:T(8,128)(2,1)S(1)}, bf16[704,640]{1,0:T(8,128)(2,1)S(1)}, u32[]{:S(2)}, u32[]{:S(2)}) collective-permute-start(bf16[704,640]{1,0:T(8,128)(2,1)S(1)} %get-tuple-element.231), channel_id=1, source_target_pairs={{0,4},{4,8},{8,12},{12,0},{1,5},{5,9},{9,13},{13,1},{2,6},{6,10},{... | collective-permute-start | bytes 2703368 | tf_op jit(solution)/shard_map/ppermute | solution.py:21
  785.5 40.3 %collective-permute-start.97 = (bf16[704,640]{1,0:T(8,128)(2,1)S(1)}, bf16[704,640]{1,0:T(8,128)(2,1)S(1)}, u32[]{:S(2)}, u32[]{:S(2)}) collective-permute-start(bf16[704,640]{1,0:T(8,128)(2,1)S(1)} %get-tuple-element.230), channel_id=1, source_target_pairs={{0,8},{4,12},{8,0},{12,4},{1,9},{5,13},{9,1},{13,5},{2,10},{6,14},... | collective-permute-start | bytes 2703368 | tf_op jit(solution)/shard_map/ppermute | solution.py:21
  787.1 38.7 %collective-permute-start.98 = (bf16[704,640]{1,0:T(8,128)(2,1)S(1)}, bf16[704,640]{1,0:T(8,128)(2,1)S(1)}, u32[]{:S(2)}, u32[]{:S(2)}) collective-permute-start(bf16[704,640]{1,0:T(8,128)(2,1)S(1)} %get-tuple-element.229), channel_id=1, source_target_pairs={{0,12},{4,0},{8,4},{12,8},{1,13},{5,1},{9,5},{13,9},{2,14},{6,2},{... | collective-permute-start | bytes 2703368 | tf_op jit(solution)/shard_map/ppermute | solution.py:21
  831.6 26.7 %collective-permute-start.105 = (bf16[640,1920]{1,0:T(8,128)(2,1)}, bf16[640,1920]{1,0:T(8,128)(2,1)}, u32[]{:S(2)}, u32[]{:S(2)}) collective-permute-start(bf16[640,1920]{1,0:T(8,128)(2,1)} %broadcast_select_fusion.4), channel_id=1, source_target_pairs={{0,16},{16,0},{1,17},{17,1},{2,18},{18,2},{3,19},{19,3},{4,20},{20... | collective-permute-start | bytes 7372808 | tf_op jit(solution)/shard_map/ppermute | solution.py:21
  (208 other events, 2941.2 us)
Sparse Core Ops, SparseCore 0:
  9.5 23.9 all-gather.3
  35.1 35.5 all-gather.5
  72.3 35.5 all-gather.7
  372.0 55.6 reduce-scatter.5
  430.7 103.7 reduce-scatter.7
  554.0 47.7 reduce-scatter.9
  605.4 58.5 reduce-scatter.11
  667.1 103.7 reduce-scatter.13
